TPU v7x, 128 devices: a whole 4x4x4 slice. The times are simulated.
128 devices in a mesh: slab: 8 (over x, core), col: 16 (over z, y).
Axes of the slice: x: 4, y: 4, z: 4, core: 2. Of those that a mesh axis runs over, the one named last changes fastest.
Arguments:
- modes: float32 [64, 393216], P(None, ('slab', 'col')), may hold values from -20 to 20
- tiles: bfloat16 [3072, 384, 384], P(('slab', 'col')), may hold values from -0.0625 to 0.0625
- tile_pair: int32 [3072], P(('slab', 'col')), may hold values from 0 to 23, as said below
- boundary: int32 [128, 2], P(('slab', 'col')), may hold values from 96 to 384, as said below
Outputs:
- filtered: float32 [64, 393216], P(None, ('slab', 'col'))
Inputs may be any that keep to these rules, and one draw needn't show every extreme that they name: `tile_pair`: each row block's 24 entries hold every number of 0 to 23 once. `boundary`: on each side, some row block reaches 384 in every draw.
All inputs are finite; a program needn't handle non-finite values.
Results may differ from a plain program's by a relative error of at most 0.0059.
Values may be sent and summed in bfloat16 or wider, within the bound.
No kernel may reach another device: no remote copies, remote signals or barrier semaphores. Data moves between devices by JAX's collectives and lax.ppermute only.
A program may use at most 64 MiB of HBM per device.

v0:
```python
import functools

import jax
import jax.numpy as jnp
from jax import lax
from jax.experimental import pallas as pl
from jax.experimental.pallas import tpu as pltpu
from jax.sharding import PartitionSpec as P

DEG = 8
center = 0.25
AXES = ("slab", "col")
K = 64
TB = 384
RT = 8
TL = 24
ROWS = RT * TB
F32 = jnp.float32
BF16 = jnp.bfloat16

VM = pl.BlockSpec(memory_space=pltpu.VMEM)
SM = pl.BlockSpec(memory_space=pltpu.SMEM)
ANY = pl.BlockSpec(memory_space=pl.ANY)


def vmem(shape, dtype):
    return pltpu.VMEM(shape, dtype)


def pin(x):
    return pltpu.with_memory_space_constraint(x, pltpu.VMEM)


def params(mib):
    return pltpu.CompilerParams(vmem_limit_bytes=mib << 20)


def target_columns(r):
    return max(r - 1, 0) * TB, min(r + 2, RT) * TB


def target_rows(r):
    start = 0 if r == 0 else (3 * r - 1)
    return start * TB, (start + (2 if r in (0, RT - 1) else 3)) * TB


def target_pairs(r):
    return [3 * c + (r - c) + 1 for c in (r - 1, r, r + 1) if 0 <= c < RT]


def dot(a, b):
    return jnp.dot(a, b, preferred_element_type=F32)


def overflow(low, high, we_ref, bound_ref, par_ref, se_ref, so_ref):
    column = lax.broadcasted_iota(jnp.int32, (K, TB), 1)
    low = jnp.where(column < bound_ref[0, 0], low, 0.0).astype(BF16)
    high = jnp.where(column >= TB - bound_ref[0, 1], high, 0.0).astype(BF16)
    s_low = dot(low, we_ref[0]).astype(BF16)
    s_high = dot(high, we_ref[1]).astype(BF16)
    even = par_ref[0] == 0
    se_ref[...] = jnp.where(even, s_high, s_low)
    so_ref[...] = jnp.where(even, s_low, s_high)


def first_kernel(pair_ref, bound_ref, par_ref, modes_ref, tiles_ref, we_ref, ye_ref, se_ref, so_ref, sems):
    low_at = jnp.int32(0)
    high_at = jnp.int32(0)
    for t in range(TL):
        low_at = jnp.where(pair_ref[t] == 0, t, low_at)
        high_at = jnp.where(pair_ref[t] == TL - 1, t, high_at)
    copies = [
        pltpu.make_async_copy(modes_ref.at[:, pl.ds(0, TB)], ye_ref.at[:, pl.ds(0, TB)], sems.at[0]),
        pltpu.make_async_copy(tiles_ref.at[low_at], we_ref.at[0], sems.at[1]),
        pltpu.make_async_copy(modes_ref.at[:, pl.ds(ROWS - TB, TB)], ye_ref.at[:, pl.ds(TB, TB)], sems.at[2]),
        pltpu.make_async_copy(tiles_ref.at[high_at], we_ref.at[1], sems.at[3]),
    ]
    for c in copies:
        c.start()
    for c in copies:
        c.wait()
    overflow(ye_ref[:, :TB], ye_ref[:, TB:], we_ref, bound_ref, par_ref, se_ref, so_ref)


def load_kernel(pair_ref, modes_ref, tiles_ref, y0_ref, w_ref, next_ref, inv, xs, sems, msem):
    mcopy = pltpu.make_async_copy(modes_ref, y0_ref, msem)
    mcopy.start()
    for t in range(TL):
        inv[pair_ref[t]] = t
    copies = {}
    slot = 0
    for r in range(RT):
        for p in target_pairs(r):
            copies[p] = pltpu.make_async_copy(
                tiles_ref.at[inv[p]], w_ref.at[pl.ds(slot * TB, TB)], sems.at[slot]
            )
            copies[p].start()
            slot += 1
    mcopy.wait()
    xs[...] = y0_ref[...].astype(BF16)
    for r in range(RT):
        for p in target_pairs(r):
            copies[p].wait()
        c0, c1 = target_columns(r)
        w0, w1 = target_rows(r)
        here = slice(r * TB, (r + 1) * TB)
        next_ref[:, here] = dot(xs[:, c0:c1], w_ref[w0:w1]) - center * y0_ref[:, here]


def edge_kernel(factor, bound_ref, par_ref, y_ref, re_ref, ro_ref, we_ref, ye_ref, se_ref, so_ref):
    even = par_ref[0] == 0
    re, ro = re_ref[...], ro_ref[...]
    low = y_ref[:, :TB] + factor * jnp.where(even, ro, re).astype(F32)
    high = y_ref[:, ROWS - TB :] + factor * jnp.where(even, re, ro).astype(F32)
    ye_ref[:, :TB] = low
    ye_ref[:, TB:] = high
    overflow(low, high, we_ref, bound_ref, par_ref, se_ref, so_ref)


def gram(y):
    return lax.dot_general(
        y, y, (((1,), (1,)), ((), ())), precision=lax.Precision.HIGHEST, preferred_element_type=F32
    )


def step_kernel(last, y_ref, ye_ref, z_ref, ze_ref, w_ref, next_ref, *rest):
    xs = rest[-1]
    xs[:, :TB] = ye_ref[:, :TB].astype(BF16)
    xs[:, TB : ROWS - TB] = y_ref[:, TB : ROWS - TB].astype(BF16)
    xs[:, ROWS - TB :] = ye_ref[:, TB:].astype(BF16)
    for r in range(RT):
        c0, c1 = target_columns(r)
        w0, w1 = target_rows(r)
        here = slice(r * TB, (r + 1) * TB)
        if r == 0:
            y, z = ye_ref[:, :TB], ze_ref[:, :TB]
        elif r == RT - 1:
            y, z = ye_ref[:, TB:], ze_ref[:, TB:]
        else:
            y, z = y_ref[:, here], z_ref[:, here]
        next_ref[:, here] = 2.0 * (dot(xs[:, c0:c1], w_ref[w0:w1]) - center * y) - z
    if last:
        rest[0][...] = gram(next_ref[:, TB : ROWS - TB])


def final_kernel(par_ref, y_ref, re_ref, ro_ref, gi_ref, ye_ref, g_ref):
    even = par_ref[0] == 0
    re, ro = re_ref[...], ro_ref[...]
    ye_ref[:, :TB] = y_ref[:, :TB] + 2.0 * jnp.where(even, ro, re).astype(F32)
    ye_ref[:, TB:] = y_ref[:, ROWS - TB :] + 2.0 * jnp.where(even, re, ro).astype(F32)
    g = gi_ref[...] + gram(ye_ref[...])
    g_ref[...] = jnp.concatenate([g[: K // 2], g[K // 2 :]], axis=1)


def whiten_kernel(scale, g_ref, y_ref, ye_ref, out_ref):
    g = g_ref[...] * scale
    g = jnp.concatenate([g[:, :K], g[:, K:]], axis=0)
    row = lax.broadcasted_iota(jnp.int32, (K, K), 0)
    col = lax.broadcasted_iota(jnp.int32, (K, K), 1)
    eye = (row == col).astype(F32)
    whole = jnp.concatenate([g, eye], axis=1)
    blocks = [whole[8 * i : 8 * i + 8] for i in range(K // 8)]
    sub = lax.broadcasted_iota(jnp.int32, (8, 1), 0)
    for k in range(K):
        b, s = divmod(k, 8)
        pivot_row = blocks[b][s : s + 1]
        scaled = pivot_row / pivot_row[:, k : k + 1]
        for i in range(b, K // 8):
            mult = blocks[i][:, k : k + 1]
            if i == b:
                mult = jnp.where(sub > s, mult, 0.0)
            blocks[i] = blocks[i] - mult * scaled
    whole = jnp.concatenate(blocks, axis=0)
    diagonal = jnp.sum(jnp.where(row == col, whole[:, :K], 0.0), axis=1, keepdims=True)
    linv = whole[:, K:] / jnp.sqrt(diagonal)

    def apply(y):
        return jnp.dot(linv, y, precision=lax.Precision.HIGHEST, preferred_element_type=F32)

    out_ref[:, :TB] = apply(ye_ref[:, :TB])
    for r in range(1, RT - 1):
        out_ref[:, r * TB : (r + 1) * TB] = apply(y_ref[:, r * TB : (r + 1) * TB])
    out_ref[:, ROWS - TB :] = apply(ye_ref[:, TB:])


def local(modes, tiles, tile_pair, boundary):
    slabs, cols = lax.axis_size("slab"), lax.axis_size("col")
    count = slabs * cols
    parity = (lax.axis_index("col") & 1).astype(jnp.int32).reshape(1)
    pairs_even = [(i, i ^ 1) for i in range(count)]
    pairs_odd = [(i, (i + 1) % count if i % 2 else (i - 1) % count) for i in range(count)]

    def exchange(se, so):
        ro = lax.ppermute(so, AXES, pairs_odd)
        re = lax.ppermute(se, AXES, pairs_even)
        return re, ro

    send = vmem((K, TB), BF16)
    edges = vmem((K, 2 * TB), F32)
    block = vmem((K, ROWS), F32)
    we, ye, se, so = pl.pallas_call(
        first_kernel,
        out_shape=(vmem((2, TB, TB), BF16), edges, send, send),
        in_specs=[SM, SM, SM, ANY, ANY],
        out_specs=(VM, VM, VM, VM),
        scratch_shapes=[pltpu.SemaphoreType.DMA((4,))],
        compiler_params=params(8),
        name="first",
    )(tile_pair, boundary, parity, modes, tiles)
    re, ro = exchange(se, so)
    flops = 2 * K * TB * TB * 22
    y0, w, y = pl.pallas_call(
        load_kernel,
        out_shape=(block, vmem(((TL - 2) * TB, TB), BF16), block),
        in_specs=[SM, ANY, ANY],
        out_specs=(VM, VM, VM),
        scratch_shapes=[
            pltpu.SMEM((TL,), jnp.int32),
            pltpu.VMEM((K, ROWS), BF16),
            pltpu.SemaphoreType.DMA((TL - 2,)),
            pltpu.SemaphoreType.DMA,
        ],
        compiler_params=params(16),
        cost_estimate=pl.CostEstimate(flops=flops, bytes_accessed=8 << 20, transcendentals=0),
        name="load",
    )(tile_pair, modes, tiles)
    z, ze = y0, ye
    for k in range(1, DEG):
        ye, se, so = pl.pallas_call(
            functools.partial(edge_kernel, 1.0 if k == 1 else 2.0),
            out_shape=(edges, send, send),
            in_specs=[SM, SM, VM, VM, VM, VM],
            out_specs=(VM, VM, VM),
            compiler_params=params(8),
            name="edge",
        )(boundary, parity, pin(y), re, ro, pin(we))
        re, ro = exchange(se, so)
        last = k == DEG - 1
        outs = pl.pallas_call(
            functools.partial(step_kernel, last),
            out_shape=(block, vmem((K, K), F32)) if last else block,
            in_specs=[VM] * 5,
            out_specs=(VM, VM) if last else VM,
            scratch_shapes=[pltpu.VMEM((K, ROWS), BF16)],
            compiler_params=params(12),
            cost_estimate=pl.CostEstimate(flops=flops, bytes_accessed=8 << 20, transcendentals=0),
            name="step",
        )(pin(y), pin(ye), pin(z), pin(ze), pin(w))
        z, ze = y, ye
        if last:
            y, gi = outs
        else:
            y = outs
    ye, g = pl.pallas_call(
        final_kernel,
        out_shape=(edges, vmem((K // 2, 2 * K), F32)),
        in_specs=[SM, VM, VM, VM, VM],
        out_specs=(VM, VM),
        compiler_params=params(8),
        name="final",
    )(parity, pin(y), re, ro, pin(gi))
    stride = 1
    for axis_bits in ((1, 3), (4, 12), (16,), (32, 96)):
        for bits in axis_bits:
            g = g + lax.ppermute(g, AXES, [(i, i ^ bits) for i in range(count)])
    return pl.pallas_call(
        functools.partial(whiten_kernel, 1.0 / (ROWS * count)),
        out_shape=jax.ShapeDtypeStruct((K, ROWS), F32),
        in_specs=[VM, VM, VM],
        out_specs=VM,
        compiler_params=params(16),
        name="whiten",
    )(g, pin(y), pin(ye))


def solution(mesh):
    placed = (
        P(None, AXES),
        P(AXES, None, None),
        P(AXES),
        P(AXES, None),
    )
    return jax.shard_map(
        local, mesh=mesh, in_specs=placed, out_specs=P(None, AXES), check_vma=False
    )
```

profile of v0, /device:TPU:0, one launch (start us, length us, event | category | flops | bytes accessed | tf_op | source)
XLA Modules:
  0.0 124.2 jit_solution(1190496271950681306)
XLA Ops:
  0.0 3.0 %copy-done = bf16[24,384,384]{2,1,0:T(8,128)(2,1)S(1)} copy-done((bf16[24,384,384]{2,1,0:T(8,128)(2,1)S(1)}, bf16[24,384,384]{2,1,0:T(8,128)(2,1)}, u32[]{:S(2)}) %copy-start) | copy-done | bytes 7077912
  6.5 1.7 %collective-permute-start = (bf16[64,384]{1,0:T(8,128)(2,1)S(1)}, bf16[64,384]{1,0:T(8,128)(2,1)S(1)}, u32[]{:S(2)}, u32[]{:S(2)}) collective-permute-start(bf16[64,384]{1,0:T(8,128)(2,1)S(1)} %get-tuple-element.38), channel_id=1, source_target_pairs={{0,1},{1,0},{2,3},{3,2},{4,5},{5,4},{6,7},{7,6},{8,9},{9,8},{10,11... | collective-permute-start | bytes 147464 | tf_op jit(solution)/shard_map/ppermute | solution.py:195
  8.2 7.0 %collective-permute-start.1 = (bf16[64,384]{1,0:T(8,128)(2,1)S(1)}, bf16[64,384]{1,0:T(8,128)(2,1)S(1)}, u32[]{:S(2)}, u32[]{:S(2)}) collective-permute-start(bf16[64,384]{1,0:T(8,128)(2,1)S(1)} %get-tuple-element.39), channel_id=1, source_target_pairs={{0,127},{1,2},{2,1},{3,4},{4,3},{5,6},{6,5},{7,8},{8,7},{9,10},{10... | collective-permute-start | bytes 147464 | tf_op jit(solution)/shard_map/ppermute | solution.py:194
  15.2 4.6 %load.1 = (f32[64,3072]{1,0:T(8,128)S(1)}, bf16[8448,384]{1,0:T(8,128)(2,1)S(1)}, f32[64,3072]{1,0:T(8,128)S(1)}) custom-call(s32[24]{0:T(128)S(1)} %copy-done.7, f32[64,3072]{1,0:T(8,128)S(1)} %copy-done.3, bf16[24,384,384]{2,1,0:T(8,128)(2,1)S(1)} %copy-done.1), custom_call_target="tpu_custom_call" | custom-call | flops 415236096 | bytes 8388608 | tf_op jit(solution)/shard_map/load/pallas_call | solution.py:212
  20.8 4.3 %collective-permute-start.3 = (bf16[64,384]{1,0:T(8,128)(2,1)S(1)}, bf16[64,384]{1,0:T(8,128)(2,1)S(1)}, u32[]{:S(2)}, u32[]{:S(2)}) collective-permute-start(bf16[64,384]{1,0:T(8,128)(2,1)S(1)} %get-tuple-element.46), channel_id=1, source_target_pairs={{0,127},{1,2},{2,1},{3,4},{4,3},{5,6},{6,5},{7,8},{8,7},{9,10},{10... | collective-permute-start | bytes 147464 | tf_op jit(solution)/shard_map/ppermute | solution.py:194
  26.3 3.5 %collective-permute-done.3.ro_ref = bf16[64,384]{1,0:T(8,128)(2,1)S(1)} collective-permute-done((bf16[64,384]{1,0:T(8,128)(2,1)S(1)}, bf16[64,384]{1,0:T(8,128)(2,1)S(1)}, u32[]{:S(2)}, u32[]{:S(2)}) %collective-permute-start.3) | collective-permute-done | bytes 49184 | tf_op jit(solution)/shard_map/ppermute | solution.py:194
  30.7 4.3 %collective-permute-start.5 = (bf16[64,384]{1,0:T(8,128)(2,1)S(1)}, bf16[64,384]{1,0:T(8,128)(2,1)S(1)}, u32[]{:S(2)}, u32[]{:S(2)}) collective-permute-start(bf16[64,384]{1,0:T(8,128)(2,1)S(1)} %get-tuple-element.49), channel_id=1, source_target_pairs={{0,127},{1,2},{2,1},{3,4},{4,3},{5,6},{6,5},{7,8},{8,7},{9,10},{10... | collective-permute-start | bytes 147464 | tf_op jit(solution)/shard_map/ppermute | solution.py:194
  35.0 1.2 step.8.y_ref.z_ref
  36.2 3.5 %collective-permute-done.5.ro_ref = bf16[64,384]{1,0:T(8,128)(2,1)S(1)} collective-permute-done((bf16[64,384]{1,0:T(8,128)(2,1)S(1)}, bf16[64,384]{1,0:T(8,128)(2,1)S(1)}, u32[]{:S(2)}, u32[]{:S(2)}) %collective-permute-start.5) | collective-permute-done | bytes 49184 | tf_op jit(solution)/shard_map/ppermute | solution.py:194
  40.6 4.3 %collective-permute-start.7 = (bf16[64,384]{1,0:T(8,128)(2,1)S(1)}, bf16[64,384]{1,0:T(8,128)(2,1)S(1)}, u32[]{:S(2)}, u32[]{:S(2)}) collective-permute-start(bf16[64,384]{1,0:T(8,128)(2,1)S(1)} %get-tuple-element.52), channel_id=1, source_target_pairs={{0,127},{1,2},{2,1},{3,4},{4,3},{5,6},{6,5},{7,8},{8,7},{9,10},{10... | collective-permute-start | bytes 147464 | tf_op jit(solution)/shard_map/ppermute | solution.py:194
  44.9 1.2 step.9.y_ref.z_ref
  46.1 3.5 %collective-permute-done.7.ro_ref = bf16[64,384]{1,0:T(8,128)(2,1)S(1)} collective-permute-done((bf16[64,384]{1,0:T(8,128)(2,1)S(1)}, bf16[64,384]{1,0:T(8,128)(2,1)S(1)}, u32[]{:S(2)}, u32[]{:S(2)}) %collective-permute-start.7) | collective-permute-done | bytes 49184 | tf_op jit(solution)/shard_map/ppermute | solution.py:194
  50.5 4.4 %collective-permute-start.9 = (bf16[64,384]{1,0:T(8,128)(2,1)S(1)}, bf16[64,384]{1,0:T(8,128)(2,1)S(1)}, u32[]{:S(2)}, u32[]{:S(2)}) collective-permute-start(bf16[64,384]{1,0:T(8,128)(2,1)S(1)} %get-tuple-element.55), channel_id=1, source_target_pairs={{0,127},{1,2},{2,1},{3,4},{4,3},{5,6},{6,5},{7,8},{8,7},{9,10},{10... | collective-permute-start | bytes 147464 | tf_op jit(solution)/shard_map/ppermute | solution.py:194
  54.9 1.2 step.10.y_ref.z_ref
  56.1 3.4 %collective-permute-done.9.ro_ref = bf16[64,384]{1,0:T(8,128)(2,1)S(1)} collective-permute-done((bf16[64,384]{1,0:T(8,128)(2,1)S(1)}, bf16[64,384]{1,0:T(8,128)(2,1)S(1)}, u32[]{:S(2)}, u32[]{:S(2)}) %collective-permute-start.9) | collective-permute-done | bytes 49184 | tf_op jit(solution)/shard_map/ppermute | solution.py:194
  60.4 4.4 %collective-permute-start.11 = (bf16[64,384]{1,0:T(8,128)(2,1)S(1)}, bf16[64,384]{1,0:T(8,128)(2,1)S(1)}, u32[]{:S(2)}, u32[]{:S(2)}) collective-permute-start(bf16[64,384]{1,0:T(8,128)(2,1)S(1)} %get-tuple-element.58), channel_id=1, source_target_pairs={{0,127},{1,2},{2,1},{3,4},{4,3},{5,6},{6,5},{7,8},{8,7},{9,10},{10... | collective-permute-start | bytes 147464 | tf_op jit(solution)/shard_map/ppermute | solution.py:194
  64.8 1.2 step.11.y_ref.z_ref
  66.0 3.4 %collective-permute-done.11.ro_ref = bf16[64,384]{1,0:T(8,128)(2,1)S(1)} collective-permute-done((bf16[64,384]{1,0:T(8,128)(2,1)S(1)}, bf16[64,384]{1,0:T(8,128)(2,1)S(1)}, u32[]{:S(2)}, u32[]{:S(2)}) %collective-permute-start.11) | collective-permute-done | bytes 49184 | tf_op jit(solution)/shard_map/ppermute | solution.py:194
  70.4 4.4 %collective-permute-start.13 = (bf16[64,384]{1,0:T(8,128)(2,1)S(1)}, bf16[64,384]{1,0:T(8,128)(2,1)S(1)}, u32[]{:S(2)}, u32[]{:S(2)}) collective-permute-start(bf16[64,384]{1,0:T(8,128)(2,1)S(1)} %get-tuple-element.61), channel_id=1, source_target_pairs={{0,127},{1,2},{2,1},{3,4},{4,3},{5,6},{6,5},{7,8},{8,7},{9,10},{10... | collective-permute-start | bytes 147464 | tf_op jit(solution)/shard_map/ppermute | solution.py:194
  74.9 1.2 step.12.y_ref
  76.1 3.4 %collective-permute-done.13.ro_ref = bf16[64,384]{1,0:T(8,128)(2,1)S(1)} collective-permute-done((bf16[64,384]{1,0:T(8,128)(2,1)S(1)}, bf16[64,384]{1,0:T(8,128)(2,1)S(1)}, u32[]{:S(2)}, u32[]{:S(2)}) %collective-permute-start.13) | collective-permute-done | bytes 49184 | tf_op jit(solution)/shard_map/ppermute | solution.py:194
  80.3 4.4 %collective-permute-start.15 = (bf16[64,384]{1,0:T(8,128)(2,1)S(1)}, bf16[64,384]{1,0:T(8,128)(2,1)S(1)}, u32[]{:S(2)}, u32[]{:S(2)}) collective-permute-start(bf16[64,384]{1,0:T(8,128)(2,1)S(1)} %get-tuple-element.65), channel_id=1, source_target_pairs={{0,127},{1,2},{2,1},{3,4},{4,3},{5,6},{6,5},{7,8},{8,7},{9,10},{10... | collective-permute-start | bytes 147464 | tf_op jit(solution)/shard_map/ppermute | solution.py:194
  84.8 1.9 %step.13 = (f32[64,3072]{1,0:T(8,128)S(1)}, f32[64,64]{1,0:T(8,128)S(1)}) custom-call(f32[64,3072]{1,0:T(8,128)S(1)} %step.12.y_ref, f32[64,768]{1,0:T(8,128)S(1)} %get-tuple-element.62.ye_ref, f32[64,3072]{1,0:T(8,128)S(1)} %step.11.y_ref.z_ref, f32[64,768]{1,0:T(8,128)S(1)} %get-tuple-element.59.ye_ref.ze_ref, bf16[8448,384]{1,0:T(8,128)(2,1)S(1)} %get-tuple-element.44.w_ref), custom_call_target="tpu_custom_call" | custom-call | flops 415236096 | bytes 8388608 | tf_op jit(solution)/shard_map/step/pallas_call | solution.py:239
  86.7 2.7 %collective-permute-done.15.ro_ref = bf16[64,384]{1,0:T(8,128)(2,1)S(1)} collective-permute-done((bf16[64,384]{1,0:T(8,128)(2,1)S(1)}, bf16[64,384]{1,0:T(8,128)(2,1)S(1)}, u32[]{:S(2)}, u32[]{:S(2)}) %collective-permute-start.15) | collective-permute-done | bytes 49184 | tf_op jit(solution)/shard_map/ppermute | solution.py:194
  89.8 3.7 %collective-permute-done.16 = f32[32,128]{1,0:T(8,128)S(1)} collective-permute-done((f32[32,128]{1,0:T(8,128)S(1)}, f32[32,128]{1,0:T(8,128)S(1)}, u32[]{:S(2)}, u32[]{:S(2)}) %collective-permute-start.16) | collective-permute-done | bytes 16416 | tf_op jit(solution)/shard_map/ppermute | solution.py:265
  93.5 4.9 %collective-permute-done.17 = f32[32,128]{1,0:T(8,128)S(1)} collective-permute-done((f32[32,128]{1,0:T(8,128)S(1)}, f32[32,128]{1,0:T(8,128)S(1)}, u32[]{:S(2)}, u32[]{:S(2)}) %collective-permute-start.17) | collective-permute-done | bytes 16416 | tf_op jit(solution)/shard_map/ppermute | solution.py:265
  98.5 3.7 %collective-permute-done.18 = f32[32,128]{1,0:T(8,128)S(1)} collective-permute-done((f32[32,128]{1,0:T(8,128)S(1)}, f32[32,128]{1,0:T(8,128)S(1)}, u32[]{:S(2)}, u32[]{:S(2)}) %collective-permute-start.18) | collective-permute-done | bytes 16416 | tf_op jit(solution)/shard_map/ppermute | solution.py:265
  102.2 4.9 %collective-permute-done.19 = f32[32,128]{1,0:T(8,128)S(1)} collective-permute-done((f32[32,128]{1,0:T(8,128)S(1)}, f32[32,128]{1,0:T(8,128)S(1)}, u32[]{:S(2)}, u32[]{:S(2)}) %collective-permute-start.19) | collective-permute-done | bytes 16416 | tf_op jit(solution)/shard_map/ppermute | solution.py:265
  107.2 1.2 collective-permute-done.20
  108.4 3.7 %collective-permute-done.21 = f32[32,128]{1,0:T(8,128)S(1)} collective-permute-done((f32[32,128]{1,0:T(8,128)S(1)}, f32[32,128]{1,0:T(8,128)S(1)}, u32[]{:S(2)}, u32[]{:S(2)}) %collective-permute-start.21) | collective-permute-done | bytes 16416 | tf_op jit(solution)/shard_map/ppermute | solution.py:265
  112.1 4.9 %collective-permute-done.22 = f32[32,128]{1,0:T(8,128)S(1)} collective-permute-done((f32[32,128]{1,0:T(8,128)S(1)}, f32[32,128]{1,0:T(8,128)S(1)}, u32[]{:S(2)}, u32[]{:S(2)}) %collective-permute-start.22) | collective-permute-done | bytes 16416 | tf_op jit(solution)/shard_map/ppermute | solution.py:265
  117.1 7.2 %whiten.1 = f32[64,3072]{1,0:T(8,128)} custom-call(f32[32,128]{1,0:T(8,128)S(1)} %add.27.g_ref, f32[64,3072]{1,0:T(8,128)S(1)} %get-tuple-element.63.y_ref, f32[64,768]{1,0:T(8,128)S(1)} %get-tuple-element.68.ye_ref), custom_call_target="tpu_custom_call" | custom-call | tf_op jit(solution)/shard_map/whiten/pallas_call | solution.py:266
  (55 shorter events, 11.3 us)
Async XLA Ops:
  0.0 15.2 %copy-start.7 = (s32[24]{0:T(128)S(1)}, s32[24]{0:T(128)}, u32[]{:S(2)}) copy-start(s32[24]{0:T(128)} %pair_ref.3) | copy-start | bytes 292
  0.0 3.0 %copy-start = (bf16[24,384,384]{2,1,0:T(8,128)(2,1)S(1)}, bf16[24,384,384]{2,1,0:T(8,128)(2,1)}, u32[]{:S(2)}) copy-start(bf16[24,384,384]{2,1,0:T(8,128)(2,1)} %tiles_ref.3) | copy-start | bytes 21233668
  3.0 1.1 copy-start.2
  4.2 0.7 copy-start.4
  4.8 0.7 copy-start.6
  5.5 9.8 %copy-start.1 = (bf16[24,384,384]{2,1,0:T(8,128)(2,1)S(1)}, bf16[24,384,384]{2,1,0:T(8,128)(2,1)}, u32[]{:S(2)}) copy-start(bf16[24,384,384]{2,1,0:T(8,128)(2,1)} %tiles_ref.3) | copy-start | bytes 21233668
  5.5 9.8 %copy-start.3 = (f32[64,3072]{1,0:T(8,128)S(1)}, f32[64,3072]{1,0:T(8,128)}, u32[]{:S(2)}) copy-start(f32[64,3072]{1,0:T(8,128)} %modes_ref.3) | copy-start | bytes 2359300
  5.5 14.4 %copy-start.5 = (s32[1,2]{1,0:T(1,128)S(1)}, s32[1,2]{1,0:T(1,128)}, u32[]{:S(2)}) copy-start(s32[1,2]{1,0:T(1,128)} %bound_ref.15) | copy-start | bytes 28
  6.5 13.4 %collective-permute-start = (bf16[64,384]{1,0:T(8,128)(2,1)S(1)}, bf16[64,384]{1,0:T(8,128)(2,1)S(1)}, u32[]{:S(2)}, u32[]{:S(2)}) collective-permute-start(bf16[64,384]{1,0:T(8,128)(2,1)S(1)} %get-tuple-element.38), channel_id=1, source_target_pairs={{0,1},{1,0},{2,3},{3,2},{4,5},{5,4},{6,7},{7,6},{8,9},{9,8},{10,11... | collective-permute-start | bytes 147464 | tf_op jit(solution)/shard_map/ppermute | solution.py:195
  8.2 11.7 %collective-permute-start.1 = (bf16[64,384]{1,0:T(8,128)(2,1)S(1)}, bf16[64,384]{1,0:T(8,128)(2,1)S(1)}, u32[]{:S(2)}, u32[]{:S(2)}) collective-permute-start(bf16[64,384]{1,0:T(8,128)(2,1)S(1)} %get-tuple-element.39), channel_id=1, source_target_pairs={{0,127},{1,2},{2,1},{3,4},{4,3},{5,6},{6,5},{7,8},{8,7},{9,10},{10... | collective-permute-start | bytes 147464 | tf_op jit(solution)/shard_map/ppermute | solution.py:194
  20.7 5.6 %collective-permute-start.2 = (bf16[64,384]{1,0:T(8,128)(2,1)S(1)}, bf16[64,384]{1,0:T(8,128)(2,1)S(1)}, u32[]{:S(2)}, u32[]{:S(2)}) collective-permute-start(bf16[64,384]{1,0:T(8,128)(2,1)S(1)} %get-tuple-element.45), channel_id=1, source_target_pairs={{0,1},{1,0},{2,3},{3,2},{4,5},{5,4},{6,7},{7,6},{8,9},{9,8},{10,11... | collective-permute-start | bytes 147464 | tf_op jit(solution)/shard_map/ppermute | solution.py:195
  20.8 9.0 %collective-permute-start.3 = (bf16[64,384]{1,0:T(8,128)(2,1)S(1)}, bf16[64,384]{1,0:T(8,128)(2,1)S(1)}, u32[]{:S(2)}, u32[]{:S(2)}) collective-permute-start(bf16[64,384]{1,0:T(8,128)(2,1)S(1)} %get-tuple-element.46), channel_id=1, source_target_pairs={{0,127},{1,2},{2,1},{3,4},{4,3},{5,6},{6,5},{7,8},{8,7},{9,10},{10... | collective-permute-start | bytes 147464 | tf_op jit(solution)/shard_map/ppermute | solution.py:194
  30.6 5.6 %collective-permute-start.4 = (bf16[64,384]{1,0:T(8,128)(2,1)S(1)}, bf16[64,384]{1,0:T(8,128)(2,1)S(1)}, u32[]{:S(2)}, u32[]{:S(2)}) collective-permute-start(bf16[64,384]{1,0:T(8,128)(2,1)S(1)} %get-tuple-element.48), channel_id=1, source_target_pairs={{0,1},{1,0},{2,3},{3,2},{4,5},{5,4},{6,7},{7,6},{8,9},{9,8},{10,11... | collective-permute-start | bytes 147464 | tf_op jit(solution)/shard_map/ppermute | solution.py:195
  30.7 9.0 %collective-permute-start.5 = (bf16[64,384]{1,0:T(8,128)(2,1)S(1)}, bf16[64,384]{1,0:T(8,128)(2,1)S(1)}, u32[]{:S(2)}, u32[]{:S(2)}) collective-permute-start(bf16[64,384]{1,0:T(8,128)(2,1)S(1)} %get-tuple-element.49), channel_id=1, source_target_pairs={{0,127},{1,2},{2,1},{3,4},{4,3},{5,6},{6,5},{7,8},{8,7},{9,10},{10... | collective-permute-start | bytes 147464 | tf_op jit(solution)/shard_map/ppermute | solution.py:194
  40.5 5.6 %collective-permute-start.6 = (bf16[64,384]{1,0:T(8,128)(2,1)S(1)}, bf16[64,384]{1,0:T(8,128)(2,1)S(1)}, u32[]{:S(2)}, u32[]{:S(2)}) collective-permute-start(bf16[64,384]{1,0:T(8,128)(2,1)S(1)} %get-tuple-element.51), channel_id=1, source_target_pairs={{0,1},{1,0},{2,3},{3,2},{4,5},{5,4},{6,7},{7,6},{8,9},{9,8},{10,11... | collective-permute-start | bytes 147464 | tf_op jit(solution)/shard_map/ppermute | solution.py:195
  40.6 9.0 %collective-permute-start.7 = (bf16[64,384]{1,0:T(8,128)(2,1)S(1)}, bf16[64,384]{1,0:T(8,128)(2,1)S(1)}, u32[]{:S(2)}, u32[]{:S(2)}) collective-permute-start(bf16[64,384]{1,0:T(8,128)(2,1)S(1)} %get-tuple-element.52), channel_id=1, source_target_pairs={{0,127},{1,2},{2,1},{3,4},{4,3},{5,6},{6,5},{7,8},{8,7},{9,10},{10... | collective-permute-start | bytes 147464 | tf_op jit(solution)/shard_map/ppermute | solution.py:194
  50.4 5.7 %collective-permute-start.8 = (bf16[64,384]{1,0:T(8,128)(2,1)S(1)}, bf16[64,384]{1,0:T(8,128)(2,1)S(1)}, u32[]{:S(2)}, u32[]{:S(2)}) collective-permute-start(bf16[64,384]{1,0:T(8,128)(2,1)S(1)} %get-tuple-element.54), channel_id=1, source_target_pairs={{0,1},{1,0},{2,3},{3,2},{4,5},{5,4},{6,7},{7,6},{8,9},{9,8},{10,11... | collective-permute-start | bytes 147464 | tf_op jit(solution)/shard_map/ppermute | solution.py:195
  50.5 9.0 %collective-permute-start.9 = (bf16[64,384]{1,0:T(8,128)(2,1)S(1)}, bf16[64,384]{1,0:T(8,128)(2,1)S(1)}, u32[]{:S(2)}, u32[]{:S(2)}) collective-permute-start(bf16[64,384]{1,0:T(8,128)(2,1)S(1)} %get-tuple-element.55), channel_id=1, source_target_pairs={{0,127},{1,2},{2,1},{3,4},{4,3},{5,6},{6,5},{7,8},{8,7},{9,10},{10... | collective-permute-start | bytes 147464 | tf_op jit(solution)/shard_map/ppermute | solution.py:194
  60.3 5.7 %collective-permute-start.10 = (bf16[64,384]{1,0:T(8,128)(2,1)S(1)}, bf16[64,384]{1,0:T(8,128)(2,1)S(1)}, u32[]{:S(2)}, u32[]{:S(2)}) collective-permute-start(bf16[64,384]{1,0:T(8,128)(2,1)S(1)} %get-tuple-element.57), channel_id=1, source_target_pairs={{0,1},{1,0},{2,3},{3,2},{4,5},{5,4},{6,7},{7,6},{8,9},{9,8},{10,11... | collective-permute-start | bytes 147464 | tf_op jit(solution)/shard_map/ppermute | solution.py:195
  60.4 9.0 %collective-permute-start.11 = (bf16[64,384]{1,0:T(8,128)(2,1)S(1)}, bf16[64,384]{1,0:T(8,128)(2,1)S(1)}, u32[]{:S(2)}, u32[]{:S(2)}) collective-permute-start(bf16[64,384]{1,0:T(8,128)(2,1)S(1)} %get-tuple-element.58), channel_id=1, source_target_pairs={{0,127},{1,2},{2,1},{3,4},{4,3},{5,6},{6,5},{7,8},{8,7},{9,10},{10... | collective-permute-start | bytes 147464 | tf_op jit(solution)/shard_map/ppermute | solution.py:194
  70.2 5.9 %collective-permute-start.12 = (bf16[64,384]{1,0:T(8,128)(2,1)S(1)}, bf16[64,384]{1,0:T(8,128)(2,1)S(1)}, u32[]{:S(2)}, u32[]{:S(2)}) collective-permute-start(bf16[64,384]{1,0:T(8,128)(2,1)S(1)} %get-tuple-element.60), channel_id=1, source_target_pairs={{0,1},{1,0},{2,3},{3,2},{4,5},{5,4},{6,7},{7,6},{8,9},{9,8},{10,11... | collective-permute-start | bytes 147464 | tf_op jit(solution)/shard_map/ppermute | solution.py:195
  70.4 9.0 %collective-permute-start.13 = (bf16[64,384]{1,0:T(8,128)(2,1)S(1)}, bf16[64,384]{1,0:T(8,128)(2,1)S(1)}, u32[]{:S(2)}, u32[]{:S(2)}) collective-permute-start(bf16[64,384]{1,0:T(8,128)(2,1)S(1)} %get-tuple-element.61), channel_id=1, source_target_pairs={{0,127},{1,2},{2,1},{3,4},{4,3},{5,6},{6,5},{7,8},{8,7},{9,10},{10... | collective-permute-start | bytes 147464 | tf_op jit(solution)/shard_map/ppermute | solution.py:194
  80.2 6.4 %collective-permute-start.14 = (bf16[64,384]{1,0:T(8,128)(2,1)S(1)}, bf16[64,384]{1,0:T(8,128)(2,1)S(1)}, u32[]{:S(2)}, u32[]{:S(2)}) collective-permute-start(bf16[64,384]{1,0:T(8,128)(2,1)S(1)} %get-tuple-element.64), channel_id=1, source_target_pairs={{0,1},{1,0},{2,3},{3,2},{4,5},{5,4},{6,7},{7,6},{8,9},{9,8},{10,11... | collective-permute-start | bytes 147464 | tf_op jit(solution)/shard_map/ppermute | solution.py:195
  80.3 9.0 %collective-permute-start.15 = (bf16[64,384]{1,0:T(8,128)(2,1)S(1)}, bf16[64,384]{1,0:T(8,128)(2,1)S(1)}, u32[]{:S(2)}, u32[]{:S(2)}) collective-permute-start(bf16[64,384]{1,0:T(8,128)(2,1)S(1)} %get-tuple-element.65), channel_id=1, source_target_pairs={{0,127},{1,2},{2,1},{3,4},{4,3},{5,6},{6,5},{7,8},{8,7},{9,10},{10... | collective-permute-start | bytes 147464 | tf_op jit(solution)/shard_map/ppermute | solution.py:194
  89.8 3.8 %collective-permute-start.16 = (f32[32,128]{1,0:T(8,128)S(1)}, f32[32,128]{1,0:T(8,128)S(1)}, u32[]{:S(2)}, u32[]{:S(2)}) collective-permute-start(f32[32,128]{1,0:T(8,128)S(1)} %get-tuple-element.67), channel_id=1, source_target_pairs={{0,1},{1,0},{2,3},{3,2},{4,5},{5,4},{6,7},{7,6},{8,9},{9,8},{10,11... | collective-permute-start | bytes 49160 | tf_op jit(solution)/shard_map/ppermute | solution.py:265
  93.5 4.9 %collective-permute-start.17 = (f32[32,128]{1,0:T(8,128)S(1)}, f32[32,128]{1,0:T(8,128)S(1)}, u32[]{:S(2)}, u32[]{:S(2)}) collective-permute-start(f32[32,128]{1,0:T(8,128)S(1)} %add.21), channel_id=1, source_target_pairs={{0,3},{1,2},{2,1},{3,0},{4,7},{5,6},{6,5},{7,4},{8,11},{9,10},{10,... | collective-permute-start | bytes 49160 | tf_op jit(solution)/shard_map/ppermute | solution.py:265
  98.5 3.7 %collective-permute-start.18 = (f32[32,128]{1,0:T(8,128)S(1)}, f32[32,128]{1,0:T(8,128)S(1)}, u32[]{:S(2)}, u32[]{:S(2)}) collective-permute-start(f32[32,128]{1,0:T(8,128)S(1)} %add.22), channel_id=1, source_target_pairs={{0,4},{1,5},{2,6},{3,7},{4,0},{5,1},{6,2},{7,3},{8,12},{9,13},{10,... | collective-permute-start | bytes 49160 | tf_op jit(solution)/shard_map/ppermute | solution.py:265
  102.2 4.9 %collective-permute-start.19 = (f32[32,128]{1,0:T(8,128)S(1)}, f32[32,128]{1,0:T(8,128)S(1)}, u32[]{:S(2)}, u32[]{:S(2)}) collective-permute-start(f32[32,128]{1,0:T(8,128)S(1)} %add.23), channel_id=1, source_target_pairs={{0,12},{1,13},{2,14},{3,15},{4,8},{5,9},{6,10},{7,11},{8,4},{9,5},... | collective-permute-start | bytes 49160 | tf_op jit(solution)/shard_map/ppermute | solution.py:265
  107.2 1.2 collective-permute-start.20
  108.4 3.7 %collective-permute-start.21 = (f32[32,128]{1,0:T(8,128)S(1)}, f32[32,128]{1,0:T(8,128)S(1)}, u32[]{:S(2)}, u32[]{:S(2)}) collective-permute-start(f32[32,128]{1,0:T(8,128)S(1)} %add.25), channel_id=1, source_target_pairs={{0,32},{1,33},{2,34},{3,35},{4,36},{5,37},{6,38},{7,39},{8,40},{9,... | collective-permute-start | bytes 49160 | tf_op jit(solution)/shard_map/ppermute | solution.py:265
  112.1 4.9 %collective-permute-start.22 = (f32[32,128]{1,0:T(8,128)S(1)}, f32[32,128]{1,0:T(8,128)S(1)}, u32[]{:S(2)}, u32[]{:S(2)}) collective-permute-start(f32[32,128]{1,0:T(8,128)S(1)} %add.26), channel_id=1, source_target_pairs={{0,96},{1,97},{2,98},{3,99},{4,100},{5,101},{6,102},{7,103},{8,104... | collective-permute-start | bytes 49160 | tf_op jit(solution)/shard_map/ppermute | solution.py:265
where the time goes:
time: 124 us
  waiting for transfers between devices  50.5 us (41%)
  starting transfers between devices  40.3 us (32%)
  Pallas kernels  27.5 us (22%)
  local copies, waits for them, and re-layouts  5.48 us (4%)
    ppermute x8, starting transfers between devices, exchange(): ro = lax.ppermute(so, AXES, pairs_odd)  37.8 us
    ppermute x7, waiting for transfers between devices, local(): g = g + lax.ppermute(g, AXES, [(i, i ^ bits) for i in range(count)])  27.2 us
    ppermute x8, waiting for transfers between devices, exchange(): ro = lax.ppermute(so, AXES, pairs_odd)  23.3 us
    pallas_call x7, Pallas kernels, local(): pl.pallas_call(functools.partial(step_kernel, last), out_shape=(block, vm...  8.98 us
    pallas_call x1, Pallas kernels, local(): pl.pallas_call(functools.partial(whiten_kernel, 1.0 / (ROWS * count)), ou...  7.16 us
    unnamed x16, local copies, waits for them, and re-layouts  5.48 us
    pallas_call x7, Pallas kernels, local(): pl.pallas_call(functools.partial(edge_kernel, 1.0 if k == 1 else 2.0), ou...  5.38 us
    pallas_call x1, Pallas kernels, local(): pl.pallas_call(load_kernel, out_shape=(block, vmem(((TL - 2) * TB, TB), B...  4.63 us
  transfers between devices with their start and end apart: 23, of which 14 were waited for; matrix products, arithmetic and copies ran while one was open for 0% of the time, Pallas kernels for 11%

commit v1 on v0

v1 whole, which is shorter than its diff:
```python
import functools

import jax
import jax.numpy as jnp
from jax import lax
from jax.experimental import pallas as pl
from jax.experimental.pallas import tpu as pltpu
from jax.sharding import PartitionSpec as P

DEG = 8
center = 0.25
AXES = ("slab", "col")
K = 64
TB = 384
RT = 8
TL = 24
ROWS = RT * TB
F32 = jnp.float32
BF16 = jnp.bfloat16

VM = pl.BlockSpec(memory_space=pltpu.VMEM)
SM = pl.BlockSpec(memory_space=pltpu.SMEM)
HBM = pl.BlockSpec(memory_space=pltpu.HBM)


def pin(x):
    return pltpu.with_memory_space_constraint(x, pltpu.VMEM)


def hbm(x):
    return pltpu.with_memory_space_constraint(x, pltpu.HBM)


def params(mib):
    return pltpu.CompilerParams(vmem_limit_bytes=mib << 20)


def cost(tile_products):
    return pl.CostEstimate(flops=2 * K * TB * TB * tile_products, bytes_accessed=8 << 20, transcendentals=0)


def dot(a, b):
    return jnp.dot(a, b, preferred_element_type=F32)


def tile(i, n=1):
    return slice(i * TB, (i + n) * TB)


OUTER = [1, 3, 20, 22]
INNER = [3 * c + (r - c) + 1 for r in range(1, RT - 1) for c in (r - 1, r, r + 1)]


def inner(r, first=0, count=3):
    return tile(3 * (r - 1) + first, count)


def first_kernel(
    bound_ref, par_ref, pair_ref, modes_ref, tiles_ref,
    outer_ref, we_ref, z_ref, se_ref, so_ref, inv_ref,
    pair, bound, ym, sems, ssem,
):
    to_smem = pltpu.make_async_copy(pair_ref, pair, ssem.at[0])
    to_smem.start()
    bound_copy = pltpu.make_async_copy(bound_ref, bound, ssem.at[1])
    bound_copy.start()
    modes = [
        pltpu.make_async_copy(modes_ref.at[:, tile(0, 2)], ym.at[:, tile(0, 2)], sems.at[6]),
        pltpu.make_async_copy(modes_ref.at[:, tile(6, 2)], ym.at[:, tile(2, 2)], sems.at[7]),
    ]
    for c in modes:
        c.start()
    to_smem.wait()
    for t in range(TL):
        inv_ref[pair[t]] = t
    copies = [
        pltpu.make_async_copy(tiles_ref.at[inv_ref[p]], outer_ref.at[tile(i)], sems.at[i])
        for i, p in enumerate(OUTER)
    ] + [
        pltpu.make_async_copy(tiles_ref.at[inv_ref[p]], we_ref.at[tile(i)], sems.at[4 + i])
        for i, p in enumerate((0, TL - 1))
    ]
    for c in copies:
        c.start()
    bound_copy.wait()
    for c in modes + copies:
        c.wait()
    row = lax.broadcasted_iota(jnp.int32, (TB, TB), 0)
    zero = jnp.zeros((TB, TB), BF16)
    w_low = jnp.where(row < bound[0, 0], we_ref[tile(0)], zero)
    w_high = jnp.where(row >= TB - bound[0, 1], we_ref[tile(1)], zero)
    we_ref[tile(0)] = w_low
    we_ref[tile(1)] = w_high
    xs = ym[...].astype(BF16)
    z_low = dot(xs[:, tile(0, 2)], outer_ref[tile(0, 2)]) - center * ym[:, tile(0)]
    z_high = dot(xs[:, tile(2, 2)], outer_ref[tile(2, 2)]) - center * ym[:, tile(3)]
    z_ref[:, tile(0)] = z_low
    z_ref[:, tile(1)] = z_high
    even = par_ref[0] == 0
    send(even, xs[:, tile(0)], xs[:, tile(3)], z_low, z_high, se_ref, so_ref)
    se_ref[2 * K :] = jnp.where(even, w_high, w_low)
    so_ref[2 * K :] = jnp.where(even, w_low, w_high)


def send(even, x_low, x_high, z_low, z_high, se_ref, so_ref):
    z_low, z_high = z_low.astype(BF16), z_high.astype(BF16)
    se_ref[:K] = jnp.where(even, x_high, x_low)
    se_ref[K : 2 * K] = jnp.where(even, z_high, z_low)
    so_ref[:K] = jnp.where(even, x_low, x_high)
    so_ref[K : 2 * K] = jnp.where(even, z_low, z_high)


def interior(factor, previous, xs, ys, w_in, w_out, w_edge, j_ref, i_ref, b_ref, o_ref, xn):
    for r in range(1, RT - 1):
        acc = dot(xs[:, tile(r - 1, 3)], w_in[inner(r)]) - center * ys(r)
        nxt = acc if previous is None else factor * acc - previous(r)
        j_ref[:, tile(r - 1)] = nxt
        xn[:, tile(r - 1)] = nxt.astype(BF16)
    o_ref[:, tile(0)] = factor * dot(xs[:, tile(0)], w_edge[tile(0)])
    o_ref[:, tile(1)] = factor * dot(xs[:, tile(RT - 1)], w_edge[tile(1)])
    for r in range(2, RT - 2):
        acc = dot(xn[:, tile(r - 2, 3)], w_in[inner(r)]) - center * j_ref[:, tile(r - 1)]
        i_ref[:, tile(r - 2)] = 2.0 * acc - ys(r)
    b_ref[:, tile(0)] = 2.0 * dot(xn[:, tile(0)], w_out[tile(1)]) - ys(0)
    acc = dot(xn[:, tile(0, 2)], w_in[inner(1, 1, 2)]) - center * j_ref[:, tile(0)]
    b_ref[:, tile(1)] = 2.0 * acc - ys(1)
    acc = dot(xn[:, tile(4, 2)], w_in[inner(6, 0, 2)]) - center * j_ref[:, tile(5)]
    b_ref[:, tile(2)] = 2.0 * acc - ys(6)
    b_ref[:, tile(3)] = 2.0 * dot(xn[:, tile(5)], w_out[tile(2)]) - ys(7)


def load_kernel(
    inv_ref, modes_ref, tiles_ref, w_out, w_edge,
    w_in, j_ref, i_ref, b_ref, o_ref,
    y0, xs, xn, sems, msem,
):
    mcopy = pltpu.make_async_copy(modes_ref, y0, msem)
    mcopy.start()
    copies = [
        pltpu.make_async_copy(tiles_ref.at[inv_ref[p]], w_in.at[tile(i)], sems.at[i])
        for i, p in enumerate(INNER)
    ]
    for c in copies:
        c.start()
    mcopy.wait()
    for c in copies:
        c.wait()
    xs[...] = y0[...].astype(BF16)
    interior(1.0, None, xs, lambda r: y0[:, tile(r)], w_in, w_out, w_edge, j_ref, i_ref, b_ref, o_ref, xn)


def step_kernel(last, e_ref, m_ref, z_ref, w_in, w_out, w_edge, j_ref, i_ref, b_ref, o_ref, *rest):
    xs, xn = rest[-2:]
    xs[:, tile(0, 2)] = e_ref[:, tile(0, 2)].astype(BF16)
    xs[:, tile(2, 4)] = m_ref[...].astype(BF16)
    xs[:, tile(6, 2)] = e_ref[:, tile(2, 2)].astype(BF16)

    def ys(r):
        if r < 2:
            return e_ref[:, tile(r)]
        if r >= RT - 2:
            return e_ref[:, tile(r - 4)]
        return m_ref[:, tile(r - 2)]

    interior(
        2.0, lambda r: z_ref[:, tile(r - 1)], xs, ys, w_in, w_out, w_edge, j_ref, i_ref, b_ref, o_ref, xn
    )
    if last:
        rest[0][...] = gram(i_ref[...])


def gram(y):
    return lax.dot_general(
        y, y, (((1,), (1,)), ((), ())), precision=lax.Precision.HIGHEST, preferred_element_type=F32
    )


def edges(factor, even, re_ref, ro_ref, z_ref, o_ref, b_ref, w_in, w_out, w_low, w_high):
    re, ro = re_ref[: 2 * K], ro_ref[: 2 * K]
    low, high = jnp.where(even, ro, re), jnp.where(even, re, ro)
    y_low = z_ref[:, tile(0)] + factor * dot(low[:K], w_low)
    y_high = z_ref[:, tile(1)] + factor * dot(high[:K], w_high)
    far_low = (low[K:].astype(F32) + o_ref[:, tile(0)]).astype(BF16)
    far_high = (high[K:].astype(F32) + o_ref[:, tile(1)]).astype(BF16)
    x_low, x_high = y_low.astype(BF16), y_high.astype(BF16)
    acc = dot(far_low, w_low) + dot(x_low, w_out[tile(0)]) - center * y_low
    e0 = b_ref[:, tile(0)] + 2.0 * acc
    acc = dot(far_high, w_high) + dot(x_high, w_out[tile(3)]) - center * y_high
    e3 = b_ref[:, tile(3)] + 2.0 * acc
    e1 = b_ref[:, tile(1)] + 2.0 * dot(x_low, w_in[inner(1, 0, 1)])
    e2 = b_ref[:, tile(2)] + 2.0 * dot(x_high, w_in[inner(6, 2, 1)])
    return y_low, y_high, (e0, e1, e2, e3)


def edge_kernel(
    at_first, par_ref, re_ref, ro_ref, z_ref, o_ref, b_ref, w_in, w_out, *rest
):
    even = par_ref[0] == 0
    if at_first:
        e_ref, zn_ref, se_ref, so_ref, wn_ref = rest
        we, wo = re_ref[2 * K :], ro_ref[2 * K :]
        w_low, w_high = jnp.where(even, wo, we), jnp.where(even, we, wo)
        wn_ref[tile(0)] = w_low
        wn_ref[tile(1)] = w_high
    else:
        wn_ref, e_ref, zn_ref, se_ref, so_ref = rest
    w_low, w_high = wn_ref[tile(0)], wn_ref[tile(1)]
    y_low, y_high, e = edges(
        1.0 if at_first else 2.0, even, re_ref, ro_ref, z_ref, o_ref, b_ref, w_in, w_out, w_low, w_high
    )
    for i in range(4):
        e_ref[:, tile(i)] = e[i]
    x = [v.astype(BF16) for v in e]
    z_low = 2.0 * (dot(x[0], w_out[tile(0)]) + dot(x[1], w_out[tile(1)]) - center * e[0]) - y_low
    z_high = 2.0 * (dot(x[2], w_out[tile(2)]) + dot(x[3], w_out[tile(3)]) - center * e[3]) - y_high
    zn_ref[:, tile(0)] = z_low
    zn_ref[:, tile(1)] = z_high
    send(even, x[0], x[3], z_low, z_high, se_ref, so_ref)


def final_kernel(par_ref, re_ref, ro_ref, z_ref, o_ref, b_ref, w_in, w_out, wn_ref, gi_ref, e_ref, g_ref):
    even = par_ref[0] == 0
    w_low, w_high = wn_ref[tile(0)], wn_ref[tile(1)]
    _, _, e = edges(2.0, even, re_ref, ro_ref, z_ref, o_ref, b_ref, w_in, w_out, w_low, w_high)
    for i in range(4):
        e_ref[:, tile(i)] = e[i]
    g = gi_ref[...] + gram(e_ref[...])
    g_ref[...] = jnp.concatenate([g[: K // 2], g[K // 2 :]], axis=1)


def whiten_kernel(scale, g_ref, e_ref, i_ref, out_ref):
    g = g_ref[...] * scale
    g = jnp.concatenate([g[:, :K], g[:, K:]], axis=0)
    row = lax.broadcasted_iota(jnp.int32, (K, K), 0)
    col = lax.broadcasted_iota(jnp.int32, (K, K), 1)
    eye = (row == col).astype(F32)
    whole = jnp.concatenate([g, eye], axis=1)
    blocks = [whole[8 * i : 8 * i + 8] for i in range(K // 8)]
    sub = lax.broadcasted_iota(jnp.int32, (8, 1), 0)
    for k in range(K):
        b, s = divmod(k, 8)
        pivot_row = blocks[b][s : s + 1]
        scaled = pivot_row / pivot_row[:, k : k + 1]
        for i in range(b, K // 8):
            mult = blocks[i][:, k : k + 1]
            if i == b:
                mult = jnp.where(sub > s, mult, 0.0)
            blocks[i] = blocks[i] - mult * scaled
    whole = jnp.concatenate(blocks, axis=0)
    diagonal = jnp.sum(jnp.where(row == col, whole[:, :K], 0.0), axis=1, keepdims=True)
    linv = whole[:, K:] / jnp.sqrt(diagonal)

    def apply(y):
        return jnp.dot(linv, y, precision=lax.Precision.HIGHEST, preferred_element_type=F32)

    out_ref[:, tile(0, 2)] = apply(e_ref[:, tile(0, 2)])
    out_ref[:, tile(2, 4)] = apply(i_ref[...])
    out_ref[:, tile(6, 2)] = apply(e_ref[:, tile(2, 2)])


def local(modes, tiles, tile_pair, boundary):
    count = lax.axis_size("slab") * lax.axis_size("col")
    parity = (lax.axis_index("col") & 1).astype(jnp.int32).reshape(1)
    pairs_even = [(i, i ^ 1) for i in range(count)]
    pairs_odd = [(i, (i + 1) % count if i % 2 else (i - 1) % count) for i in range(count)]

    def exchange(se, so):
        ro = lax.ppermute(so, AXES, pairs_odd)
        re = lax.ppermute(se, AXES, pairs_even)
        return re, ro

    def f32(tiles_wide):
        return pltpu.VMEM((K, tiles_wide * TB), F32)

    def weights(n):
        return pltpu.VMEM((n * TB, TB), BF16)

    def sends(rows):
        return pltpu.VMEM((rows, TB), BF16)

    w_out, w_edge, z, se, so, inv = pl.pallas_call(
        first_kernel,
        out_shape=(
            weights(4), weights(2), f32(2), sends(2 * K + TB), sends(2 * K + TB), pltpu.SMEM((TL,), jnp.int32),
        ),
        in_specs=[HBM, SM, HBM, HBM, HBM],
        out_specs=(VM, VM, VM, VM, VM, SM),
        scratch_shapes=[
            pltpu.SMEM((TL,), jnp.int32),
            pltpu.SMEM((1, 2), jnp.int32),
            pltpu.VMEM((K, 4 * TB), F32),
            pltpu.SemaphoreType.DMA((8,)),
            pltpu.SemaphoreType.DMA((2,)),
        ],
        compiler_params=params(8),
        name="first",
    )(hbm(boundary), parity, hbm(tile_pair), hbm(modes), hbm(tiles))
    re, ro = exchange(se, so)
    inner_shapes = (f32(6), f32(4), f32(4), f32(2))
    w_in, j, mid, b, o = pl.pallas_call(
        load_kernel,
        out_shape=(weights(18),) + inner_shapes,
        in_specs=[SM, HBM, HBM, VM, VM],
        out_specs=(VM,) * 5,
        scratch_shapes=[
            pltpu.VMEM((K, ROWS), F32),
            pltpu.VMEM((K, ROWS), BF16),
            pltpu.VMEM((K, 6 * TB), BF16),
            pltpu.SemaphoreType.DMA((18,)),
            pltpu.SemaphoreType.DMA,
        ],
        compiler_params=params(12),
        cost_estimate=cost(40),
        name="load",
    )(inv, hbm(modes), hbm(tiles), pin(w_out), pin(w_edge))
    wn = None
    for k in range(2, DEG, 2):
        at_first = k == 2
        outs = pl.pallas_call(
            functools.partial(edge_kernel, at_first),
            out_shape=(f32(4), f32(2), sends(2 * K), sends(2 * K)) + ((weights(2),) if at_first else ()),
            in_specs=[SM] + [VM] * (7 if at_first else 8),
            out_specs=(VM,) * (5 if at_first else 4),
            compiler_params=params(8),
            name="edge",
        )(parity, re, ro, pin(z), pin(o), pin(b), pin(w_in), pin(w_out), *(() if at_first else (pin(wn),)))
        e, z, se, so = outs[:4]
        if at_first:
            wn = outs[4]
        re, ro = exchange(se, so)
        last = k == DEG - 2
        outs = pl.pallas_call(
            functools.partial(step_kernel, last),
            out_shape=inner_shapes + ((pltpu.VMEM((K, K), F32),) if last else ()),
            in_specs=[VM] * 6,
            out_specs=(VM,) * (5 if last else 4),
            scratch_shapes=[pltpu.VMEM((K, ROWS), BF16), pltpu.VMEM((K, 6 * TB), BF16)],
            compiler_params=params(8),
            cost_estimate=cost(40),
            name="step",
        )(pin(e), pin(mid), pin(j), pin(w_in), pin(w_out), pin(w_edge))
        j, mid, b, o = outs[:4]
    e, g = pl.pallas_call(
        final_kernel,
        out_shape=(f32(4), pltpu.VMEM((K // 2, 2 * K), F32)),
        in_specs=[SM] + [VM] * 9,
        out_specs=(VM, VM),
        compiler_params=params(8),
        name="final",
    )(parity, re, ro, pin(z), pin(o), pin(b), pin(w_in), pin(w_out), pin(wn), pin(outs[4]))
    for bits in (1, 3, 4, 12, 16, 32, 96):
        g = g + lax.ppermute(g, AXES, [(i, i ^ bits) for i in range(count)])
    return pl.pallas_call(
        functools.partial(whiten_kernel, 1.0 / (ROWS * count)),
        out_shape=jax.ShapeDtypeStruct((K, ROWS), F32),
        in_specs=[VM, VM, VM],
        out_specs=VM,
        compiler_params=params(16),
        name="whiten",
    )(g, pin(e), pin(mid))


def solution(mesh):
    placed = (
        P(None, AXES),
        P(AXES, None, None),
        P(AXES),
        P(AXES, None),
    )
    return jax.shard_map(
        local, mesh=mesh, in_specs=placed, out_specs=P(None, AXES), check_vma=False
    )
```

time: 124 us -> 85.1 us (0.69)
  waiting for transfers between devices: 50.5 us -> 29.4 us
  starting transfers between devices: 40.3 us -> 30.6 us
  local copies, waits for them, and re-layouts: 5.48 us -> 0 us
  Pallas kernels: 27.5 us -> 24.7 us
    ppermute x8 -> x4, waiting for transfers between devices: 23.3 us -> 2.21 us  [exchange(): ro = lax.ppermute(so, AXES, pairs_odd)]
    ppermute x8 -> x4, starting transfers between devices: 37.8 us -> 28.6 us  [exchange(): ro = lax.ppermute(so, AXES, pairs_odd)]
    unnamed x16 -> x0, local copies, waits for them, and re-layouts: 5.48 us -> none
    pallas_call x17 -> x9, Pallas kernels: 20.4 us -> 17.6 us  [the longest x3 6.65 us: local(): pl.pallas_call(functools.partial(step_kernel, last), out_shape=inner_shap...]
    ppermute x8 -> x4, starting transfers between devices: 2.52 us -> 1.99 us  [exchange(): re = lax.ppermute(se, AXES, pairs_even)]
  transfers between devices with their start and end apart: 23 -> 15, of which waited for: 14 -> 10; matrix products, arithmetic and copies ran while one was open for 0% -> 0% of each run, Pallas kernels for 11% -> 13%
where the time goes in v1:
time: 85.1 us; the launch traced here: 84.9 us
  starting transfers between devices  30.6 us (36%)
  waiting for transfers between devices  29.4 us (35%)
  Pallas kernels  24.7 us (29%)
    ppermute x4, starting transfers between devices, exchange(): ro = lax.ppermute(so, AXES, pairs_odd)  28.6 us
    ppermute x7, waiting for transfers between devices, local(): g = g + lax.ppermute(g, AXES, [(i, i ^ bits) for i in range(count)])  27.2 us
    pallas_call x1, Pallas kernels, local(): pl.pallas_call(functools.partial(whiten_kernel, 1.0 / (ROWS * count)), ou...  7.15 us
    pallas_call x3, Pallas kernels, local(): pl.pallas_call(functools.partial(step_kernel, last), out_shape=inner_shap...  6.65 us
    pallas_call x1, Pallas kernels, local(): pl.pallas_call(load_kernel, out_shape=(weights(18),) + inner_shapes, in_s...  4.68 us
    pallas_call x1, Pallas kernels, local(): pl.pallas_call(first_kernel, out_shape=(weights(4), weights(2), f32(2), s...  2.7 us
    pallas_call x3, Pallas kernels, local(): pl.pallas_call(functools.partial(edge_kernel, at_first), out_shape=(f32(4...  2.56 us
    ppermute x4, waiting for transfers between devices, exchange(): ro = lax.ppermute(so, AXES, pairs_odd)  2.21 us
  transfers between devices with their start and end apart: 15, of which 10 were waited for; matrix products, arithmetic and copies ran while one was open for 0% of the time, Pallas kernels for 13%

profile of v1, /device:TPU:0, one launch (start us, length us, event | category | flops | bytes accessed | tf_op | source)
XLA Modules:
  0.0 84.9 jit_solution(6859497776797054003)
XLA Ops:
  0.0 2.7 %first.1 = (bf16[1536,384]{1,0:T(8,128)(2,1)S(1)}, bf16[768,384]{1,0:T(8,128)(2,1)S(1)}, f32[64,768]{1,0:T(8,128)S(1)}, bf16[512,384]{1,0:T(8,128)(2,1)S(1)}, bf...) custom-call(s32[1,2]{1,0:T(1,128)} %bound_ref.1, s32[1]{0:T(128)} %bitcast.par_ref, s32[24]{0:T(128)} %pair_ref.1, ...), custom_call_target="tpu_custom_call" | custom-call | tf_op jit(solution)/shard_map/first/pallas_call | solution.py:281
  2.7 1.7 %collective-permute-start = (bf16[512,384]{1,0:T(8,128)(2,1)S(1)}, bf16[512,384]{1,0:T(8,128)(2,1)S(1)}, u32[]{:S(2)}, u32[]{:S(2)}) collective-permute-start(bf16[512,384]{1,0:T(8,128)(2,1)S(1)} %get-tuple-element.43), channel_id=1, source_target_pairs={{0,1},{1,0},{2,3},{3,2},{4,5},{5,4},{6,7},{7,6},{8,9},{9,8},{10,11... | collective-permute-start | bytes 1179656 | tf_op jit(solution)/shard_map/ppermute | solution.py:269
  4.4 7.0 %collective-permute-start.1 = (bf16[512,384]{1,0:T(8,128)(2,1)S(1)}, bf16[512,384]{1,0:T(8,128)(2,1)S(1)}, u32[]{:S(2)}, u32[]{:S(2)}) collective-permute-start(bf16[512,384]{1,0:T(8,128)(2,1)S(1)} %get-tuple-element.44), channel_id=1, source_target_pairs={{0,127},{1,2},{2,1},{3,4},{4,3},{5,6},{6,5},{7,8},{8,7},{9,10},{10... | collective-permute-start | bytes 1179656 | tf_op jit(solution)/shard_map/ppermute | solution.py:268
  11.5 4.7 %load.1 = (bf16[6912,384]{1,0:T(8,128)(2,1)S(1)}, f32[64,2304]{1,0:T(8,128)S(1)}, f32[64,1536]{1,0:T(8,128)S(1)}, f32[64,1536]{1,0:T(8,128)S(1)}, f32[64,768]{1,0:T(8,128)S(1)}) custom-call(s32[24]{0:T(128)S(4)} %get-tuple-element.46.inv_ref, f32[64,3072]{1,0:T(8,128)} %modes_ref.3, bf16[24,384,384]{2,1,0:T(8,128)(2,1)} %tiles_ref.3, ...), custom_call_target="tpu_custom_call" | custom-call | flops 754974720 | bytes 8388608 | tf_op jit(solution)/shard_map/load/pallas_call | solution.py:300
  16.1 0.0 collective-permute-done.re_ref
  16.2 1.0 %collective-permute-done.1.ro_ref = bf16[512,384]{1,0:T(8,128)(2,1)S(1)} collective-permute-done((bf16[512,384]{1,0:T(8,128)(2,1)S(1)}, bf16[512,384]{1,0:T(8,128)(2,1)S(1)}, u32[]{:S(2)}, u32[]{:S(2)}) %collective-permute-start.1) | collective-permute-done | bytes 393248 | tf_op jit(solution)/shard_map/ppermute | solution.py:268
  17.2 0.9 %edge.3 = (f32[64,1536]{1,0:T(8,128)S(1)}, f32[64,768]{1,0:T(8,128)S(1)}, bf16[128,384]{1,0:T(8,128)(2,1)S(1)}, bf16[128,384]{1,0:T(8,128)(2,1)S(1)}, bf16[768,384]{1,0:T(8,128)(2,1)S(1)}) custom-call(s32[1]{0:T(128)} %bitcast.par_ref, bf16[512,384]{1,0:T(8,128)(2,1)S(1)} %collective-permute-done.re_ref, bf16[512,384]{1,0:T(8,128)(2,1)S(1)} %collective-permute-done.1.ro_ref, ...), custom_call_target="tpu_custom_call" | custom-call | tf_op jit(solution)/shard_map/edge/pallas_call | solution.py:319
  18.1 0.1 collective-permute-start.2
  18.2 7.1 %collective-permute-start.3 = (bf16[128,384]{1,0:T(8,128)(2,1)S(1)}, bf16[128,384]{1,0:T(8,128)(2,1)S(1)}, u32[]{:S(2)}, u32[]{:S(2)}) collective-permute-start(bf16[128,384]{1,0:T(8,128)(2,1)S(1)} %get-tuple-element.53), channel_id=1, source_target_pairs={{0,127},{1,2},{2,1},{3,4},{4,3},{5,6},{6,5},{7,8},{8,7},{9,10},{10... | collective-permute-start | bytes 294920 | tf_op jit(solution)/shard_map/ppermute | solution.py:268
  25.3 1.8 %step.3 = (f32[64,2304]{1,0:T(8,128)S(1)}, f32[64,1536]{1,0:T(8,128)S(1)}, f32[64,1536]{1,0:T(8,128)S(1)}, f32[64,768]{1,0:T(8,128)S(1)}) custom-call(f32[64,1536]{1,0:T(8,128)S(1)} %get-tuple-element.55.e_ref, f32[64,1536]{1,0:T(8,128)S(1)} %get-tuple-element.56.m_ref, f32[64,2304]{1,0:T(8,128)S(1)} %get-tuple-element.57.z_ref, ...), custom_call_target="tpu_custom_call" | custom-call | flops 754974720 | bytes 8388608 | tf_op jit(solution)/shard_map/step/pallas_call | solution.py:332
  27.1 0.0 collective-permute-done.2.re_ref
  27.1 0.7 collective-permute-done.3.ro_ref
  27.7 0.8 edge.4
  28.6 0.1 collective-permute-start.4
  28.7 7.2 %collective-permute-start.5 = (bf16[128,384]{1,0:T(8,128)(2,1)S(1)}, bf16[128,384]{1,0:T(8,128)(2,1)S(1)}, u32[]{:S(2)}, u32[]{:S(2)}) collective-permute-start(bf16[128,384]{1,0:T(8,128)(2,1)S(1)} %get-tuple-element.62), channel_id=1, source_target_pairs={{0,127},{1,2},{2,1},{3,4},{4,3},{5,6},{6,5},{7,8},{8,7},{9,10},{10... | collective-permute-start | bytes 294920 | tf_op jit(solution)/shard_map/ppermute | solution.py:268
  35.8 1.9 %step.4 = (f32[64,2304]{1,0:T(8,128)S(1)}, f32[64,1536]{1,0:T(8,128)S(1)}, f32[64,1536]{1,0:T(8,128)S(1)}, f32[64,768]{1,0:T(8,128)S(1)}) custom-call(f32[64,1536]{1,0:T(8,128)S(1)} %get-tuple-element.64.e_ref, f32[64,1536]{1,0:T(8,128)S(1)} %get-tuple-element.65.m_ref, f32[64,2304]{1,0:T(8,128)S(1)} %get-tuple-element.66.z_ref, ...), custom_call_target="tpu_custom_call" | custom-call | flops 754974720 | bytes 8388608 | tf_op jit(solution)/shard_map/step/pallas_call | solution.py:332
  37.7 0.0 collective-permute-done.4.re_ref
  37.7 0.5 collective-permute-done.5.ro_ref
  38.2 0.8 edge.5
  39.1 0.1 collective-permute-start.6
  39.2 7.3 %collective-permute-start.7 = (bf16[128,384]{1,0:T(8,128)(2,1)S(1)}, bf16[128,384]{1,0:T(8,128)(2,1)S(1)}, u32[]{:S(2)}, u32[]{:S(2)}) collective-permute-start(bf16[128,384]{1,0:T(8,128)(2,1)S(1)} %get-tuple-element.70), channel_id=1, source_target_pairs={{0,127},{1,2},{2,1},{3,4},{4,3},{5,6},{6,5},{7,8},{8,7},{9,10},{10... | collective-permute-start | bytes 294920 | tf_op jit(solution)/shard_map/ppermute | solution.py:268
  46.5 3.0 %step.5 = (f32[64,2304]{1,0:T(8,128)}, f32[64,1536]{1,0:T(8,128)S(1)}, f32[64,1536]{1,0:T(8,128)S(1)}, f32[64,768]{1,0:T(8,128)S(1)}, f32[64,64]{1,0:T(8,128)S(1)}) custom-call(f32[64,1536]{1,0:T(8,128)S(1)} %get-tuple-element.72.e_ref, f32[64,1536]{1,0:T(8,128)S(1)} %get-tuple-element.73.m_ref, f32[64,2304]{1,0:T(8,128)S(1)} %get-tuple-element.74.z_ref, ...), custom_call_target="tpu_custom_call" | custom-call | flops 754974720 | bytes 8388608 | tf_op jit(solution)/shard_map/step/pallas_call | solution.py:332
  49.5 1.0 %final.1 = (f32[64,1536]{1,0:T(8,128)S(1)}, f32[32,128]{1,0:T(8,128)S(1)}) custom-call(s32[1]{0:T(128)} %bitcast.par_ref, bf16[128,384]{1,0:T(8,128)(2,1)S(1)} %collective-permute-done.6.re_ref, bf16[128,384]{1,0:T(8,128)(2,1)S(1)} %collective-permute-done.7.ro_ref, f32[64,768]{1,0:T(8,128)S(1)} %get-tuple-element.71.z_ref, ...), custom_call_target="tpu_custom_call" | custom-call | tf_op jit(solution)/shard_map/final/pallas_call | solution.py:343
  50.5 0.0 collective-permute-start.8
  50.5 3.7 %collective-permute-done.8 = f32[32,128]{1,0:T(8,128)S(1)} collective-permute-done((f32[32,128]{1,0:T(8,128)S(1)}, f32[32,128]{1,0:T(8,128)S(1)}, u32[]{:S(2)}, u32[]{:S(2)}) %collective-permute-start.8) | collective-permute-done | bytes 16416 | tf_op jit(solution)/shard_map/ppermute | solution.py:352
  54.2 4.9 %collective-permute-done.9 = f32[32,128]{1,0:T(8,128)S(1)} collective-permute-done((f32[32,128]{1,0:T(8,128)S(1)}, f32[32,128]{1,0:T(8,128)S(1)}, u32[]{:S(2)}, u32[]{:S(2)}) %collective-permute-start.9) | collective-permute-done | bytes 16416 | tf_op jit(solution)/shard_map/ppermute | solution.py:352
  59.2 3.7 %collective-permute-done.10 = f32[32,128]{1,0:T(8,128)S(1)} collective-permute-done((f32[32,128]{1,0:T(8,128)S(1)}, f32[32,128]{1,0:T(8,128)S(1)}, u32[]{:S(2)}, u32[]{:S(2)}) %collective-permute-start.10) | collective-permute-done | bytes 16416 | tf_op jit(solution)/shard_map/ppermute | solution.py:352
  62.9 4.9 %collective-permute-done.11 = f32[32,128]{1,0:T(8,128)S(1)} collective-permute-done((f32[32,128]{1,0:T(8,128)S(1)}, f32[32,128]{1,0:T(8,128)S(1)}, u32[]{:S(2)}, u32[]{:S(2)}) %collective-permute-start.11) | collective-permute-done | bytes 16416 | tf_op jit(solution)/shard_map/ppermute | solution.py:352
  67.9 1.2 %collective-permute-done.12 = f32[32,128]{1,0:T(8,128)S(1)} collective-permute-done((f32[32,128]{1,0:T(8,128)S(1)}, f32[32,128]{1,0:T(8,128)S(1)}, u32[]{:S(2)}, u32[]{:S(2)}) %collective-permute-start.12) | collective-permute-done | bytes 16416 | tf_op jit(solution)/shard_map/ppermute | solution.py:352
  69.1 3.7 %collective-permute-done.13 = f32[32,128]{1,0:T(8,128)S(1)} collective-permute-done((f32[32,128]{1,0:T(8,128)S(1)}, f32[32,128]{1,0:T(8,128)S(1)}, u32[]{:S(2)}, u32[]{:S(2)}) %collective-permute-start.13) | collective-permute-done | bytes 16416 | tf_op jit(solution)/shard_map/ppermute | solution.py:352
  72.8 4.9 %collective-permute-done.14 = f32[32,128]{1,0:T(8,128)S(1)} collective-permute-done((f32[32,128]{1,0:T(8,128)S(1)}, f32[32,128]{1,0:T(8,128)S(1)}, u32[]{:S(2)}, u32[]{:S(2)}) %collective-permute-start.14) | collective-permute-done | bytes 16416 | tf_op jit(solution)/shard_map/ppermute | solution.py:352
  77.8 7.2 %whiten.1 = f32[64,3072]{1,0:T(8,128)} custom-call(f32[32,128]{1,0:T(8,128)S(1)} %add.27.g_ref, f32[64,1536]{1,0:T(8,128)S(1)} %get-tuple-element.79.e_ref, f32[64,1536]{1,0:T(8,128)S(1)} %get-tuple-element.80.i_ref), custom_call_target="tpu_custom_call" | custom-call | tf_op jit(solution)/shard_map/whiten/pallas_call | solution.py:353
  (15 shorter events, 0.1 us)
Async XLA Ops:
  2.7 13.4 %collective-permute-start = (bf16[512,384]{1,0:T(8,128)(2,1)S(1)}, bf16[512,384]{1,0:T(8,128)(2,1)S(1)}, u32[]{:S(2)}, u32[]{:S(2)}) collective-permute-start(bf16[512,384]{1,0:T(8,128)(2,1)S(1)} %get-tuple-element.43), channel_id=1, source_target_pairs={{0,1},{1,0},{2,3},{3,2},{4,5},{5,4},{6,7},{7,6},{8,9},{9,8},{10,11... | collective-permute-start | bytes 1179656 | tf_op jit(solution)/shard_map/ppermute | solution.py:269
  4.4 12.7 %collective-permute-start.1 = (bf16[512,384]{1,0:T(8,128)(2,1)S(1)}, bf16[512,384]{1,0:T(8,128)(2,1)S(1)}, u32[]{:S(2)}, u32[]{:S(2)}) collective-permute-start(bf16[512,384]{1,0:T(8,128)(2,1)S(1)} %get-tuple-element.44), channel_id=1, source_target_pairs={{0,127},{1,2},{2,1},{3,4},{4,3},{5,6},{6,5},{7,8},{8,7},{9,10},{10... | collective-permute-start | bytes 1179656 | tf_op jit(solution)/shard_map/ppermute | solution.py:268
  18.1 9.0 %collective-permute-start.2 = (bf16[128,384]{1,0:T(8,128)(2,1)S(1)}, bf16[128,384]{1,0:T(8,128)(2,1)S(1)}, u32[]{:S(2)}, u32[]{:S(2)}) collective-permute-start(bf16[128,384]{1,0:T(8,128)(2,1)S(1)} %get-tuple-element.52), channel_id=1, source_target_pairs={{0,1},{1,0},{2,3},{3,2},{4,5},{5,4},{6,7},{7,6},{8,9},{9,8},{10,11... | collective-permute-start | bytes 294920 | tf_op jit(solution)/shard_map/ppermute | solution.py:269
  18.2 9.6 %collective-permute-start.3 = (bf16[128,384]{1,0:T(8,128)(2,1)S(1)}, bf16[128,384]{1,0:T(8,128)(2,1)S(1)}, u32[]{:S(2)}, u32[]{:S(2)}) collective-permute-start(bf16[128,384]{1,0:T(8,128)(2,1)S(1)} %get-tuple-element.53), channel_id=1, source_target_pairs={{0,127},{1,2},{2,1},{3,4},{4,3},{5,6},{6,5},{7,8},{8,7},{9,10},{10... | collective-permute-start | bytes 294920 | tf_op jit(solution)/shard_map/ppermute | solution.py:268
  28.6 9.1 %collective-permute-start.4 = (bf16[128,384]{1,0:T(8,128)(2,1)S(1)}, bf16[128,384]{1,0:T(8,128)(2,1)S(1)}, u32[]{:S(2)}, u32[]{:S(2)}) collective-permute-start(bf16[128,384]{1,0:T(8,128)(2,1)S(1)} %get-tuple-element.61), channel_id=1, source_target_pairs={{0,1},{1,0},{2,3},{3,2},{4,5},{5,4},{6,7},{7,6},{8,9},{9,8},{10,11... | collective-permute-start | bytes 294920 | tf_op jit(solution)/shard_map/ppermute | solution.py:269
  28.7 9.6 %collective-permute-start.5 = (bf16[128,384]{1,0:T(8,128)(2,1)S(1)}, bf16[128,384]{1,0:T(8,128)(2,1)S(1)}, u32[]{:S(2)}, u32[]{:S(2)}) collective-permute-start(bf16[128,384]{1,0:T(8,128)(2,1)S(1)} %get-tuple-element.62), channel_id=1, source_target_pairs={{0,127},{1,2},{2,1},{3,4},{4,3},{5,6},{6,5},{7,8},{8,7},{9,10},{10... | collective-permute-start | bytes 294920 | tf_op jit(solution)/shard_map/ppermute | solution.py:268
  39.1 10.4 %collective-permute-start.6 = (bf16[128,384]{1,0:T(8,128)(2,1)S(1)}, bf16[128,384]{1,0:T(8,128)(2,1)S(1)}, u32[]{:S(2)}, u32[]{:S(2)}) collective-permute-start(bf16[128,384]{1,0:T(8,128)(2,1)S(1)} %get-tuple-element.69), channel_id=1, source_target_pairs={{0,1},{1,0},{2,3},{3,2},{4,5},{5,4},{6,7},{7,6},{8,9},{9,8},{10,11... | collective-permute-start | bytes 294920 | tf_op jit(solution)/shard_map/ppermute | solution.py:269
  39.2 10.3 %collective-permute-start.7 = (bf16[128,384]{1,0:T(8,128)(2,1)S(1)}, bf16[128,384]{1,0:T(8,128)(2,1)S(1)}, u32[]{:S(2)}, u32[]{:S(2)}) collective-permute-start(bf16[128,384]{1,0:T(8,128)(2,1)S(1)} %get-tuple-element.70), channel_id=1, source_target_pairs={{0,127},{1,2},{2,1},{3,4},{4,3},{5,6},{6,5},{7,8},{8,7},{9,10},{10... | collective-permute-start | bytes 294920 | tf_op jit(solution)/shard_map/ppermute | solution.py:268
  50.5 3.8 %collective-permute-start.8 = (f32[32,128]{1,0:T(8,128)S(1)}, f32[32,128]{1,0:T(8,128)S(1)}, u32[]{:S(2)}, u32[]{:S(2)}) collective-permute-start(f32[32,128]{1,0:T(8,128)S(1)} %get-tuple-element.78), channel_id=1, source_target_pairs={{0,1},{1,0},{2,3},{3,2},{4,5},{5,4},{6,7},{7,6},{8,9},{9,8},{10,11... | collective-permute-start | bytes 49160 | tf_op jit(solution)/shard_map/ppermute | solution.py:352
  54.2 4.9 %collective-permute-start.9 = (f32[32,128]{1,0:T(8,128)S(1)}, f32[32,128]{1,0:T(8,128)S(1)}, u32[]{:S(2)}, u32[]{:S(2)}) collective-permute-start(f32[32,128]{1,0:T(8,128)S(1)} %add.21), channel_id=1, source_target_pairs={{0,3},{1,2},{2,1},{3,0},{4,7},{5,6},{6,5},{7,4},{8,11},{9,10},{10,... | collective-permute-start | bytes 49160 | tf_op jit(solution)/shard_map/ppermute | solution.py:352
  59.2 3.7 %collective-permute-start.10 = (f32[32,128]{1,0:T(8,128)S(1)}, f32[32,128]{1,0:T(8,128)S(1)}, u32[]{:S(2)}, u32[]{:S(2)}) collective-permute-start(f32[32,128]{1,0:T(8,128)S(1)} %add.22), channel_id=1, source_target_pairs={{0,4},{1,5},{2,6},{3,7},{4,0},{5,1},{6,2},{7,3},{8,12},{9,13},{10,... | collective-permute-start | bytes 49160 | tf_op jit(solution)/shard_map/ppermute | solution.py:352
  62.9 4.9 %collective-permute-start.11 = (f32[32,128]{1,0:T(8,128)S(1)}, f32[32,128]{1,0:T(8,128)S(1)}, u32[]{:S(2)}, u32[]{:S(2)}) collective-permute-start(f32[32,128]{1,0:T(8,128)S(1)} %add.23), channel_id=1, source_target_pairs={{0,12},{1,13},{2,14},{3,15},{4,8},{5,9},{6,10},{7,11},{8,4},{9,5},... | collective-permute-start | bytes 49160 | tf_op jit(solution)/shard_map/ppermute | solution.py:352
  67.9 1.2 %collective-permute-start.12 = (f32[32,128]{1,0:T(8,128)S(1)}, f32[32,128]{1,0:T(8,128)S(1)}, u32[]{:S(2)}, u32[]{:S(2)}) collective-permute-start(f32[32,128]{1,0:T(8,128)S(1)} %add.24), channel_id=1, source_target_pairs={{0,16},{1,17},{2,18},{3,19},{4,20},{5,21},{6,22},{7,23},{8,24},{9,... | collective-permute-start | bytes 49160 | tf_op jit(solution)/shard_map/ppermute | solution.py:352
  69.1 3.7 %collective-permute-start.13 = (f32[32,128]{1,0:T(8,128)S(1)}, f32[32,128]{1,0:T(8,128)S(1)}, u32[]{:S(2)}, u32[]{:S(2)}) collective-permute-start(f32[32,128]{1,0:T(8,128)S(1)} %add.25), channel_id=1, source_target_pairs={{0,32},{1,33},{2,34},{3,35},{4,36},{5,37},{6,38},{7,39},{8,40},{9,... | collective-permute-start | bytes 49160 | tf_op jit(solution)/shard_map/ppermute | solution.py:352
  72.8 4.9 %collective-permute-start.14 = (f32[32,128]{1,0:T(8,128)S(1)}, f32[32,128]{1,0:T(8,128)S(1)}, u32[]{:S(2)}, u32[]{:S(2)}) collective-permute-start(f32[32,128]{1,0:T(8,128)S(1)} %add.26), channel_id=1, source_target_pairs={{0,96},{1,97},{2,98},{3,99},{4,100},{5,101},{6,102},{7,103},{8,104... | collective-permute-start | bytes 49160 | tf_op jit(solution)/shard_map/ppermute | solution.py:352

commit v2 on v1

--- a/solution.py
+++ b/solution.py
@@ -170,9 +170,14 @@
 
 
 def gram(y):
-    return lax.dot_general(
-        y, y, (((1,), (1,)), ((), ())), precision=lax.Precision.HIGHEST, preferred_element_type=F32
-    )
+    parts = jnp.concatenate(split(y), axis=0)
+    p = lax.dot_general(parts, parts, (((1,), (1,)), ((), ())), preferred_element_type=F32)
+
+    def block(a, b):
+        return p[a * K : (a + 1) * K, b * K : (b + 1) * K]
+
+    small = block(1, 1) + (block(0, 2) + block(2, 0))
+    return block(0, 0) + ((block(0, 1) + block(1, 0)) + small)
 
 
 def edges(factor, even, re_ref, ro_ref, z_ref, o_ref, b_ref, w_in, w_out, w_low, w_high):
@@ -228,34 +233,73 @@
     g_ref[...] = jnp.concatenate([g[: K // 2], g[K // 2 :]], axis=1)
 
 
-def whiten_kernel(scale, g_ref, e_ref, i_ref, out_ref):
-    g = g_ref[...] * scale
-    g = jnp.concatenate([g[:, :K], g[:, K:]], axis=0)
+def split(x):
+    high = x.astype(BF16)
+    rest = x - high.astype(F32)
+    mid = rest.astype(BF16)
+    return high, mid, (rest - mid.astype(F32)).astype(BF16)
+
+
+def inverse_factor(g):
     row = lax.broadcasted_iota(jnp.int32, (K, K), 0)
     col = lax.broadcasted_iota(jnp.int32, (K, K), 1)
-    eye = (row == col).astype(F32)
-    whole = jnp.concatenate([g, eye], axis=1)
-    blocks = [whole[8 * i : 8 * i + 8] for i in range(K // 8)]
-    sub = lax.broadcasted_iota(jnp.int32, (8, 1), 0)
-    for k in range(K):
-        b, s = divmod(k, 8)
-        pivot_row = blocks[b][s : s + 1]
-        scaled = pivot_row / pivot_row[:, k : k + 1]
-        for i in range(b, K // 8):
-            mult = blocks[i][:, k : k + 1]
-            if i == b:
-                mult = jnp.where(sub > s, mult, 0.0)
-            blocks[i] = blocks[i] - mult * scaled
-    whole = jnp.concatenate(blocks, axis=0)
-    diagonal = jnp.sum(jnp.where(row == col, whole[:, :K], 0.0), axis=1, keepdims=True)
-    linv = whole[:, K:] / jnp.sqrt(diagonal)
-
-    def apply(y):
-        return jnp.dot(linv, y, precision=lax.Precision.HIGHEST, preferred_element_type=F32)
-
-    out_ref[:, tile(0, 2)] = apply(e_ref[:, tile(0, 2)])
-    out_ref[:, tile(2, 4)] = apply(i_ref[...])
-    out_ref[:, tile(6, 2)] = apply(e_ref[:, tile(2, 2)])
+    whole = jnp.concatenate([g, (row == col).astype(F32)], axis=1)
+    count = K // 8
+    shape = (8, 2 * K)
+    blocks = [whole[8 * i : 8 * i + 8] for i in range(count)]
+    sub = lax.broadcasted_iota(jnp.int32, shape, 0)
+    scaled = []
+    for b in range(count):
+        rows = [jnp.broadcast_to(blocks[b][a : a + 1], shape) for a in range(8)]
+        entry = {
+            (a, c): jnp.broadcast_to(rows[a][:, 8 * b + c : 8 * b + c + 1], shape)
+            for a in range(8)
+            for c in range(8)
+        }
+        columns = {
+            i: [jnp.broadcast_to(blocks[i][:, 8 * b + c : 8 * b + c + 1], shape) for c in range(8)]
+            for i in range(b + 1, count)
+        }
+        pivots, inverses = rows[0], None
+        for a in range(8):
+            inverse = 1.0 / entry[a, a]
+            inverses = inverse if a == 0 else jnp.where(sub == a, inverse, inverses)
+            if a > 0:
+                pivots = jnp.where(sub == a, rows[a], pivots)
+            for r in range(a + 1, 8):
+                m = entry[r, a] * inverse
+                rows[r] = rows[r] - m * rows[a]
+                for c in range(a + 1, 8):
+                    entry[r, c] = entry[r, c] - m * entry[a, c]
+            for i in columns:
+                m = columns[i][a] * inverse
+                for c in range(a + 1, 8):
+                    columns[i][c] = columns[i][c] - m * entry[a, c]
+                columns[i][a] = m
+        for i in columns:
+            update = columns[i][0] * rows[0]
+            for a in range(1, 8):
+                update = update + columns[i][a] * rows[a]
+            blocks[i] = blocks[i] - update
+        scaled.append(pivots * jnp.sqrt(inverses))
+    return jnp.concatenate(scaled, axis=0)[:, K:]
+
+
+def whiten_kernel(scale, g_ref, e_ref, i_ref, out_ref, buf, sems):
+    g = g_ref[...] * scale
+    high, mid, low = split(inverse_factor(jnp.concatenate([g[:, :K], g[:, K:]], axis=0)))
+    left = jnp.concatenate([high, mid, high, low, mid, high], axis=1)
+    copies = []
+    for n in range(RT // 2):
+        y = (e_ref[:, tile(0, 2)], i_ref[:, tile(0, 2)], i_ref[:, tile(2, 2)], e_ref[:, tile(2, 2)])[n]
+        yh, ym, yl = split(y)
+        right = jnp.concatenate([yh, yh, ym, yh, ym, yl], axis=0)
+        buf[:, tile(2 * n, 2)] = dot(left, right)
+        copy = pltpu.make_async_copy(buf.at[:, tile(2 * n, 2)], out_ref.at[:, tile(2 * n, 2)], sems.at[n])
+        copy.start()
+        copies.append(copy)
+    for copy in copies:
+        copy.wait()
 
 
 def local(modes, tiles, tile_pair, boundary):
@@ -348,13 +392,16 @@
         compiler_params=params(8),
         name="final",
     )(parity, re, ro, pin(z), pin(o), pin(b), pin(w_in), pin(w_out), pin(wn), pin(outs[4]))
-    for bits in (1, 3, 4, 12, 16, 32, 96):
-        g = g + lax.ppermute(g, AXES, [(i, i ^ bits) for i in range(count)])
+    for group in ((16,), (1, 3, 2), (4, 12, 8), (32, 96, 64)):
+        got = [lax.ppermute(g, AXES, [(i, i ^ bits) for i in range(count)]) for bits in group]
+        for other in got:
+            g = g + other
     return pl.pallas_call(
         functools.partial(whiten_kernel, 1.0 / (ROWS * count)),
         out_shape=jax.ShapeDtypeStruct((K, ROWS), F32),
         in_specs=[VM, VM, VM],
-        out_specs=VM,
+        out_specs=HBM,
+        scratch_shapes=[pltpu.VMEM((K, ROWS), F32), pltpu.SemaphoreType.DMA((RT // 2,))],
         compiler_params=params(16),
         name="whiten",
     )(g, pin(e), pin(mid))

time: 85.1 us -> 74.7 us (0.88)
  waiting for transfers between devices: 29.4 us -> 9.99 us
  starting transfers between devices: 30.6 us -> 43.8 us
  Pallas kernels: 24.7 us -> 20.4 us
    ppermute x7 -> x10, waiting for transfers between devices: 27.2 us -> 7.7 us  [local(): lax.ppermute(g, AXES, [(i, i ^ bits) for i in range(count)])]
    ppermute x7 -> x10, starting transfers between devices: 0.05 us -> 13.2 us  [local(): lax.ppermute(g, AXES, [(i, i ^ bits) for i in range(count)])]
    pallas_call x1, Pallas kernels: 7.15 us -> 3.4 us  [local(): pl.pallas_call(functools.partial(whiten_kernel, 1.0 / (ROWS * count)), ou...]
  transfers between devices with their start and end apart: 15 -> 18, of which waited for: 10 -> 9; matrix products, arithmetic and copies ran while one was open for 0% -> 0% of each run, Pallas kernels for 13% -> 14%
where the time goes in v2:
time: 74.7 us; the launch traced here: 74.5 us
  starting transfers between devices  43.8 us (59%)
  Pallas kernels  20.4 us (27%)
  waiting for transfers between devices  9.99 us (13%)
    ppermute x4, starting transfers between devices, exchange(): ro = lax.ppermute(so, AXES, pairs_odd)  28.6 us
    ppermute x10, starting transfers between devices, local(): lax.ppermute(g, AXES, [(i, i ^ bits) for i in range(count)])  13.2 us
    ppermute x10, waiting for transfers between devices, local(): lax.ppermute(g, AXES, [(i, i ^ bits) for i in range(count)])  7.7 us
    pallas_call x3, Pallas kernels, local(): pl.pallas_call(functools.partial(step_kernel, last), out_shape=inner_shap...  5.99 us
    pallas_call x1, Pallas kernels, local(): pl.pallas_call(load_kernel, out_shape=(weights(18),) + inner_shapes, in_s...  4.69 us
    pallas_call x1, Pallas kernels, local(): pl.pallas_call(functools.partial(whiten_kernel, 1.0 / (ROWS * count)), ou...  3.4 us
    pallas_call x1, Pallas kernels, local(): pl.pallas_call(first_kernel, out_shape=(weights(4), weights(2), f32(2), s...  2.7 us
    pallas_call x3, Pallas kernels, local(): pl.pallas_call(functools.partial(edge_kernel, at_first), out_shape=(f32(4...  2.56 us
  transfers between devices with their start and end apart: 18, of which 9 were waited for; matrix products, arithmetic and copies ran while one was open for 0% of the time, Pallas kernels for 14%

profile of v2, /device:TPU:0, one launch (start us, length us, event | category | flops | bytes accessed | tf_op | source)
XLA Modules:
  0.0 74.5 jit_solution(17463446815563791745)
XLA Ops:
  0.0 2.7 %first.1 = (bf16[1536,384]{1,0:T(8,128)(2,1)S(1)}, bf16[768,384]{1,0:T(8,128)(2,1)S(1)}, f32[64,768]{1,0:T(8,128)S(1)}, bf16[512,384]{1,0:T(8,128)(2,1)S(1)}, bf...) custom-call(s32[1,2]{1,0:T(1,128)} %bound_ref.1, s32[1]{0:T(128)} %bitcast.par_ref, s32[24]{0:T(128)} %pair_ref.1, ...), custom_call_target="tpu_custom_call" | custom-call | tf_op jit(solution)/shard_map/first/pallas_call | solution.py:325
  2.7 1.7 %collective-permute-start = (bf16[512,384]{1,0:T(8,128)(2,1)S(1)}, bf16[512,384]{1,0:T(8,128)(2,1)S(1)}, u32[]{:S(2)}, u32[]{:S(2)}) collective-permute-start(bf16[512,384]{1,0:T(8,128)(2,1)S(1)} %get-tuple-element.43), channel_id=1, source_target_pairs={{0,1},{1,0},{2,3},{3,2},{4,5},{5,4},{6,7},{7,6},{8,9},{9,8},{10,11... | collective-permute-start | bytes 1179656 | tf_op jit(solution)/shard_map/ppermute | solution.py:313
  4.4 7.0 %collective-permute-start.1 = (bf16[512,384]{1,0:T(8,128)(2,1)S(1)}, bf16[512,384]{1,0:T(8,128)(2,1)S(1)}, u32[]{:S(2)}, u32[]{:S(2)}) collective-permute-start(bf16[512,384]{1,0:T(8,128)(2,1)S(1)} %get-tuple-element.44), channel_id=1, source_target_pairs={{0,127},{1,2},{2,1},{3,4},{4,3},{5,6},{6,5},{7,8},{8,7},{9,10},{10... | collective-permute-start | bytes 1179656 | tf_op jit(solution)/shard_map/ppermute | solution.py:312
  11.5 4.7 %load.1 = (bf16[6912,384]{1,0:T(8,128)(2,1)S(1)}, f32[64,2304]{1,0:T(8,128)S(1)}, f32[64,1536]{1,0:T(8,128)S(1)}, f32[64,1536]{1,0:T(8,128)S(1)}, f32[64,768]{1,0:T(8,128)S(1)}) custom-call(s32[24]{0:T(128)S(4)} %get-tuple-element.46.inv_ref, f32[64,3072]{1,0:T(8,128)} %modes_ref.3, bf16[24,384,384]{2,1,0:T(8,128)(2,1)} %tiles_ref.3, ...), custom_call_target="tpu_custom_call" | custom-call | flops 754974720 | bytes 8388608 | tf_op jit(solution)/shard_map/load/pallas_call | solution.py:344
  16.2 1.0 %collective-permute-done.1.ro_ref = bf16[512,384]{1,0:T(8,128)(2,1)S(1)} collective-permute-done((bf16[512,384]{1,0:T(8,128)(2,1)S(1)}, bf16[512,384]{1,0:T(8,128)(2,1)S(1)}, u32[]{:S(2)}, u32[]{:S(2)}) %collective-permute-start.1) | collective-permute-done | bytes 393248 | tf_op jit(solution)/shard_map/ppermute | solution.py:312
  17.2 0.9 %edge.3 = (f32[64,1536]{1,0:T(8,128)S(1)}, f32[64,768]{1,0:T(8,128)S(1)}, bf16[128,384]{1,0:T(8,128)(2,1)S(1)}, bf16[128,384]{1,0:T(8,128)(2,1)S(1)}, bf16[768,384]{1,0:T(8,128)(2,1)S(1)}) custom-call(s32[1]{0:T(128)} %bitcast.par_ref, bf16[512,384]{1,0:T(8,128)(2,1)S(1)} %collective-permute-done.re_ref, bf16[512,384]{1,0:T(8,128)(2,1)S(1)} %collective-permute-done.1.ro_ref, ...), custom_call_target="tpu_custom_call" | custom-call | tf_op jit(solution)/shard_map/edge/pallas_call | solution.py:363
  18.1 0.1 collective-permute-start.2
  18.2 7.1 %collective-permute-start.3 = (bf16[128,384]{1,0:T(8,128)(2,1)S(1)}, bf16[128,384]{1,0:T(8,128)(2,1)S(1)}, u32[]{:S(2)}, u32[]{:S(2)}) collective-permute-start(bf16[128,384]{1,0:T(8,128)(2,1)S(1)} %get-tuple-element.53), channel_id=1, source_target_pairs={{0,127},{1,2},{2,1},{3,4},{4,3},{5,6},{6,5},{7,8},{8,7},{9,10},{10... | collective-permute-start | bytes 294920 | tf_op jit(solution)/shard_map/ppermute | solution.py:312
  25.3 1.8 %step.3 = (f32[64,2304]{1,0:T(8,128)S(1)}, f32[64,1536]{1,0:T(8,128)S(1)}, f32[64,1536]{1,0:T(8,128)S(1)}, f32[64,768]{1,0:T(8,128)S(1)}) custom-call(f32[64,1536]{1,0:T(8,128)S(1)} %get-tuple-element.55.e_ref, f32[64,1536]{1,0:T(8,128)S(1)} %get-tuple-element.56.m_ref, f32[64,2304]{1,0:T(8,128)S(1)} %get-tuple-element.57.z_ref, ...), custom_call_target="tpu_custom_call" | custom-call | flops 754974720 | bytes 8388608 | tf_op jit(solution)/shard_map/step/pallas_call | solution.py:376
  27.1 0.7 collective-permute-done.3.ro_ref
  27.7 0.8 %edge.4 = (f32[64,1536]{1,0:T(8,128)S(1)}, f32[64,768]{1,0:T(8,128)S(1)}, bf16[128,384]{1,0:T(8,128)(2,1)S(1)}, bf16[128,384]{1,0:T(8,128)(2,1)S(1)}) custom-call(s32[1]{0:T(128)} %bitcast.par_ref, bf16[128,384]{1,0:T(8,128)(2,1)S(1)} %collective-permute-done.2.re_ref, bf16[128,384]{1,0:T(8,128)(2,1)S(1)} %collective-permute-done.3.ro_ref, ...), custom_call_target="tpu_custom_call" | custom-call | tf_op jit(solution)/shard_map/edge/pallas_call | solution.py:363
  28.6 0.1 collective-permute-start.4
  28.7 7.2 %collective-permute-start.5 = (bf16[128,384]{1,0:T(8,128)(2,1)S(1)}, bf16[128,384]{1,0:T(8,128)(2,1)S(1)}, u32[]{:S(2)}, u32[]{:S(2)}) collective-permute-start(bf16[128,384]{1,0:T(8,128)(2,1)S(1)} %get-tuple-element.62), channel_id=1, source_target_pairs={{0,127},{1,2},{2,1},{3,4},{4,3},{5,6},{6,5},{7,8},{8,7},{9,10},{10... | collective-permute-start | bytes 294920 | tf_op jit(solution)/shard_map/ppermute | solution.py:312
  35.8 1.9 %step.4 = (f32[64,2304]{1,0:T(8,128)S(1)}, f32[64,1536]{1,0:T(8,128)S(1)}, f32[64,1536]{1,0:T(8,128)S(1)}, f32[64,768]{1,0:T(8,128)S(1)}) custom-call(f32[64,1536]{1,0:T(8,128)S(1)} %get-tuple-element.64.e_ref, f32[64,1536]{1,0:T(8,128)S(1)} %get-tuple-element.65.m_ref, f32[64,2304]{1,0:T(8,128)S(1)} %get-tuple-element.66.z_ref, ...), custom_call_target="tpu_custom_call" | custom-call | flops 754974720 | bytes 8388608 | tf_op jit(solution)/shard_map/step/pallas_call | solution.py:376
  37.7 0.5 collective-permute-done.5.ro_ref
  38.2 0.8 %edge.5 = (f32[64,1536]{1,0:T(8,128)S(1)}, f32[64,768]{1,0:T(8,128)S(1)}, bf16[128,384]{1,0:T(8,128)(2,1)S(1)}, bf16[128,384]{1,0:T(8,128)(2,1)S(1)}) custom-call(s32[1]{0:T(128)} %bitcast.par_ref, bf16[128,384]{1,0:T(8,128)(2,1)S(1)} %collective-permute-done.4.re_ref, bf16[128,384]{1,0:T(8,128)(2,1)S(1)} %collective-permute-done.5.ro_ref, ...), custom_call_target="tpu_custom_call" | custom-call | tf_op jit(solution)/shard_map/edge/pallas_call | solution.py:363
  39.2 7.3 %collective-permute-start.7 = (bf16[128,384]{1,0:T(8,128)(2,1)S(1)}, bf16[128,384]{1,0:T(8,128)(2,1)S(1)}, u32[]{:S(2)}, u32[]{:S(2)}) collective-permute-start(bf16[128,384]{1,0:T(8,128)(2,1)S(1)} %get-tuple-element.70), channel_id=1, source_target_pairs={{0,127},{1,2},{2,1},{3,4},{4,3},{5,6},{6,5},{7,8},{8,7},{9,10},{10... | collective-permute-start | bytes 294920 | tf_op jit(solution)/shard_map/ppermute | solution.py:312
  46.5 2.3 %step.5 = (f32[64,2304]{1,0:T(8,128)}, f32[64,1536]{1,0:T(8,128)S(1)}, f32[64,1536]{1,0:T(8,128)S(1)}, f32[64,768]{1,0:T(8,128)S(1)}, f32[64,64]{1,0:T(8,128)S(1)}) custom-call(f32[64,1536]{1,0:T(8,128)S(1)} %get-tuple-element.72.e_ref, f32[64,1536]{1,0:T(8,128)S(1)} %get-tuple-element.73.m_ref, f32[64,2304]{1,0:T(8,128)S(1)} %get-tuple-element.74.z_ref, ...), custom_call_target="tpu_custom_call" | custom-call | flops 754974720 | bytes 8388608 | tf_op jit(solution)/shard_map/step/pallas_call | solution.py:376
  48.9 1.1 %final.1 = (f32[64,1536]{1,0:T(8,128)S(1)}, f32[32,128]{1,0:T(8,128)S(1)}) custom-call(s32[1]{0:T(128)} %bitcast.par_ref, bf16[128,384]{1,0:T(8,128)(2,1)S(1)} %collective-permute-done.6.re_ref, bf16[128,384]{1,0:T(8,128)(2,1)S(1)} %collective-permute-done.7.ro_ref, f32[64,768]{1,0:T(8,128)S(1)} %get-tuple-element.71.z_ref, ...), custom_call_target="tpu_custom_call" | custom-call | tf_op jit(solution)/shard_map/final/pallas_call | solution.py:387
  50.0 1.2 %collective-permute-done.8 = f32[32,128]{1,0:T(8,128)S(1)} collective-permute-done((f32[32,128]{1,0:T(8,128)S(1)}, f32[32,128]{1,0:T(8,128)S(1)}, u32[]{:S(2)}, u32[]{:S(2)}) %collective-permute-start.8) | collective-permute-done | bytes 16416 | tf_op jit(solution)/shard_map/ppermute | solution.py:396
  51.3 3.4 %collective-permute-start.9 = (f32[32,128]{1,0:T(8,128)S(1)}, f32[32,128]{1,0:T(8,128)S(1)}, u32[]{:S(2)}, u32[]{:S(2)}) collective-permute-start(f32[32,128]{1,0:T(8,128)S(1)} %add.30), channel_id=1, source_target_pairs={{0,1},{1,0},{2,3},{3,2},{4,5},{5,4},{6,7},{7,6},{8,9},{9,8},{10,11... | collective-permute-start | bytes 49160 | tf_op jit(solution)/shard_map/ppermute | solution.py:396
  54.7 1.8 %collective-permute-done.11 = f32[32,128]{1,0:T(8,128)S(1)} collective-permute-done((f32[32,128]{1,0:T(8,128)S(1)}, f32[32,128]{1,0:T(8,128)S(1)}, u32[]{:S(2)}, u32[]{:S(2)}) %collective-permute-start.11) | collective-permute-done | bytes 16416 | tf_op jit(solution)/shard_map/ppermute | solution.py:396
  56.5 0.1 collective-permute-start.14
  56.6 0.7 collective-permute-start.13
  57.3 2.8 %collective-permute-start.12 = (f32[32,128]{1,0:T(8,128)S(1)}, f32[32,128]{1,0:T(8,128)S(1)}, u32[]{:S(2)}, u32[]{:S(2)}) collective-permute-start(f32[32,128]{1,0:T(8,128)S(1)} %add_add_fusion.2), channel_id=1, source_target_pairs={{0,4},{1,5},{2,6},{3,7},{4,0},{5,1},{6,2},{7,3},{8,12},{9,13},{10,... | collective-permute-start | bytes 49160 | tf_op jit(solution)/shard_map/ppermute | solution.py:396
  60.1 1.8 %collective-permute-done.14 = f32[32,128]{1,0:T(8,128)S(1)} collective-permute-done((f32[32,128]{1,0:T(8,128)S(1)}, f32[32,128]{1,0:T(8,128)S(1)}, u32[]{:S(2)}, u32[]{:S(2)}) %collective-permute-start.14) | collective-permute-done | bytes 16416 | tf_op jit(solution)/shard_map/ppermute | solution.py:396
  61.9 2.2 %collective-permute-start.17 = (f32[32,128]{1,0:T(8,128)S(1)}, f32[32,128]{1,0:T(8,128)S(1)}, u32[]{:S(2)}, u32[]{:S(2)}) collective-permute-start(f32[32,128]{1,0:T(8,128)S(1)} %add_add_fusion.1), channel_id=1, source_target_pairs={{0,64},{1,65},{2,66},{3,67},{4,68},{5,69},{6,70},{7,71},{8,72},{9,... | collective-permute-start | bytes 49160 | tf_op jit(solution)/shard_map/ppermute | solution.py:396
  64.0 3.2 %collective-permute-start.16 = (f32[32,128]{1,0:T(8,128)S(1)}, f32[32,128]{1,0:T(8,128)S(1)}, u32[]{:S(2)}, u32[]{:S(2)}) collective-permute-start(f32[32,128]{1,0:T(8,128)S(1)} %add_add_fusion.1), channel_id=1, source_target_pairs={{0,96},{1,97},{2,98},{3,99},{4,100},{5,101},{6,102},{7,103},{8,104... | collective-permute-start | bytes 49160 | tf_op jit(solution)/shard_map/ppermute | solution.py:396
  67.2 0.8 %collective-permute-start.15 = (f32[32,128]{1,0:T(8,128)S(1)}, f32[32,128]{1,0:T(8,128)S(1)}, u32[]{:S(2)}, u32[]{:S(2)}) collective-permute-start(f32[32,128]{1,0:T(8,128)S(1)} %add_add_fusion.1), channel_id=1, source_target_pairs={{0,32},{1,33},{2,34},{3,35},{4,36},{5,37},{6,38},{7,39},{8,40},{9,... | collective-permute-start | bytes 49160 | tf_op jit(solution)/shard_map/ppermute | solution.py:396
  68.0 1.0 %collective-permute-done.16 = f32[32,128]{1,0:T(8,128)S(1)} collective-permute-done((f32[32,128]{1,0:T(8,128)S(1)}, f32[32,128]{1,0:T(8,128)S(1)}, u32[]{:S(2)}, u32[]{:S(2)}) %collective-permute-start.16) | collective-permute-done | bytes 16416 | tf_op jit(solution)/shard_map/ppermute | solution.py:396
  69.0 2.0 %collective-permute-done.15 = f32[32,128]{1,0:T(8,128)S(1)} collective-permute-done((f32[32,128]{1,0:T(8,128)S(1)}, f32[32,128]{1,0:T(8,128)S(1)}, u32[]{:S(2)}, u32[]{:S(2)}) %collective-permute-start.15) | collective-permute-done | bytes 16416 | tf_op jit(solution)/shard_map/ppermute | solution.py:396
  71.0 3.4 %whiten.1 = f32[64,3072]{1,0:T(8,128)} custom-call(f32[32,128]{1,0:T(8,128)S(1)} %add_add_fusion.g_ref, f32[64,1536]{1,0:T(8,128)S(1)} %get-tuple-element.79.e_ref, f32[64,1536]{1,0:T(8,128)S(1)} %get-tuple-element.80.i_ref), custom_call_target="tpu_custom_call" | custom-call | tf_op jit(solution)/shard_map/whiten/pallas_call | solution.py:399
  (18 shorter events, 0.3 us)
Async XLA Ops:
  2.7 13.4 %collective-permute-start = (bf16[512,384]{1,0:T(8,128)(2,1)S(1)}, bf16[512,384]{1,0:T(8,128)(2,1)S(1)}, u32[]{:S(2)}, u32[]{:S(2)}) collective-permute-start(bf16[512,384]{1,0:T(8,128)(2,1)S(1)} %get-tuple-element.43), channel_id=1, source_target_pairs={{0,1},{1,0},{2,3},{3,2},{4,5},{5,4},{6,7},{7,6},{8,9},{9,8},{10,11... | collective-permute-start | bytes 1179656 | tf_op jit(solution)/shard_map/ppermute | solution.py:313
  4.4 12.7 %collective-permute-start.1 = (bf16[512,384]{1,0:T(8,128)(2,1)S(1)}, bf16[512,384]{1,0:T(8,128)(2,1)S(1)}, u32[]{:S(2)}, u32[]{:S(2)}) collective-permute-start(bf16[512,384]{1,0:T(8,128)(2,1)S(1)} %get-tuple-element.44), channel_id=1, source_target_pairs={{0,127},{1,2},{2,1},{3,4},{4,3},{5,6},{6,5},{7,8},{8,7},{9,10},{10... | collective-permute-start | bytes 1179656 | tf_op jit(solution)/shard_map/ppermute | solution.py:312
  18.1 9.0 %collective-permute-start.2 = (bf16[128,384]{1,0:T(8,128)(2,1)S(1)}, bf16[128,384]{1,0:T(8,128)(2,1)S(1)}, u32[]{:S(2)}, u32[]{:S(2)}) collective-permute-start(bf16[128,384]{1,0:T(8,128)(2,1)S(1)} %get-tuple-element.52), channel_id=1, source_target_pairs={{0,1},{1,0},{2,3},{3,2},{4,5},{5,4},{6,7},{7,6},{8,9},{9,8},{10,11... | collective-permute-start | bytes 294920 | tf_op jit(solution)/shard_map/ppermute | solution.py:313
  18.2 9.6 %collective-permute-start.3 = (bf16[128,384]{1,0:T(8,128)(2,1)S(1)}, bf16[128,384]{1,0:T(8,128)(2,1)S(1)}, u32[]{:S(2)}, u32[]{:S(2)}) collective-permute-start(bf16[128,384]{1,0:T(8,128)(2,1)S(1)} %get-tuple-element.53), channel_id=1, source_target_pairs={{0,127},{1,2},{2,1},{3,4},{4,3},{5,6},{6,5},{7,8},{8,7},{9,10},{10... | collective-permute-start | bytes 294920 | tf_op jit(solution)/shard_map/ppermute | solution.py:312
  28.6 9.1 %collective-permute-start.4 = (bf16[128,384]{1,0:T(8,128)(2,1)S(1)}, bf16[128,384]{1,0:T(8,128)(2,1)S(1)}, u32[]{:S(2)}, u32[]{:S(2)}) collective-permute-start(bf16[128,384]{1,0:T(8,128)(2,1)S(1)} %get-tuple-element.61), channel_id=1, source_target_pairs={{0,1},{1,0},{2,3},{3,2},{4,5},{5,4},{6,7},{7,6},{8,9},{9,8},{10,11... | collective-permute-start | bytes 294920 | tf_op jit(solution)/shard_map/ppermute | solution.py:313
  28.7 9.6 %collective-permute-start.5 = (bf16[128,384]{1,0:T(8,128)(2,1)S(1)}, bf16[128,384]{1,0:T(8,128)(2,1)S(1)}, u32[]{:S(2)}, u32[]{:S(2)}) collective-permute-start(bf16[128,384]{1,0:T(8,128)(2,1)S(1)} %get-tuple-element.62), channel_id=1, source_target_pairs={{0,127},{1,2},{2,1},{3,4},{4,3},{5,6},{6,5},{7,8},{8,7},{9,10},{10... | collective-permute-start | bytes 294920 | tf_op jit(solution)/shard_map/ppermute | solution.py:312
  39.1 9.7 %collective-permute-start.6 = (bf16[128,384]{1,0:T(8,128)(2,1)S(1)}, bf16[128,384]{1,0:T(8,128)(2,1)S(1)}, u32[]{:S(2)}, u32[]{:S(2)}) collective-permute-start(bf16[128,384]{1,0:T(8,128)(2,1)S(1)} %get-tuple-element.69), channel_id=1, source_target_pairs={{0,1},{1,0},{2,3},{3,2},{4,5},{5,4},{6,7},{7,6},{8,9},{9,8},{10,11... | collective-permute-start | bytes 294920 | tf_op jit(solution)/shard_map/ppermute | solution.py:313
  39.2 9.7 %collective-permute-start.7 = (bf16[128,384]{1,0:T(8,128)(2,1)S(1)}, bf16[128,384]{1,0:T(8,128)(2,1)S(1)}, u32[]{:S(2)}, u32[]{:S(2)}) collective-permute-start(bf16[128,384]{1,0:T(8,128)(2,1)S(1)} %get-tuple-element.70), channel_id=1, source_target_pairs={{0,127},{1,2},{2,1},{3,4},{4,3},{5,6},{6,5},{7,8},{8,7},{9,10},{10... | collective-permute-start | bytes 294920 | tf_op jit(solution)/shard_map/ppermute | solution.py:312
  50.0 1.2 %collective-permute-start.8 = (f32[32,128]{1,0:T(8,128)S(1)}, f32[32,128]{1,0:T(8,128)S(1)}, u32[]{:S(2)}, u32[]{:S(2)}) collective-permute-start(f32[32,128]{1,0:T(8,128)S(1)} %get-tuple-element.78), channel_id=1, source_target_pairs={{0,16},{1,17},{2,18},{3,19},{4,20},{5,21},{6,22},{7,23},{8,24},{9,... | collective-permute-start | bytes 49160 | tf_op jit(solution)/shard_map/ppermute | solution.py:396
  51.2 5.3 %collective-permute-start.11 = (f32[32,128]{1,0:T(8,128)S(1)}, f32[32,128]{1,0:T(8,128)S(1)}, u32[]{:S(2)}, u32[]{:S(2)}) collective-permute-start(f32[32,128]{1,0:T(8,128)S(1)} %add.30), channel_id=1, source_target_pairs={{0,2},{1,3},{2,0},{3,1},{4,6},{5,7},{6,4},{7,5},{8,10},{9,11},{10,... | collective-permute-start | bytes 49160 | tf_op jit(solution)/shard_map/ppermute | solution.py:396
  51.2 5.3 %collective-permute-start.10 = (f32[32,128]{1,0:T(8,128)S(1)}, f32[32,128]{1,0:T(8,128)S(1)}, u32[]{:S(2)}, u32[]{:S(2)}) collective-permute-start(f32[32,128]{1,0:T(8,128)S(1)} %add.30), channel_id=1, source_target_pairs={{0,3},{1,2},{2,1},{3,0},{4,7},{5,6},{6,5},{7,4},{8,11},{9,10},{10,... | collective-permute-start | bytes 49160 | tf_op jit(solution)/shard_map/ppermute | solution.py:396
  51.3 5.2 %collective-permute-start.9 = (f32[32,128]{1,0:T(8,128)S(1)}, f32[32,128]{1,0:T(8,128)S(1)}, u32[]{:S(2)}, u32[]{:S(2)}) collective-permute-start(f32[32,128]{1,0:T(8,128)S(1)} %add.30), channel_id=1, source_target_pairs={{0,1},{1,0},{2,3},{3,2},{4,5},{5,4},{6,7},{7,6},{8,9},{9,8},{10,11... | collective-permute-start | bytes 49160 | tf_op jit(solution)/shard_map/ppermute | solution.py:396
  56.5 5.3 %collective-permute-start.14 = (f32[32,128]{1,0:T(8,128)S(1)}, f32[32,128]{1,0:T(8,128)S(1)}, u32[]{:S(2)}, u32[]{:S(2)}) collective-permute-start(f32[32,128]{1,0:T(8,128)S(1)} %add_add_fusion.2), channel_id=1, source_target_pairs={{0,8},{1,9},{2,10},{3,11},{4,12},{5,13},{6,14},{7,15},{8,0},{9,1},... | collective-permute-start | bytes 49160 | tf_op jit(solution)/shard_map/ppermute | solution.py:396
  56.6 5.2 %collective-permute-start.13 = (f32[32,128]{1,0:T(8,128)S(1)}, f32[32,128]{1,0:T(8,128)S(1)}, u32[]{:S(2)}, u32[]{:S(2)}) collective-permute-start(f32[32,128]{1,0:T(8,128)S(1)} %add_add_fusion.2), channel_id=1, source_target_pairs={{0,12},{1,13},{2,14},{3,15},{4,8},{5,9},{6,10},{7,11},{8,4},{9,5},... | collective-permute-start | bytes 49160 | tf_op jit(solution)/shard_map/ppermute | solution.py:396
  57.3 4.6 %collective-permute-start.12 = (f32[32,128]{1,0:T(8,128)S(1)}, f32[32,128]{1,0:T(8,128)S(1)}, u32[]{:S(2)}, u32[]{:S(2)}) collective-permute-start(f32[32,128]{1,0:T(8,128)S(1)} %add_add_fusion.2), channel_id=1, source_target_pairs={{0,4},{1,5},{2,6},{3,7},{4,0},{5,1},{6,2},{7,3},{8,12},{9,13},{10,... | collective-permute-start | bytes 49160 | tf_op jit(solution)/shard_map/ppermute | solution.py:396
  61.9 6.1 %collective-permute-start.17 = (f32[32,128]{1,0:T(8,128)S(1)}, f32[32,128]{1,0:T(8,128)S(1)}, u32[]{:S(2)}, u32[]{:S(2)}) collective-permute-start(f32[32,128]{1,0:T(8,128)S(1)} %add_add_fusion.1), channel_id=1, source_target_pairs={{0,64},{1,65},{2,66},{3,67},{4,68},{5,69},{6,70},{7,71},{8,72},{9,... | collective-permute-start | bytes 49160 | tf_op jit(solution)/shard_map/ppermute | solution.py:396
  64.0 4.9 %collective-permute-start.16 = (f32[32,128]{1,0:T(8,128)S(1)}, f32[32,128]{1,0:T(8,128)S(1)}, u32[]{:S(2)}, u32[]{:S(2)}) collective-permute-start(f32[32,128]{1,0:T(8,128)S(1)} %add_add_fusion.1), channel_id=1, source_target_pairs={{0,96},{1,97},{2,98},{3,99},{4,100},{5,101},{6,102},{7,103},{8,104... | collective-permute-start | bytes 49160 | tf_op jit(solution)/shard_map/ppermute | solution.py:396
  67.2 3.7 %collective-permute-start.15 = (f32[32,128]{1,0:T(8,128)S(1)}, f32[32,128]{1,0:T(8,128)S(1)}, u32[]{:S(2)}, u32[]{:S(2)}) collective-permute-start(f32[32,128]{1,0:T(8,128)S(1)} %add_add_fusion.1), channel_id=1, source_target_pairs={{0,32},{1,33},{2,34},{3,35},{4,36},{5,37},{6,38},{7,39},{8,40},{9,... | collective-permute-start | bytes 49160 | tf_op jit(solution)/shard_map/ppermute | solution.py:396

commit v3 on v2

v3 whole, which is shorter than its diff:
```python
import functools

import jax
import jax.numpy as jnp
from jax import lax
from jax.experimental import pallas as pl
from jax.experimental.pallas import tpu as pltpu
from jax.sharding import PartitionSpec as P

DEG = 8
center = 0.25
AXES = ("slab", "col")
K = 64
TB = 384
RT = 8
TL = 24
ROWS = RT * TB
F32 = jnp.float32
BF16 = jnp.bfloat16

VM = pl.BlockSpec(memory_space=pltpu.VMEM)
SM = pl.BlockSpec(memory_space=pltpu.SMEM)
HBM = pl.BlockSpec(memory_space=pltpu.HBM)


def pin(x):
    return pltpu.with_memory_space_constraint(x, pltpu.VMEM)


def hbm(x):
    return pltpu.with_memory_space_constraint(x, pltpu.HBM)


def params(mib):
    return pltpu.CompilerParams(vmem_limit_bytes=mib << 20)


def cost(tile_products):
    return pl.CostEstimate(flops=2 * K * TB * TB * tile_products, bytes_accessed=8 << 20, transcendentals=0)


def dot(a, b):
    return jnp.dot(a, b, preferred_element_type=F32)


def tile(i, n=1):
    return slice(i * TB, (i + n) * TB)


OUTER = [1, 3, 20, 22]
INNER = [3 * c + (r - c) + 1 for r in range(1, RT - 1) for c in (r - 1, r, r + 1)]


def inner(r, first=0, count=3):
    return tile(3 * (r - 1) + first, count)


def first_kernel(
    bound_ref, par_ref, pair_ref, modes_ref, tiles_ref,
    outer_ref, we_ref, z_ref, se_ref, so_ref, inv_ref,
    pair, bound, ym, sems, ssem,
):
    to_smem = pltpu.make_async_copy(pair_ref, pair, ssem.at[0])
    to_smem.start()
    bound_copy = pltpu.make_async_copy(bound_ref, bound, ssem.at[1])
    bound_copy.start()
    modes = [
        pltpu.make_async_copy(modes_ref.at[:, tile(0, 2)], ym.at[:, tile(0, 2)], sems.at[6]),
        pltpu.make_async_copy(modes_ref.at[:, tile(6, 2)], ym.at[:, tile(2, 2)], sems.at[7]),
    ]
    for c in modes:
        c.start()
    to_smem.wait()
    for t in range(TL):
        inv_ref[pair[t]] = t
    copies = [
        pltpu.make_async_copy(tiles_ref.at[inv_ref[p]], outer_ref.at[tile(i)], sems.at[i])
        for i, p in enumerate(OUTER)
    ] + [
        pltpu.make_async_copy(tiles_ref.at[inv_ref[p]], we_ref.at[tile(i)], sems.at[4 + i])
        for i, p in enumerate((0, TL - 1))
    ]
    for c in copies:
        c.start()
    bound_copy.wait()
    for c in modes + copies:
        c.wait()
    row = lax.broadcasted_iota(jnp.int32, (TB, TB), 0)
    zero = jnp.zeros((TB, TB), BF16)
    w_low = jnp.where(row < bound[0, 0], we_ref[tile(0)], zero)
    w_high = jnp.where(row >= TB - bound[0, 1], we_ref[tile(1)], zero)
    we_ref[tile(0)] = w_low
    we_ref[tile(1)] = w_high
    xs = ym[...].astype(BF16)
    z_low = dot(xs[:, tile(0, 2)], outer_ref[tile(0, 2)]) - center * ym[:, tile(0)]
    z_high = dot(xs[:, tile(2, 2)], outer_ref[tile(2, 2)]) - center * ym[:, tile(3)]
    z_ref[:, tile(0)] = z_low
    z_ref[:, tile(1)] = z_high
    even = par_ref[0] == 0
    send(even, (xs[:, tile(0)], z_low), (xs[:, tile(3)], z_high), se_ref, so_ref)
    se_ref[2 * K :] = jnp.where(even, w_high, w_low)
    so_ref[2 * K :] = jnp.where(even, w_low, w_high)


def send(even, low, high, se_ref, so_ref):
    for i, (a, b) in enumerate(zip(low, high)):
        a, b = a.astype(BF16), b.astype(BF16)
        se_ref[i * K : (i + 1) * K] = jnp.where(even, b, a)
        so_ref[i * K : (i + 1) * K] = jnp.where(even, a, b)


def one_on(factor, now, before, xs, w_in, xn, keep):
    for r in range(1, RT - 1):
        acc = dot(xs[:, tile(r - 1, 3)], w_in[inner(r)]) - center * now(r)
        value = acc if before is None else factor * acc - before(r)
        keep(r, value)
        xn[:, tile(r - 1)] = value.astype(BF16)


def two_on(now, one, xn, w_in, w_out, b_ref, keep):
    for r in range(2, RT - 2):
        acc = dot(xn[:, tile(r - 2, 3)], w_in[inner(r)]) - center * one(r)
        keep(r, 2.0 * acc - now(r))
    b_ref[:, tile(0)] = 2.0 * dot(xn[:, tile(0)], w_out[tile(1)]) - now(0)
    acc = dot(xn[:, tile(0, 2)], w_in[inner(1, 1, 2)]) - center * one(1)
    b_ref[:, tile(1)] = 2.0 * acc - now(1)
    acc = dot(xn[:, tile(4, 2)], w_in[inner(6, 0, 2)]) - center * one(6)
    b_ref[:, tile(2)] = 2.0 * acc - now(6)
    b_ref[:, tile(3)] = 2.0 * dot(xn[:, tile(5)], w_out[tile(2)]) - now(7)


def overflow(factor, xs, w_edge, o_ref):
    o_ref[:, tile(0)] = factor * dot(xs[:, tile(0)], w_edge[tile(0)])
    o_ref[:, tile(1)] = factor * dot(xs[:, tile(RT - 1)], w_edge[tile(1)])


def load_kernel(
    par_ref, inv_ref, modes_ref, tiles_ref, w_out, w_edge,
    w_in, j_ref, m_ref, b_ref, o_ref, fe_ref, fo_ref,
    y0, xs, xn, sems, msem,
):
    mcopy = pltpu.make_async_copy(modes_ref, y0, msem)
    mcopy.start()
    copies = [
        pltpu.make_async_copy(tiles_ref.at[inv_ref[p]], w_in.at[tile(i)], sems.at[i])
        for i, p in enumerate(INNER)
    ]
    for c in copies:
        c.start()
    mcopy.wait()
    for c in copies:
        c.wait()
    xs[...] = y0[...].astype(BF16)
    even = par_ref[0] == 0
    w_low, w_high = w_out[tile(0)], w_out[tile(3)]
    fe_ref[...] = jnp.where(even, w_high, w_low)
    fo_ref[...] = jnp.where(even, w_low, w_high)

    def keep_one(r, value):
        j_ref[:, tile(r - 1)] = value

    def keep_two(r, value):
        m_ref[:, tile(r - 2)] = value

    def now(r):
        return y0[:, tile(r)]

    one_on(1.0, now, None, xs, w_in, xn, keep_one)
    overflow(1.0, xs, w_edge, o_ref)
    two_on(now, lambda r: j_ref[:, tile(r - 1)], xn, w_in, w_out, b_ref, keep_two)


def step_kernel(later, last, *refs):
    if later:
        e_ref, n_ref, p_ref, q_ref = refs[:4]
    else:
        e_ref, n_ref, p_ref = refs[:3]
    w_in, w_out, w_edge, m_ref, b_ref, o_ref, t_ref, c_ref, *rest = refs[4 if later else 3 :]
    xs, xn, xm, one_ref = rest[-4:]
    edge = 3 if later else 2

    def now(r):
        if r < edge:
            return e_ref[:, tile(r)]
        if r >= RT - edge:
            return e_ref[:, tile(r - RT + 2 * edge)]
        return n_ref[:, tile(r - edge)]

    def before(r):
        if not later:
            return p_ref[:, tile(r - 1)]
        if r in (1, 6):
            return p_ref[:, tile(0 if r == 1 else 1)]
        return q_ref[:, tile(r - 2)]

    def one(r):
        return one_ref[:, tile(r - 1)]

    def keep_one(r, value):
        one_ref[:, tile(r - 1)] = value

    def keep_two(r, value):
        m_ref[:, tile(r - 2)] = value
        xm[:, tile(r - 2)] = value.astype(BF16)

    for r in range(RT):
        xs[:, tile(r)] = now(r).astype(BF16)
    one_on(2.0, now, before, xs, w_in, xn, keep_one)
    overflow(2.0, xs, w_edge, o_ref)
    two_on(now, one, xn, w_in, w_out, b_ref, keep_two)
    for r in (3, 4):
        acc = dot(xm[:, tile(r - 3, 3)], w_in[inner(r)]) - center * m_ref[:, tile(r - 2)]
        t_ref[:, tile(r - 3)] = 2.0 * acc - one(r)
    c_ref[:, tile(0)] = 2.0 * dot(xm[:, tile(0)], w_in[inner(1, 2, 1)]) - one(1)
    acc = dot(xm[:, tile(0, 2)], w_in[inner(2, 1, 2)]) - center * m_ref[:, tile(0)]
    c_ref[:, tile(1)] = 2.0 * acc - one(2)
    acc = dot(xm[:, tile(2, 2)], w_in[inner(5, 0, 2)]) - center * m_ref[:, tile(3)]
    c_ref[:, tile(2)] = 2.0 * acc - one(5)
    c_ref[:, tile(3)] = 2.0 * dot(xm[:, tile(3)], w_in[inner(6, 0, 1)]) - one(6)
    if last:
        rest[0][...] = gram(t_ref[...])


def gram(y):
    parts = jnp.concatenate(split(y), axis=0)
    p = lax.dot_general(parts, parts, (((1,), (1,)), ((), ())), preferred_element_type=F32)

    def block(a, b):
        return p[a * K : (a + 1) * K, b * K : (b + 1) * K]

    small = block(1, 1) + (block(0, 2) + block(2, 0))
    return block(0, 0) + ((block(0, 1) + block(1, 0)) + small)


def bf(x):
    return x.astype(BF16)


def side_weights(side, w_in, w_out):
    if side == 0:
        rows = {(0, 0): w_out[tile(0)], (1, 0): w_out[tile(1)]}
        near, far = (0, 1, 2), (0, 1, 2)
    else:
        rows = {(0, 0): w_out[tile(3)], (1, 0): w_out[tile(2)]}
        near, far = (2, 1, 0), (2, 1, 0)
    first, second = (1, 2) if side == 0 else (6, 5)
    for source in range(3):
        rows[source, 1] = w_in[inner(first, near[source], 1)]
    rows[1, 2] = w_in[inner(second, far[0], 1)]
    return rows


def chosen(even, re, ro):
    return jnp.where(even, ro, re), jnp.where(even, re, ro)


def prepare(ws, ys, x2s, before):
    both = range(2)
    x = [[bf(y) for y in ys[i][:2]] for i in both]
    next1 = [dot(x[i][1], ws[i][1, 1]) + dot(x2s[i], ws[i][2, 1]) for i in both]
    next1 = [next1[i] + dot(x[i][0], ws[i][0, 1]) for i in both]
    next1 = [bf(2.0 * (next1[i] - center * ys[i][1]) - before[i][1]) for i in both]
    z = [dot(x[i][0], ws[i][0, 0]) + dot(x[i][1], ws[i][1, 0]) for i in both]
    s = [2.0 * dot(next1[i], ws[i][1, 0]) - ys[i][0] for i in both]
    z = [2.0 * (z[i] - center * ys[i][0]) - before[i][0] for i in both]
    return z, [(x[i][0], z[i], s[i]) for i in both]


def edge2_kernel(
    par_ref, re_ref, ro_ref, z_ref, o_ref, b_ref, w_in, w_out, m_ref, j_ref,
    e_ref, zn_ref, se_ref, so_ref, wn_ref,
):
    even = par_ref[0] == 0
    got = chosen(even, re_ref[: 2 * K], ro_ref[: 2 * K])
    for side, w in enumerate(chosen(even, re_ref[2 * K :], ro_ref[2 * K :])):
        wn_ref[tile(side)] = w
    both = range(2)
    w = [side_weights(i, w_in, w_out) for i in both]
    wn = [wn_ref[tile(i)] for i in both]
    outer, second = (0, 3), (1, 2)
    far = [bf(got[i][K:].astype(F32) + o_ref[:, tile(i)]) for i in both]
    share = [dot(jnp.concatenate([got[i][:K], far[i]], axis=0), wn[i]) for i in both]
    y0_1 = [z_ref[:, tile(i)] + share[i][:K] for i in both]
    x0_1 = [bf(y) for y in y0_1]
    y1 = [b_ref[:, tile(second[i])] + 2.0 * dot(x0_1[i], w[i][0, 1]) for i in both]
    y0 = [dot(x0_1[i], w[i][0, 0]) + share[i][K:] for i in both]
    y0 = [b_ref[:, tile(outer[i])] + 2.0 * (y0[i] - center * y0_1[i]) for i in both]
    for i in both:
        e_ref[:, tile(outer[i])] = y0[i]
        e_ref[:, tile(second[i])] = y1[i]
    x2 = [bf(m_ref[:, tile(3 * i)]) for i in both]
    before = [(y0_1[i], j_ref[:, tile(5 * i)]) for i in both]
    z, parts = prepare(w, [(y0[i], y1[i]) for i in both], x2, before)
    for i in both:
        zn_ref[:, tile(i)] = z[i]
    send(even, parts[0], parts[1], se_ref, so_ref)


def three_on(got, w, wn, wf, we, z_ref, o_ref, b_ref, c_ref):
    both = range(2)
    outer, second = (0, 3), (1, 2)
    far1 = [got[i][K : 2 * K].astype(F32) + o_ref[:, tile(i)] for i in both]
    xf = [bf(f) for f in far1]
    share = [dot(jnp.concatenate([got[i][:K], xf[i]], axis=0), wn[i]) for i in both]
    y0_1 = [z_ref[:, tile(i)] + 2.0 * share[i][:K] for i in both]
    x0 = [bf(y) for y in y0_1]
    far2 = [dot(xf[i], wf[i]) for i in both]
    y1_2 = [b_ref[:, tile(second[i])] + 2.0 * dot(x0[i], w[i][0, 1]) for i in both]
    y0_2 = [dot(x0[i], w[i][0, 0]) + share[i][K:] for i in both]
    far2 = [far2[i] + dot(x0[i], we[i]) for i in both]
    y0_2 = [b_ref[:, tile(outer[i])] + 2.0 * (y0_2[i] - center * y0_1[i]) for i in both]
    far2 = [got[i][2 * K :].astype(F32) + 2.0 * (far2[i] - center * far1[i]) for i in both]
    x1, x0, xf = [bf(y) for y in y1_2], [bf(y) for y in y0_2], [bf(f) for f in far2]
    y2_3 = [c_ref[:, tile(second[i])] + 2.0 * dot(x1[i], w[i][1, 2]) for i in both]
    y1_3 = [dot(x1[i], w[i][1, 1]) + dot(x0[i], w[i][0, 1]) for i in both]
    y0_3 = [dot(x1[i], w[i][1, 0]) + dot(x0[i], w[i][0, 0]) + dot(xf[i], wn[i]) for i in both]
    y1_3 = [c_ref[:, tile(outer[i])] + 2.0 * (y1_3[i] - center * y1_2[i]) for i in both]
    y0_3 = [2.0 * (y0_3[i] - center * y0_2[i]) - y0_1[i] for i in both]
    return list(zip(y0_2, y1_2)), list(zip(y0_3, y1_3, y2_3))


def edge3_kernel(
    last, par_ref, re_ref, ro_ref, z_ref, o_ref, b_ref, c_ref, w_in, w_out, wn_ref, w_edge, fe_ref, fo_ref, *rest
):
    even = par_ref[0] == 0
    got = chosen(even, re_ref[...], ro_ref[...])
    far = chosen(even, fe_ref[...], fo_ref[...])
    e_ref = rest[1] if last else rest[0]
    both = range(2)
    w = [side_weights(i, w_in, w_out) for i in both]
    wn, we = [wn_ref[tile(i)] for i in both], [w_edge[tile(i)] for i in both]
    two, three = three_on(got, w, wn, far, we, z_ref, o_ref, b_ref, c_ref)
    for i in both:
        for n in range(3):
            e_ref[:, tile(5 - n if i else n)] = three[i][n]
    if not last:
        _, p_ref, zn_ref, _, _ = rest
        z, parts = prepare(w, three, [bf(y[2]) for y in three], two)
        for i in both:
            p_ref[:, tile(i)] = two[i][1]
            zn_ref[:, tile(i)] = z[i]
    if last:
        g = rest[0][...] + gram(e_ref[...])
        rest[2][...] = jnp.concatenate([g[: K // 2], g[K // 2 :]], axis=1)
    else:
        send(even, parts[0], parts[1], rest[3], rest[4])


def split(x):
    high = x.astype(BF16)
    rest = x - high.astype(F32)
    mid = rest.astype(BF16)
    return high, mid, (rest - mid.astype(F32)).astype(BF16)


def inverse_factor(g):
    row = lax.broadcasted_iota(jnp.int32, (K, K), 0)
    col = lax.broadcasted_iota(jnp.int32, (K, K), 1)
    whole = jnp.concatenate([g, (row == col).astype(F32)], axis=1)
    count = K // 8
    shape = (8, 2 * K)
    blocks = [whole[8 * i : 8 * i + 8] for i in range(count)]
    sub = lax.broadcasted_iota(jnp.int32, shape, 0)
    scaled = []
    for b in range(count):
        rows = [jnp.broadcast_to(blocks[b][a : a + 1], shape) for a in range(8)]
        entry = {
            (a, c): jnp.broadcast_to(rows[a][:, 8 * b + c : 8 * b + c + 1], shape)
            for a in range(8)
            for c in range(8)
        }
        columns = {
            i: [jnp.broadcast_to(blocks[i][:, 8 * b + c : 8 * b + c + 1], shape) for c in range(8)]
            for i in range(b + 1, count)
        }
        pivots, inverses = rows[0], None
        for a in range(8):
            inverse = 1.0 / entry[a, a]
            inverses = inverse if a == 0 else jnp.where(sub == a, inverse, inverses)
            if a > 0:
                pivots = jnp.where(sub == a, rows[a], pivots)
            for r in range(a + 1, 8):
                m = entry[r, a] * inverse
                rows[r] = rows[r] - m * rows[a]
                for c in range(a + 1, 8):
                    entry[r, c] = entry[r, c] - m * entry[a, c]
            for i in columns:
                m = columns[i][a] * inverse
                for c in range(a + 1, 8):
                    columns[i][c] = columns[i][c] - m * entry[a, c]
                columns[i][a] = m
        for i in columns:
            update = columns[i][0] * rows[0]
            for a in range(1, 8):
                update = update + columns[i][a] * rows[a]
            blocks[i] = blocks[i] - update
        scaled.append(pivots * jnp.sqrt(inverses))
    return jnp.concatenate(scaled, axis=0)[:, K:]


def whiten_kernel(scale, g_ref, e_ref, i_ref, out_ref, buf, sems):
    g = g_ref[...] * scale
    high, mid, low = split(inverse_factor(jnp.concatenate([g[:, :K], g[:, K:]], axis=0)))
    left = jnp.concatenate([high, mid, high, low, mid, high], axis=1)
    copies = []
    for n, (at, y) in enumerate(
        ((tile(0, 3), e_ref[:, tile(0, 3)]), (tile(3, 2), i_ref[...]), (tile(5, 3), e_ref[:, tile(3, 3)]))
    ):
        yh, ym, yl = split(y)
        right = jnp.concatenate([yh, yh, ym, yh, ym, yl], axis=0)
        buf[:, at] = dot(left, right)
        copy = pltpu.make_async_copy(buf.at[:, at], out_ref.at[:, at], sems.at[n])
        copy.start()
        copies.append(copy)
    for copy in copies:
        copy.wait()


def local(modes, tiles, tile_pair, boundary):
    count = lax.axis_size("slab") * lax.axis_size("col")
    parity = (lax.axis_index("col") & 1).astype(jnp.int32).reshape(1)
    pairs_even = [(i, i ^ 1) for i in range(count)]
    pairs_odd = [(i, (i + 1) % count if i % 2 else (i - 1) % count) for i in range(count)]

    def exchange(se, so):
        ro = lax.ppermute(so, AXES, pairs_odd)
        re = lax.ppermute(se, AXES, pairs_even)
        return re, ro

    def f32(tiles_wide):
        return pltpu.VMEM((K, tiles_wide * TB), F32)

    def weights(n):
        return pltpu.VMEM((n * TB, TB), BF16)

    def sends(rows):
        return pltpu.VMEM((rows, TB), BF16)

    w_out, w_edge, z, se, so, inv = pl.pallas_call(
        first_kernel,
        out_shape=(
            weights(4), weights(2), f32(2), sends(2 * K + TB), sends(2 * K + TB), pltpu.SMEM((TL,), jnp.int32),
        ),
        in_specs=[HBM, SM, HBM, HBM, HBM],
        out_specs=(VM, VM, VM, VM, VM, SM),
        scratch_shapes=[
            pltpu.SMEM((TL,), jnp.int32),
            pltpu.SMEM((1, 2), jnp.int32),
            pltpu.VMEM((K, 4 * TB), F32),
            pltpu.SemaphoreType.DMA((8,)),
            pltpu.SemaphoreType.DMA((2,)),
        ],
        compiler_params=params(8),
        name="first",
    )(hbm(boundary), parity, hbm(tile_pair), hbm(modes), hbm(tiles))
    re, ro = exchange(se, so)
    w_in, j, m, b, o, fe, fo = pl.pallas_call(
        load_kernel,
        out_shape=(weights(18), f32(6), f32(4), f32(4), f32(2), weights(1), weights(1)),
        in_specs=[SM, SM, HBM, HBM, VM, VM],
        out_specs=(VM,) * 7,
        scratch_shapes=[
            pltpu.VMEM((K, ROWS), F32),
            pltpu.VMEM((K, ROWS), BF16),
            pltpu.VMEM((K, 6 * TB), BF16),
            pltpu.SemaphoreType.DMA((18,)),
            pltpu.SemaphoreType.DMA,
        ],
        compiler_params=params(12),
        cost_estimate=cost(40),
        name="load",
    )(parity, inv, hbm(modes), hbm(tiles), pin(w_out), pin(w_edge))
    fe, fo = exchange(fe, fo)
    e, z, se, so, wn = pl.pallas_call(
        edge2_kernel,
        out_shape=(f32(4), f32(2), sends(3 * K), sends(3 * K), weights(2)),
        in_specs=[SM] + [VM] * 9,
        out_specs=(VM,) * 5,
        compiler_params=params(8),
        name="edge2",
    )(parity, re, ro, pin(z), pin(o), pin(b), pin(w_in), pin(w_out), pin(m), pin(j))
    state = (e, m, j)
    for later in (False, True):
        re, ro = exchange(se, so)
        outs = pl.pallas_call(
            functools.partial(step_kernel, later, later),
            out_shape=(f32(4), f32(4), f32(2), f32(2), f32(4)) + ((pltpu.VMEM((K, K), F32),) if later else ()),
            in_specs=[VM] * (len(state) + 3),
            out_specs=(VM,) * (6 if later else 5),
            scratch_shapes=[
                pltpu.VMEM((K, ROWS), BF16),
                pltpu.VMEM((K, 6 * TB), BF16),
                pltpu.VMEM((K, 4 * TB), BF16),
                pltpu.VMEM((K, 6 * TB), F32),
            ],
            compiler_params=params(10),
            cost_estimate=cost(52),
            name="step",
        )(*(pin(x) for x in state), pin(w_in), pin(w_out), pin(w_edge))
        m, b, o, t, c = outs[:5]
        shared = (
            parity, re, ro, pin(z), pin(o), pin(b), pin(c), pin(w_in), pin(w_out), pin(wn), pin(w_edge), fe, fo
        )
        if not later:
            e, p, z, se, so = pl.pallas_call(
                functools.partial(edge3_kernel, False),
                out_shape=(f32(6), f32(2), f32(2), sends(3 * K), sends(3 * K)),
                in_specs=[SM] + [VM] * 12,
                out_specs=(VM,) * 5,
                compiler_params=params(8),
                name="edge3",
            )(*shared)
            state = (e, t, p, m)
    e, g = pl.pallas_call(
        functools.partial(edge3_kernel, True),
        out_shape=(f32(6), pltpu.VMEM((K // 2, 2 * K), F32)),
        in_specs=[SM] + [VM] * 13,
        out_specs=(VM, VM),
        compiler_params=params(8),
        name="final",
    )(*shared, pin(outs[5]))
    for group in ((16,), (1, 3, 2), (4, 12, 8), (32, 96, 64)):
        got = [lax.ppermute(g, AXES, [(i, i ^ bits) for i in range(count)]) for bits in group]
        for other in got:
            g = g + other
    return pl.pallas_call(
        functools.partial(whiten_kernel, 1.0 / (ROWS * count)),
        out_shape=jax.ShapeDtypeStruct((K, ROWS), F32),
        in_specs=[VM, VM, VM],
        out_specs=HBM,
        scratch_shapes=[pltpu.VMEM((K, ROWS), F32), pltpu.SemaphoreType.DMA((3,))],
        compiler_params=params(16),
        name="whiten",
    )(g, pin(e), pin(t))


def solution(mesh):
    placed = (
        P(None, AXES),
        P(AXES, None, None),
        P(AXES),
        P(AXES, None),
    )
    return jax.shard_map(
        local, mesh=mesh, in_specs=placed, out_specs=P(None, AXES), check_vma=False
    )
```

time: 74.7 us -> 70.5 us (0.944)
  starting transfers between devices: 43.8 us -> 36.2 us
  waiting for transfers between devices: 9.99 us -> 12.5 us
  Pallas kernels: 20.4 us -> 21.3 us
    ppermute x4, starting transfers between devices: 28.6 us -> 19.9 us  [exchange(): ro = lax.ppermute(so, AXES, pairs_odd)]
    ppermute x10, waiting for transfers between devices: 7.7 us -> 9.38 us  [local(): lax.ppermute(g, AXES, [(i, i ^ bits) for i in range(count)])]
    ppermute x4, starting transfers between devices: 1.99 us -> 3.01 us  [exchange(): re = lax.ppermute(se, AXES, pairs_even)]
    ppermute x4, waiting for transfers between devices: 2.27 us -> 3.14 us  [exchange(): ro = lax.ppermute(so, AXES, pairs_odd)]
    pallas_call x8 -> x6, Pallas kernels: 14.3 us -> 15.2 us  [the longest x2 5.28 us: local(): pl.pallas_call(functools.partial(step_kernel, later, later), out_shape=(f...]
  transfers between devices with their start and end apart: 18 -> 18, of which waited for: 9 -> 9; matrix products, arithmetic and copies ran while one was open for 0% -> 0% of each run, Pallas kernels for 14% -> 16%
where the time goes in v3:
time: 70.5 us; the launch traced here: 70.3 us
  starting transfers between devices  36.2 us (51%)
  Pallas kernels  21.3 us (30%)
  waiting for transfers between devices  12.5 us (18%)
    ppermute x4, starting transfers between devices, exchange(): ro = lax.ppermute(so, AXES, pairs_odd)  19.9 us
    ppermute x10, starting transfers between devices, local(): lax.ppermute(g, AXES, [(i, i ^ bits) for i in range(count)])  13.3 us
    ppermute x10, waiting for transfers between devices, local(): lax.ppermute(g, AXES, [(i, i ^ bits) for i in range(count)])  9.38 us
    pallas_call x2, Pallas kernels, local(): pl.pallas_call(functools.partial(step_kernel, later, later), out_shape=(f...  5.28 us
    pallas_call x1, Pallas kernels, local(): pl.pallas_call(load_kernel, out_shape=(weights(18), f32(6), f32(4), f32(4...  4.88 us
    pallas_call x1, Pallas kernels, local(): pl.pallas_call(functools.partial(whiten_kernel, 1.0 / (ROWS * count)), ou...  3.4 us
    ppermute x4, waiting for transfers between devices, exchange(): ro = lax.ppermute(so, AXES, pairs_odd)  3.14 us
    ppermute x4, starting transfers between devices, exchange(): re = lax.ppermute(se, AXES, pairs_even)  3.01 us
  transfers between devices with their start and end apart: 18, of which 9 were waited for; matrix products, arithmetic and copies ran while one was open for 0% of the time, Pallas kernels for 16%

profile of v3, /device:TPU:0, one launch (start us, length us, event | category | flops | bytes accessed | tf_op | source)
XLA Modules:
  0.0 70.3 jit_solution(13002382876522964635)
XLA Ops:
  0.0 2.7 %first.1 = (bf16[1536,384]{1,0:T(8,128)(2,1)S(1)}, bf16[768,384]{1,0:T(8,128)(2,1)S(1)}, f32[64,768]{1,0:T(8,128)S(1)}, bf16[512,384]{1,0:T(8,128)(2,1)S(1)}, bf...) custom-call(s32[1,2]{1,0:T(1,128)} %bound_ref.1, s32[1]{0:T(128)} %bitcast.par_ref, s32[24]{0:T(128)} %pair_ref.1, ...), custom_call_target="tpu_custom_call" | custom-call | tf_op jit(solution)/shard_map/first/pallas_call | solution.py:439
  2.7 1.7 %collective-permute-start = (bf16[512,384]{1,0:T(8,128)(2,1)S(1)}, bf16[512,384]{1,0:T(8,128)(2,1)S(1)}, u32[]{:S(2)}, u32[]{:S(2)}) collective-permute-start(bf16[512,384]{1,0:T(8,128)(2,1)S(1)} %get-tuple-element.40), channel_id=1, source_target_pairs={{0,1},{1,0},{2,3},{3,2},{4,5},{5,4},{6,7},{7,6},{8,9},{9,8},{10,11... | collective-permute-start | bytes 1179656 | tf_op jit(solution)/shard_map/ppermute | solution.py:427
  4.5 7.0 %collective-permute-start.1 = (bf16[512,384]{1,0:T(8,128)(2,1)S(1)}, bf16[512,384]{1,0:T(8,128)(2,1)S(1)}, u32[]{:S(2)}, u32[]{:S(2)}) collective-permute-start(bf16[512,384]{1,0:T(8,128)(2,1)S(1)} %get-tuple-element.41), channel_id=1, source_target_pairs={{0,127},{1,2},{2,1},{3,4},{4,3},{5,6},{6,5},{7,8},{8,7},{9,10},{10... | collective-permute-start | bytes 1179656 | tf_op jit(solution)/shard_map/ppermute | solution.py:426
  11.5 4.9 %load.1 = (bf16[6912,384]{1,0:T(8,128)(2,1)S(1)}, f32[64,2304]{1,0:T(8,128)S(1)}, f32[64,1536]{1,0:T(8,128)S(1)}, f32[64,1536]{1,0:T(8,128)S(1)}, f32[64,768]{1,...) custom-call(s32[1]{0:T(128)} %bitcast.par_ref, s32[24]{0:T(128)S(4)} %get-tuple-element.43.inv_ref, ...), custom_call_target="tpu_custom_call" | custom-call | flops 754974720 | bytes 8388608 | tf_op jit(solution)/shard_map/load/pallas_call | solution.py:457
  16.4 0.1 collective-permute-start.4
  16.4 1.0 %collective-permute-start.5 = (bf16[384,384]{1,0:T(8,128)(2,1)S(1)}, bf16[384,384]{1,0:T(8,128)(2,1)S(1)}, u32[]{:S(2)}, u32[]{:S(2)}) collective-permute-start(bf16[384,384]{1,0:T(8,128)(2,1)S(1)} %get-tuple-element.60), channel_id=1, source_target_pairs={{0,127},{1,2},{2,1},{3,4},{4,3},{5,6},{6,5},{7,8},{8,7},{9,10},{10... | collective-permute-start | bytes 884744 | tf_op jit(solution)/shard_map/ppermute | solution.py:426
  17.5 1.2 %edge2.1 = (f32[64,1536]{1,0:T(8,128)S(1)}, f32[64,768]{1,0:T(8,128)S(1)}, bf16[192,384]{1,0:T(8,128)(2,1)S(1)}, bf16[192,384]{1,0:T(8,128)(2,1)S(1)}, bf16[768,384]{1,0:T(8,128)(2,1)S(1)}) custom-call(s32[1]{0:T(128)} %bitcast.par_ref, bf16[512,384]{1,0:T(8,128)(2,1)S(1)} %collective-permute-done.re_ref, ...), custom_call_target="tpu_custom_call" | custom-call | tf_op jit(solution)/shard_map/edge2/pallas_call | solution.py:474
  18.6 1.1 %collective-permute-start.2 = (bf16[192,384]{1,0:T(8,128)(2,1)S(1)}, bf16[192,384]{1,0:T(8,128)(2,1)S(1)}, u32[]{:S(2)}, u32[]{:S(2)}) collective-permute-start(bf16[192,384]{1,0:T(8,128)(2,1)S(1)} %get-tuple-element.51), channel_id=1, source_target_pairs={{0,1},{1,0},{2,3},{3,2},{4,5},{5,4},{6,7},{7,6},{8,9},{9,8},{10,11... | collective-permute-start | bytes 442376 | tf_op jit(solution)/shard_map/ppermute | solution.py:427
  19.7 5.8 %collective-permute-start.3 = (bf16[192,384]{1,0:T(8,128)(2,1)S(1)}, bf16[192,384]{1,0:T(8,128)(2,1)S(1)}, u32[]{:S(2)}, u32[]{:S(2)}) collective-permute-start(bf16[192,384]{1,0:T(8,128)(2,1)S(1)} %get-tuple-element.52), channel_id=1, source_target_pairs={{0,127},{1,2},{2,1},{3,4},{4,3},{5,6},{6,5},{7,8},{8,7},{9,10},{10... | collective-permute-start | bytes 442376 | tf_op jit(solution)/shard_map/ppermute | solution.py:426
  25.5 2.5 %step.2 = (f32[64,1536]{1,0:T(8,128)S(1)}, f32[64,1536]{1,0:T(8,128)S(1)}, f32[64,768]{1,0:T(8,128)S(1)}, f32[64,768]{1,0:T(8,128)S(1)}, f32[64,1536]{1,0:T(8,128)S(1)}) custom-call(f32[64,1536]{1,0:T(8,128)S(1)} %get-tuple-element.54.refs_0_, f32[64,1536]{1,0:T(8,128)S(1)} %get-tuple-element.49.m_ref.refs_1_, ...), custom_call_target="tpu_custom_call" | custom-call | flops 981467136 | bytes 8388608 | tf_op jit(solution)/shard_map/step/pallas_call | solution.py:485
  28.0 0.1 collective-permute-done.5.fo_ref
  28.1 1.6 %collective-permute-done.3.ro_ref = bf16[192,384]{1,0:T(8,128)(2,1)S(1)} collective-permute-done((bf16[192,384]{1,0:T(8,128)(2,1)S(1)}, bf16[192,384]{1,0:T(8,128)(2,1)S(1)}, u32[]{:S(2)}, u32[]{:S(2)}) %collective-permute-start.3) | collective-permute-done | bytes 147488 | tf_op jit(solution)/shard_map/ppermute | solution.py:426
  29.7 2.0 %edge3.1 = (f32[64,2304]{1,0:T(8,128)S(1)}, f32[64,768]{1,0:T(8,128)S(1)}, f32[64,768]{1,0:T(8,128)S(1)}, bf16[192,384]{1,0:T(8,128)(2,1)S(1)}, bf16[192,384]{1,0:T(8,128)(2,1)S(1)}) custom-call(s32[1]{0:T(128)} %bitcast.par_ref, bf16[192,384]{1,0:T(8,128)(2,1)S(1)} %collective-permute-done.2.re_ref, bf16[192,384]{1,0:T(8,128)(2,1)S(1)} %collective-permute-done.3.ro_ref, ...), custom_call_target="tpu_custom_call" | custom-call | tf_op jit(solution)/shard_map/edge3/pallas_call | solution.py:505
  31.7 0.1 collective-permute-start.6
  31.8 6.1 %collective-permute-start.7 = (bf16[192,384]{1,0:T(8,128)(2,1)S(1)}, bf16[192,384]{1,0:T(8,128)(2,1)S(1)}, u32[]{:S(2)}, u32[]{:S(2)}) collective-permute-start(bf16[192,384]{1,0:T(8,128)(2,1)S(1)} %get-tuple-element.62), channel_id=1, source_target_pairs={{0,127},{1,2},{2,1},{3,4},{4,3},{5,6},{6,5},{7,8},{8,7},{9,10},{10... | collective-permute-start | bytes 442376 | tf_op jit(solution)/shard_map/ppermute | solution.py:426
  37.9 2.8 %step.3 = (f32[64,1536]{1,0:T(8,128)}, f32[64,1536]{1,0:T(8,128)S(1)}, f32[64,768]{1,0:T(8,128)S(1)}, f32[64,768]{1,0:T(8,128)S(1)}, f32[64,1536]{1,0:T(8,128)S(1)}, /*index=5*/f32[64,64]{1,0:T(8,128)S(1)}) custom-call(f32[64,2304]{1,0:T(8,128)S(1)} %get-tuple-element.64.refs_0_, f32[64,768]{1,0:T(8,128)S(1)} %get-tuple-element.65.refs_1_, ...), custom_call_target="tpu_custom_call" | custom-call | flops 981467136 | bytes 8388608 | tf_op jit(solution)/shard_map/step/pallas_call | solution.py:485
  40.7 1.5 %collective-permute-done.7.ro_ref = bf16[192,384]{1,0:T(8,128)(2,1)S(1)} collective-permute-done((bf16[192,384]{1,0:T(8,128)(2,1)S(1)}, bf16[192,384]{1,0:T(8,128)(2,1)S(1)}, u32[]{:S(2)}, u32[]{:S(2)}) %collective-permute-start.7) | collective-permute-done | bytes 147488 | tf_op jit(solution)/shard_map/ppermute | solution.py:426
  42.1 1.9 %final.1 = (f32[64,2304]{1,0:T(8,128)S(1)}, f32[32,128]{1,0:T(8,128)S(1)}) custom-call(s32[1]{0:T(128)} %bitcast.par_ref, bf16[192,384]{1,0:T(8,128)(2,1)S(1)} %collective-permute-done.6.re_ref, bf16[192,384]{1,0:T(8,128)(2,1)S(1)} %collective-permute-done.7.ro_ref, f32[64,768]{1,0:T(8,128)S(1)} %get-tuple-element.63.z_ref, ...), custom_call_target="tpu_custom_call" | custom-call | tf_op jit(solution)/shard_map/final/pallas_call | solution.py:514
  44.0 1.3 %collective-permute-start.8 = (f32[32,128]{1,0:T(8,128)S(1)}, f32[32,128]{1,0:T(8,128)S(1)}, u32[]{:S(2)}, u32[]{:S(2)}) collective-permute-start(f32[32,128]{1,0:T(8,128)S(1)} %get-tuple-element.72), channel_id=1, source_target_pairs={{0,16},{1,17},{2,18},{3,19},{4,20},{5,21},{6,22},{7,23},{8,24},{9,... | collective-permute-start | bytes 49160 | tf_op jit(solution)/shard_map/ppermute | solution.py:523
  45.4 0.8 %collective-permute-done.8 = f32[32,128]{1,0:T(8,128)S(1)} collective-permute-done((f32[32,128]{1,0:T(8,128)S(1)}, f32[32,128]{1,0:T(8,128)S(1)}, u32[]{:S(2)}, u32[]{:S(2)}) %collective-permute-start.8) | collective-permute-done | bytes 16416 | tf_op jit(solution)/shard_map/ppermute | solution.py:523
  46.3 3.4 %collective-permute-start.9 = (f32[32,128]{1,0:T(8,128)S(1)}, f32[32,128]{1,0:T(8,128)S(1)}, u32[]{:S(2)}, u32[]{:S(2)}) collective-permute-start(f32[32,128]{1,0:T(8,128)S(1)} %add.30), channel_id=1, source_target_pairs={{0,1},{1,0},{2,3},{3,2},{4,5},{5,4},{6,7},{7,6},{8,9},{9,8},{10,11... | collective-permute-start | bytes 49160 | tf_op jit(solution)/shard_map/ppermute | solution.py:523
  49.7 1.8 %collective-permute-done.11 = f32[32,128]{1,0:T(8,128)S(1)} collective-permute-done((f32[32,128]{1,0:T(8,128)S(1)}, f32[32,128]{1,0:T(8,128)S(1)}, u32[]{:S(2)}, u32[]{:S(2)}) %collective-permute-start.11) | collective-permute-done | bytes 16416 | tf_op jit(solution)/shard_map/ppermute | solution.py:523
  51.5 0.1 collective-permute-start.14
  51.6 3.5 %collective-permute-start.13 = (f32[32,128]{1,0:T(8,128)S(1)}, f32[32,128]{1,0:T(8,128)S(1)}, u32[]{:S(2)}, u32[]{:S(2)}) collective-permute-start(f32[32,128]{1,0:T(8,128)S(1)} %add_add_fusion.2), channel_id=1, source_target_pairs={{0,12},{1,13},{2,14},{3,15},{4,8},{5,9},{6,10},{7,11},{8,4},{9,5},... | collective-permute-start | bytes 49160 | tf_op jit(solution)/shard_map/ppermute | solution.py:523
  55.0 0.8 %collective-permute-start.12 = (f32[32,128]{1,0:T(8,128)S(1)}, f32[32,128]{1,0:T(8,128)S(1)}, u32[]{:S(2)}, u32[]{:S(2)}) collective-permute-start(f32[32,128]{1,0:T(8,128)S(1)} %add_add_fusion.2), channel_id=1, source_target_pairs={{0,4},{1,5},{2,6},{3,7},{4,0},{5,1},{6,2},{7,3},{8,12},{9,13},{10,... | collective-permute-start | bytes 49160 | tf_op jit(solution)/shard_map/ppermute | solution.py:523
  55.8 1.1 %collective-permute-done.14 = f32[32,128]{1,0:T(8,128)S(1)} collective-permute-done((f32[32,128]{1,0:T(8,128)S(1)}, f32[32,128]{1,0:T(8,128)S(1)}, u32[]{:S(2)}, u32[]{:S(2)}) %collective-permute-start.14) | collective-permute-done | bytes 16416 | tf_op jit(solution)/shard_map/ppermute | solution.py:523
  56.9 1.8 %collective-permute-done.12 = f32[32,128]{1,0:T(8,128)S(1)} collective-permute-done((f32[32,128]{1,0:T(8,128)S(1)}, f32[32,128]{1,0:T(8,128)S(1)}, u32[]{:S(2)}, u32[]{:S(2)}) %collective-permute-start.12) | collective-permute-done | bytes 16416 | tf_op jit(solution)/shard_map/ppermute | solution.py:523
  58.8 3.0 %collective-permute-start.17 = (f32[32,128]{1,0:T(8,128)S(1)}, f32[32,128]{1,0:T(8,128)S(1)}, u32[]{:S(2)}, u32[]{:S(2)}) collective-permute-start(f32[32,128]{1,0:T(8,128)S(1)} %add_add_fusion.1), channel_id=1, source_target_pairs={{0,64},{1,65},{2,66},{3,67},{4,68},{5,69},{6,70},{7,71},{8,72},{9,... | collective-permute-start | bytes 49160 | tf_op jit(solution)/shard_map/ppermute | solution.py:523
  61.8 1.1 %collective-permute-start.16 = (f32[32,128]{1,0:T(8,128)S(1)}, f32[32,128]{1,0:T(8,128)S(1)}, u32[]{:S(2)}, u32[]{:S(2)}) collective-permute-start(f32[32,128]{1,0:T(8,128)S(1)} %add_add_fusion.1), channel_id=1, source_target_pairs={{0,96},{1,97},{2,98},{3,99},{4,100},{5,101},{6,102},{7,103},{8,104... | collective-permute-start | bytes 49160 | tf_op jit(solution)/shard_map/ppermute | solution.py:523
  63.0 1.1 %collective-permute-done.17 = f32[32,128]{1,0:T(8,128)S(1)} collective-permute-done((f32[32,128]{1,0:T(8,128)S(1)}, f32[32,128]{1,0:T(8,128)S(1)}, u32[]{:S(2)}, u32[]{:S(2)}) %collective-permute-start.17) | collective-permute-done | bytes 16416 | tf_op jit(solution)/shard_map/ppermute | solution.py:523
  64.0 2.7 %collective-permute-done.16 = f32[32,128]{1,0:T(8,128)S(1)} collective-permute-done((f32[32,128]{1,0:T(8,128)S(1)}, f32[32,128]{1,0:T(8,128)S(1)}, u32[]{:S(2)}, u32[]{:S(2)}) %collective-permute-start.16) | collective-permute-done | bytes 16416 | tf_op jit(solution)/shard_map/ppermute | solution.py:523
  66.8 3.4 %whiten.1 = f32[64,3072]{1,0:T(8,128)} custom-call(f32[32,128]{1,0:T(8,128)S(1)} %add_add_fusion.g_ref, f32[64,2304]{1,0:T(8,128)S(1)} %get-tuple-element.73.e_ref, f32[64,768]{1,0:T(8,128)S(1)} %get-tuple-element.74.i_ref), custom_call_target="tpu_custom_call" | custom-call | tf_op jit(solution)/shard_map/whiten/pallas_call | solution.py:526
  (16 shorter events, 0.1 us)
Async XLA Ops:
  2.7 14.7 %collective-permute-start = (bf16[512,384]{1,0:T(8,128)(2,1)S(1)}, bf16[512,384]{1,0:T(8,128)(2,1)S(1)}, u32[]{:S(2)}, u32[]{:S(2)}) collective-permute-start(bf16[512,384]{1,0:T(8,128)(2,1)S(1)} %get-tuple-element.40), channel_id=1, source_target_pairs={{0,1},{1,0},{2,3},{3,2},{4,5},{5,4},{6,7},{7,6},{8,9},{9,8},{10,11... | collective-permute-start | bytes 1179656 | tf_op jit(solution)/shard_map/ppermute | solution.py:427
  4.5 13.0 %collective-permute-start.1 = (bf16[512,384]{1,0:T(8,128)(2,1)S(1)}, bf16[512,384]{1,0:T(8,128)(2,1)S(1)}, u32[]{:S(2)}, u32[]{:S(2)}) collective-permute-start(bf16[512,384]{1,0:T(8,128)(2,1)S(1)} %get-tuple-element.41), channel_id=1, source_target_pairs={{0,127},{1,2},{2,1},{3,4},{4,3},{5,6},{6,5},{7,8},{8,7},{9,10},{10... | collective-permute-start | bytes 1179656 | tf_op jit(solution)/shard_map/ppermute | solution.py:426
  16.4 11.7 %collective-permute-start.4 = (bf16[384,384]{1,0:T(8,128)(2,1)S(1)}, bf16[384,384]{1,0:T(8,128)(2,1)S(1)}, u32[]{:S(2)}, u32[]{:S(2)}) collective-permute-start(bf16[384,384]{1,0:T(8,128)(2,1)S(1)} %get-tuple-element.59), channel_id=1, source_target_pairs={{0,1},{1,0},{2,3},{3,2},{4,5},{5,4},{6,7},{7,6},{8,9},{9,8},{10,11... | collective-permute-start | bytes 884744 | tf_op jit(solution)/shard_map/ppermute | solution.py:427
  16.4 11.7 %collective-permute-start.5 = (bf16[384,384]{1,0:T(8,128)(2,1)S(1)}, bf16[384,384]{1,0:T(8,128)(2,1)S(1)}, u32[]{:S(2)}, u32[]{:S(2)}) collective-permute-start(bf16[384,384]{1,0:T(8,128)(2,1)S(1)} %get-tuple-element.60), channel_id=1, source_target_pairs={{0,127},{1,2},{2,1},{3,4},{4,3},{5,6},{6,5},{7,8},{8,7},{9,10},{10... | collective-permute-start | bytes 884744 | tf_op jit(solution)/shard_map/ppermute | solution.py:426
  18.6 9.5 %collective-permute-start.2 = (bf16[192,384]{1,0:T(8,128)(2,1)S(1)}, bf16[192,384]{1,0:T(8,128)(2,1)S(1)}, u32[]{:S(2)}, u32[]{:S(2)}) collective-permute-start(bf16[192,384]{1,0:T(8,128)(2,1)S(1)} %get-tuple-element.51), channel_id=1, source_target_pairs={{0,1},{1,0},{2,3},{3,2},{4,5},{5,4},{6,7},{7,6},{8,9},{9,8},{10,11... | collective-permute-start | bytes 442376 | tf_op jit(solution)/shard_map/ppermute | solution.py:427
  19.7 10.0 %collective-permute-start.3 = (bf16[192,384]{1,0:T(8,128)(2,1)S(1)}, bf16[192,384]{1,0:T(8,128)(2,1)S(1)}, u32[]{:S(2)}, u32[]{:S(2)}) collective-permute-start(bf16[192,384]{1,0:T(8,128)(2,1)S(1)} %get-tuple-element.52), channel_id=1, source_target_pairs={{0,127},{1,2},{2,1},{3,4},{4,3},{5,6},{6,5},{7,8},{8,7},{9,10},{10... | collective-permute-start | bytes 442376 | tf_op jit(solution)/shard_map/ppermute | solution.py:426
  31.7 9.0 %collective-permute-start.6 = (bf16[192,384]{1,0:T(8,128)(2,1)S(1)}, bf16[192,384]{1,0:T(8,128)(2,1)S(1)}, u32[]{:S(2)}, u32[]{:S(2)}) collective-permute-start(bf16[192,384]{1,0:T(8,128)(2,1)S(1)} %get-tuple-element.61), channel_id=1, source_target_pairs={{0,1},{1,0},{2,3},{3,2},{4,5},{5,4},{6,7},{7,6},{8,9},{9,8},{10,11... | collective-permute-start | bytes 442376 | tf_op jit(solution)/shard_map/ppermute | solution.py:427
  31.8 10.4 %collective-permute-start.7 = (bf16[192,384]{1,0:T(8,128)(2,1)S(1)}, bf16[192,384]{1,0:T(8,128)(2,1)S(1)}, u32[]{:S(2)}, u32[]{:S(2)}) collective-permute-start(bf16[192,384]{1,0:T(8,128)(2,1)S(1)} %get-tuple-element.62), channel_id=1, source_target_pairs={{0,127},{1,2},{2,1},{3,4},{4,3},{5,6},{6,5},{7,8},{8,7},{9,10},{10... | collective-permute-start | bytes 442376 | tf_op jit(solution)/shard_map/ppermute | solution.py:426
  44.0 2.2 %collective-permute-start.8 = (f32[32,128]{1,0:T(8,128)S(1)}, f32[32,128]{1,0:T(8,128)S(1)}, u32[]{:S(2)}, u32[]{:S(2)}) collective-permute-start(f32[32,128]{1,0:T(8,128)S(1)} %get-tuple-element.72), channel_id=1, source_target_pairs={{0,16},{1,17},{2,18},{3,19},{4,20},{5,21},{6,22},{7,23},{8,24},{9,... | collective-permute-start | bytes 49160 | tf_op jit(solution)/shard_map/ppermute | solution.py:523
  46.2 5.2 %collective-permute-start.11 = (f32[32,128]{1,0:T(8,128)S(1)}, f32[32,128]{1,0:T(8,128)S(1)}, u32[]{:S(2)}, u32[]{:S(2)}) collective-permute-start(f32[32,128]{1,0:T(8,128)S(1)} %add.30), channel_id=1, source_target_pairs={{0,2},{1,3},{2,0},{3,1},{4,6},{5,7},{6,4},{7,5},{8,10},{9,11},{10,... | collective-permute-start | bytes 49160 | tf_op jit(solution)/shard_map/ppermute | solution.py:523
  46.2 5.2 %collective-permute-start.10 = (f32[32,128]{1,0:T(8,128)S(1)}, f32[32,128]{1,0:T(8,128)S(1)}, u32[]{:S(2)}, u32[]{:S(2)}) collective-permute-start(f32[32,128]{1,0:T(8,128)S(1)} %add.30), channel_id=1, source_target_pairs={{0,3},{1,2},{2,1},{3,0},{4,7},{5,6},{6,5},{7,4},{8,11},{9,10},{10,... | collective-permute-start | bytes 49160 | tf_op jit(solution)/shard_map/ppermute | solution.py:523
  46.3 5.2 %collective-permute-start.9 = (f32[32,128]{1,0:T(8,128)S(1)}, f32[32,128]{1,0:T(8,128)S(1)}, u32[]{:S(2)}, u32[]{:S(2)}) collective-permute-start(f32[32,128]{1,0:T(8,128)S(1)} %add.30), channel_id=1, source_target_pairs={{0,1},{1,0},{2,3},{3,2},{4,5},{5,4},{6,7},{7,6},{8,9},{9,8},{10,11... | collective-permute-start | bytes 49160 | tf_op jit(solution)/shard_map/ppermute | solution.py:523
  51.5 5.4 %collective-permute-start.14 = (f32[32,128]{1,0:T(8,128)S(1)}, f32[32,128]{1,0:T(8,128)S(1)}, u32[]{:S(2)}, u32[]{:S(2)}) collective-permute-start(f32[32,128]{1,0:T(8,128)S(1)} %add_add_fusion.2), channel_id=1, source_target_pairs={{0,8},{1,9},{2,10},{3,11},{4,12},{5,13},{6,14},{7,15},{8,0},{9,1},... | collective-permute-start | bytes 49160 | tf_op jit(solution)/shard_map/ppermute | solution.py:523
  51.6 5.4 %collective-permute-start.13 = (f32[32,128]{1,0:T(8,128)S(1)}, f32[32,128]{1,0:T(8,128)S(1)}, u32[]{:S(2)}, u32[]{:S(2)}) collective-permute-start(f32[32,128]{1,0:T(8,128)S(1)} %add_add_fusion.2), channel_id=1, source_target_pairs={{0,12},{1,13},{2,14},{3,15},{4,8},{5,9},{6,10},{7,11},{8,4},{9,5},... | collective-permute-start | bytes 49160 | tf_op jit(solution)/shard_map/ppermute | solution.py:523
  55.0 3.7 %collective-permute-start.12 = (f32[32,128]{1,0:T(8,128)S(1)}, f32[32,128]{1,0:T(8,128)S(1)}, u32[]{:S(2)}, u32[]{:S(2)}) collective-permute-start(f32[32,128]{1,0:T(8,128)S(1)} %add_add_fusion.2), channel_id=1, source_target_pairs={{0,4},{1,5},{2,6},{3,7},{4,0},{5,1},{6,2},{7,3},{8,12},{9,13},{10,... | collective-permute-start | bytes 49160 | tf_op jit(solution)/shard_map/ppermute | solution.py:523
  58.8 5.2 %collective-permute-start.17 = (f32[32,128]{1,0:T(8,128)S(1)}, f32[32,128]{1,0:T(8,128)S(1)}, u32[]{:S(2)}, u32[]{:S(2)}) collective-permute-start(f32[32,128]{1,0:T(8,128)S(1)} %add_add_fusion.1), channel_id=1, source_target_pairs={{0,64},{1,65},{2,66},{3,67},{4,68},{5,69},{6,70},{7,71},{8,72},{9,... | collective-permute-start | bytes 49160 | tf_op jit(solution)/shard_map/ppermute | solution.py:523
  61.8 4.9 %collective-permute-start.16 = (f32[32,128]{1,0:T(8,128)S(1)}, f32[32,128]{1,0:T(8,128)S(1)}, u32[]{:S(2)}, u32[]{:S(2)}) collective-permute-start(f32[32,128]{1,0:T(8,128)S(1)} %add_add_fusion.1), channel_id=1, source_target_pairs={{0,96},{1,97},{2,98},{3,99},{4,100},{5,101},{6,102},{7,103},{8,104... | collective-permute-start | bytes 49160 | tf_op jit(solution)/shard_map/ppermute | solution.py:523
  63.0 3.8 %collective-permute-start.15 = (f32[32,128]{1,0:T(8,128)S(1)}, f32[32,128]{1,0:T(8,128)S(1)}, u32[]{:S(2)}, u32[]{:S(2)}) collective-permute-start(f32[32,128]{1,0:T(8,128)S(1)} %add_add_fusion.1), channel_id=1, source_target_pairs={{0,32},{1,33},{2,34},{3,35},{4,36},{5,37},{6,38},{7,39},{8,40},{9,... | collective-permute-start | bytes 49160 | tf_op jit(solution)/shard_map/ppermute | solution.py:523

commit v4 on v3

--- a/solution.py
+++ b/solution.py
@@ -43,6 +43,10 @@
     return jnp.dot(a, b, preferred_element_type=F32)
 
 
+def is_even():
+    return lax.rem(lax.axis_index("col"), 2) == 0
+
+
 def tile(i, n=1):
     return slice(i * TB, (i + n) * TB)
 
@@ -56,7 +60,7 @@
 
 
 def first_kernel(
-    bound_ref, par_ref, pair_ref, modes_ref, tiles_ref,
+    bound_ref, pair_ref, modes_ref, tiles_ref,
     outer_ref, we_ref, z_ref, se_ref, so_ref, inv_ref,
     pair, bound, ym, sems, ssem,
 ):
@@ -73,17 +77,21 @@
     to_smem.wait()
     for t in range(TL):
         inv_ref[pair[t]] = t
-    copies = [
-        pltpu.make_async_copy(tiles_ref.at[inv_ref[p]], outer_ref.at[tile(i)], sems.at[i])
-        for i, p in enumerate(OUTER)
-    ] + [
+    edge_copies = [
         pltpu.make_async_copy(tiles_ref.at[inv_ref[p]], we_ref.at[tile(i)], sems.at[4 + i])
         for i, p in enumerate((0, TL - 1))
     ]
-    for c in copies:
+    outer_copies = [
+        pltpu.make_async_copy(tiles_ref.at[inv_ref[p]], outer_ref.at[tile(i)], sems.at[i])
+        for i, p in enumerate(OUTER)
+    ]
+    for c in edge_copies + outer_copies:
         c.start()
+    for c in modes:
+        c.wait()
+    xs = ym[...].astype(BF16)
     bound_copy.wait()
-    for c in modes + copies:
+    for c in edge_copies:
         c.wait()
     row = lax.broadcasted_iota(jnp.int32, (TB, TB), 0)
     zero = jnp.zeros((TB, TB), BF16)
@@ -91,15 +99,16 @@
     w_high = jnp.where(row >= TB - bound[0, 1], we_ref[tile(1)], zero)
     we_ref[tile(0)] = w_low
     we_ref[tile(1)] = w_high
-    xs = ym[...].astype(BF16)
+    even = is_even()
+    se_ref[2 * K :] = jnp.where(even, w_high, w_low)
+    so_ref[2 * K :] = jnp.where(even, w_low, w_high)
+    for c in outer_copies:
+        c.wait()
     z_low = dot(xs[:, tile(0, 2)], outer_ref[tile(0, 2)]) - center * ym[:, tile(0)]
     z_high = dot(xs[:, tile(2, 2)], outer_ref[tile(2, 2)]) - center * ym[:, tile(3)]
     z_ref[:, tile(0)] = z_low
     z_ref[:, tile(1)] = z_high
-    even = par_ref[0] == 0
     send(even, (xs[:, tile(0)], z_low), (xs[:, tile(3)], z_high), se_ref, so_ref)
-    se_ref[2 * K :] = jnp.where(even, w_high, w_low)
-    so_ref[2 * K :] = jnp.where(even, w_low, w_high)
 
 
 def send(even, low, high, se_ref, so_ref):
@@ -135,7 +144,7 @@
 
 
 def load_kernel(
-    par_ref, inv_ref, modes_ref, tiles_ref, w_out, w_edge,
+    inv_ref, modes_ref, tiles_ref, w_out, w_edge,
     w_in, j_ref, m_ref, b_ref, o_ref, fe_ref, fo_ref,
     y0, xs, xn, sems, msem,
 ):
@@ -151,7 +160,7 @@
     for c in copies:
         c.wait()
     xs[...] = y0[...].astype(BF16)
-    even = par_ref[0] == 0
+    even = is_even()
     w_low, w_high = w_out[tile(0)], w_out[tile(3)]
     fe_ref[...] = jnp.where(even, w_high, w_low)
     fo_ref[...] = jnp.where(even, w_low, w_high)
@@ -267,10 +276,10 @@
 
 
 def edge2_kernel(
-    par_ref, re_ref, ro_ref, z_ref, o_ref, b_ref, w_in, w_out, m_ref, j_ref,
+    re_ref, ro_ref, z_ref, o_ref, b_ref, w_in, w_out, m_ref, j_ref,
     e_ref, zn_ref, se_ref, so_ref, wn_ref,
 ):
-    even = par_ref[0] == 0
+    even = is_even()
     got = chosen(even, re_ref[: 2 * K], ro_ref[: 2 * K])
     for side, w in enumerate(chosen(even, re_ref[2 * K :], ro_ref[2 * K :])):
         wn_ref[tile(side)] = w
@@ -320,9 +329,9 @@
 
 
 def edge3_kernel(
-    last, par_ref, re_ref, ro_ref, z_ref, o_ref, b_ref, c_ref, w_in, w_out, wn_ref, w_edge, fe_ref, fo_ref, *rest
+    last, re_ref, ro_ref, z_ref, o_ref, b_ref, c_ref, w_in, w_out, wn_ref, w_edge, fe_ref, fo_ref, *rest
 ):
-    even = par_ref[0] == 0
+    even = is_even()
     got = chosen(even, re_ref[...], ro_ref[...])
     far = chosen(even, fe_ref[...], fo_ref[...])
     e_ref = rest[1] if last else rest[0]
@@ -418,7 +427,6 @@
 
 def local(modes, tiles, tile_pair, boundary):
     count = lax.axis_size("slab") * lax.axis_size("col")
-    parity = (lax.axis_index("col") & 1).astype(jnp.int32).reshape(1)
     pairs_even = [(i, i ^ 1) for i in range(count)]
     pairs_odd = [(i, (i + 1) % count if i % 2 else (i - 1) % count) for i in range(count)]
 
@@ -441,7 +449,7 @@
         out_shape=(
             weights(4), weights(2), f32(2), sends(2 * K + TB), sends(2 * K + TB), pltpu.SMEM((TL,), jnp.int32),
         ),
-        in_specs=[HBM, SM, HBM, HBM, HBM],
+        in_specs=[HBM, HBM, HBM, HBM],
         out_specs=(VM, VM, VM, VM, VM, SM),
         scratch_shapes=[
             pltpu.SMEM((TL,), jnp.int32),
@@ -452,12 +460,12 @@
         ],
         compiler_params=params(8),
         name="first",
-    )(hbm(boundary), parity, hbm(tile_pair), hbm(modes), hbm(tiles))
+    )(hbm(boundary), hbm(tile_pair), hbm(modes), hbm(tiles))
     re, ro = exchange(se, so)
     w_in, j, m, b, o, fe, fo = pl.pallas_call(
         load_kernel,
         out_shape=(weights(18), f32(6), f32(4), f32(4), f32(2), weights(1), weights(1)),
-        in_specs=[SM, SM, HBM, HBM, VM, VM],
+        in_specs=[SM, HBM, HBM, VM, VM],
         out_specs=(VM,) * 7,
         scratch_shapes=[
             pltpu.VMEM((K, ROWS), F32),
@@ -469,16 +477,17 @@
         compiler_params=params(12),
         cost_estimate=cost(40),
         name="load",
-    )(parity, inv, hbm(modes), hbm(tiles), pin(w_out), pin(w_edge))
+    )(inv, hbm(modes), hbm(tiles), pin(w_out), pin(w_edge))
+    fe, fo, re = lax.optimization_barrier((fe, fo, re))
     fe, fo = exchange(fe, fo)
     e, z, se, so, wn = pl.pallas_call(
         edge2_kernel,
         out_shape=(f32(4), f32(2), sends(3 * K), sends(3 * K), weights(2)),
-        in_specs=[SM] + [VM] * 9,
+        in_specs=[VM] * 9,
         out_specs=(VM,) * 5,
         compiler_params=params(8),
         name="edge2",
-    )(parity, re, ro, pin(z), pin(o), pin(b), pin(w_in), pin(w_out), pin(m), pin(j))
+    )(re, ro, pin(z), pin(o), pin(b), pin(w_in), pin(w_out), pin(m), pin(j))
     state = (e, m, j)
     for later in (False, True):
         re, ro = exchange(se, so)
@@ -499,13 +508,13 @@
         )(*(pin(x) for x in state), pin(w_in), pin(w_out), pin(w_edge))
         m, b, o, t, c = outs[:5]
         shared = (
-            parity, re, ro, pin(z), pin(o), pin(b), pin(c), pin(w_in), pin(w_out), pin(wn), pin(w_edge), fe, fo
+            re, ro, pin(z), pin(o), pin(b), pin(c), pin(w_in), pin(w_out), pin(wn), pin(w_edge), fe, fo
         )
         if not later:
             e, p, z, se, so = pl.pallas_call(
                 functools.partial(edge3_kernel, False),
                 out_shape=(f32(6), f32(2), f32(2), sends(3 * K), sends(3 * K)),
-                in_specs=[SM] + [VM] * 12,
+                in_specs=[VM] * 12,
                 out_specs=(VM,) * 5,
                 compiler_params=params(8),
                 name="edge3",
@@ -514,7 +523,7 @@
     e, g = pl.pallas_call(
         functools.partial(edge3_kernel, True),
         out_shape=(f32(6), pltpu.VMEM((K // 2, 2 * K), F32)),
-        in_specs=[SM] + [VM] * 13,
+        in_specs=[VM] * 13,
         out_specs=(VM, VM),
         compiler_params=params(8),
         name="final",

time: 70.5 us -> 69.5 us (0.986)
  starting transfers between devices: 36.2 us -> 30.9 us
  waiting for transfers between devices: 12.5 us -> 17.5 us
    ppermute x4, waiting for transfers between devices: 3.14 us -> 9.26 us  [exchange(): ro = lax.ppermute(so, AXES, pairs_odd)]
    ppermute x10, starting transfers between devices: 13.3 us -> 11 us  [local(): lax.ppermute(g, AXES, [(i, i ^ bits) for i in range(count)])]
    ppermute x4, starting transfers between devices: 19.9 us -> 18 us  [exchange(): ro = lax.ppermute(so, AXES, pairs_odd)]
    ppermute x10, waiting for transfers between devices: 9.38 us -> 8.01 us  [local(): lax.ppermute(g, AXES, [(i, i ^ bits) for i in range(count)])]
    ppermute x4, starting transfers between devices: 3.01 us -> 2 us  [exchange(): re = lax.ppermute(se, AXES, pairs_even)]
  transfers between devices with their start and end apart: 18 -> 18, of which waited for: 9 -> 8; matrix products, arithmetic and copies ran while one was open for 0% -> 0% of each run, Pallas kernels for 16% -> 16%
where the time goes in v4:
time: 69.5 us; the launch traced here: 69.3 us
  starting transfers between devices  30.9 us (44%)
  Pallas kernels  20.6 us (30%)
  waiting for transfers between devices  17.5 us (25%)
    ppermute x4, starting transfers between devices, exchange(): ro = lax.ppermute(so, AXES, pairs_odd)  18 us
    ppermute x10, starting transfers between devices, local(): lax.ppermute(g, AXES, [(i, i ^ bits) for i in range(count)])  11 us
    ppermute x4, waiting for transfers between devices, exchange(): ro = lax.ppermute(so, AXES, pairs_odd)  9.26 us
    ppermute x10, waiting for transfers between devices, local(): lax.ppermute(g, AXES, [(i, i ^ bits) for i in range(count)])  8.01 us
    pallas_call x2, Pallas kernels, local(): pl.pallas_call(functools.partial(step_kernel, later, later), out_shape=(f...  5.04 us
    pallas_call x1, Pallas kernels, local(): pl.pallas_call(load_kernel, out_shape=(weights(18), f32(6), f32(4), f32(4...  4.77 us
    pallas_call x1, Pallas kernels, local(): pl.pallas_call(functools.partial(whiten_kernel, 1.0 / (ROWS * count)), ou...  3.4 us
    pallas_call x1, Pallas kernels, local(): pl.pallas_call(first_kernel, out_shape=(weights(4), weights(2), f32(2), s...  2.54 us
  transfers between devices with their start and end apart: 18, of which 8 were waited for; matrix products, arithmetic and copies ran while one was open for 0% of the time, Pallas kernels for 16%

profile of v4, /device:TPU:0, one launch (start us, length us, event | category | flops | bytes accessed | tf_op | source)
XLA Modules:
  0.0 69.3 jit_solution(17630183745794348364)
XLA Ops:
  0.0 2.5 %first.1 = (bf16[1536,384]{1,0:T(8,128)(2,1)S(1)}, bf16[768,384]{1,0:T(8,128)(2,1)S(1)}, f32[64,768]{1,0:T(8,128)S(1)}, bf16[512,384]{1,0:T(8,128)(2,1)S(1)}, bf...) custom-call(s32[1,2]{1,0:T(1,128)} %bound_ref.1, s32[24]{0:T(128)} %pair_ref.1, f32[64,3072]{1,0:T(8,128)} %modes_ref.3, ...), custom_call_target="tpu_custom_call" | custom-call | tf_op jit(solution)/shard_map/first/pallas_call | solution.py:447
  2.5 1.7 %collective-permute-start = (bf16[512,384]{1,0:T(8,128)(2,1)S(1)}, bf16[512,384]{1,0:T(8,128)(2,1)S(1)}, u32[]{:S(2)}, u32[]{:S(2)}) collective-permute-start(bf16[512,384]{1,0:T(8,128)(2,1)S(1)} %get-tuple-element.48), channel_id=1, source_target_pairs={{0,1},{1,0},{2,3},{3,2},{4,5},{5,4},{6,7},{7,6},{8,9},{9,8},{10,11... | collective-permute-start | bytes 1179656 | tf_op jit(solution)/shard_map/ppermute | solution.py:435
  4.3 7.0 %collective-permute-start.1 = (bf16[512,384]{1,0:T(8,128)(2,1)S(1)}, bf16[512,384]{1,0:T(8,128)(2,1)S(1)}, u32[]{:S(2)}, u32[]{:S(2)}) collective-permute-start(bf16[512,384]{1,0:T(8,128)(2,1)S(1)} %get-tuple-element.50), channel_id=1, source_target_pairs={{0,127},{1,2},{2,1},{3,4},{4,3},{5,6},{6,5},{7,8},{8,7},{9,10},{10... | collective-permute-start | bytes 1179656 | tf_op jit(solution)/shard_map/ppermute | solution.py:434
  11.3 4.8 %load.1 = (bf16[6912,384]{1,0:T(8,128)(2,1)S(1)}, f32[64,2304]{1,0:T(8,128)S(1)}, f32[64,1536]{1,0:T(8,128)S(1)}, f32[64,1536]{1,0:T(8,128)S(1)}, f32[64,768]{1,...) custom-call(s32[24]{0:T(128)S(4)} %get-tuple-element.43.inv_ref, f32[64,3072]{1,0:T(8,128)} %modes_ref.3, ...), custom_call_target="tpu_custom_call" | custom-call | flops 754974720 | bytes 8388608 | tf_op jit(solution)/shard_map/load/pallas_call | solution.py:465
  16.1 0.1 collective-permute-start.4
  16.2 5.1 %collective-permute-start.5 = (bf16[384,384]{1,0:T(8,128)(2,1)S(1)}, bf16[384,384]{1,0:T(8,128)(2,1)S(1)}, u32[]{:S(2)}, u32[]{:S(2)}) collective-permute-start(bf16[384,384]{1,0:T(8,128)(2,1)S(1)} %get-tuple-element.66), channel_id=1, source_target_pairs={{0,127},{1,2},{2,1},{3,4},{4,3},{5,6},{6,5},{7,8},{8,7},{9,10},{10... | collective-permute-start | bytes 884744 | tf_op jit(solution)/shard_map/ppermute | solution.py:434
  21.3 1.1 %edge2.1 = (f32[64,1536]{1,0:T(8,128)S(1)}, f32[64,768]{1,0:T(8,128)S(1)}, bf16[192,384]{1,0:T(8,128)(2,1)S(1)}, bf16[192,384]{1,0:T(8,128)(2,1)S(1)}, bf16[768,384]{1,0:T(8,128)(2,1)S(1)}) custom-call(bf16[512,384]{1,0:T(8,128)(2,1)S(1)} %collective-permute-done.re_ref, bf16[512,384]{1,0:T(8,128)(2,1)S(1)} %collective-permute-done.1.ro_ref, ...), custom_call_target="tpu_custom_call" | custom-call | tf_op jit(solution)/shard_map/edge2/pallas_call | solution.py:483
  22.4 0.1 collective-permute-start.2
  22.5 2.8 %collective-permute-start.3 = (bf16[192,384]{1,0:T(8,128)(2,1)S(1)}, bf16[192,384]{1,0:T(8,128)(2,1)S(1)}, u32[]{:S(2)}, u32[]{:S(2)}) collective-permute-start(bf16[192,384]{1,0:T(8,128)(2,1)S(1)} %get-tuple-element.58), channel_id=1, source_target_pairs={{0,127},{1,2},{2,1},{3,4},{4,3},{5,6},{6,5},{7,8},{8,7},{9,10},{10... | collective-permute-start | bytes 442376 | tf_op jit(solution)/shard_map/ppermute | solution.py:434
  25.4 2.3 %step.2 = (f32[64,1536]{1,0:T(8,128)S(1)}, f32[64,1536]{1,0:T(8,128)S(1)}, f32[64,768]{1,0:T(8,128)S(1)}, f32[64,768]{1,0:T(8,128)S(1)}, f32[64,1536]{1,0:T(8,128)S(1)}) custom-call(f32[64,1536]{1,0:T(8,128)S(1)} %get-tuple-element.60.refs_0_, f32[64,1536]{1,0:T(8,128)S(1)} %get-tuple-element.55.m_ref.refs_1_, ...), custom_call_target="tpu_custom_call" | custom-call | flops 981467136 | bytes 8388608 | tf_op jit(solution)/shard_map/step/pallas_call | solution.py:494
  27.7 0.2 collective-permute-done.2.re_ref
  27.9 4.7 %collective-permute-done.3.ro_ref = bf16[192,384]{1,0:T(8,128)(2,1)S(1)} collective-permute-done((bf16[192,384]{1,0:T(8,128)(2,1)S(1)}, bf16[192,384]{1,0:T(8,128)(2,1)S(1)}, u32[]{:S(2)}, u32[]{:S(2)}) %collective-permute-start.3) | collective-permute-done | bytes 147488 | tf_op jit(solution)/shard_map/ppermute | solution.py:434
  32.6 1.9 %edge3.1 = (f32[64,2304]{1,0:T(8,128)S(1)}, f32[64,768]{1,0:T(8,128)S(1)}, f32[64,768]{1,0:T(8,128)S(1)}, bf16[192,384]{1,0:T(8,128)(2,1)S(1)}, bf16[192,384]{1,0:T(8,128)(2,1)S(1)}) custom-call(bf16[192,384]{1,0:T(8,128)(2,1)S(1)} %collective-permute-done.2.re_ref, bf16[192,384]{1,0:T(8,128)(2,1)S(1)} %collective-permute-done.3.ro_ref, ...), custom_call_target="tpu_custom_call" | custom-call | tf_op jit(solution)/shard_map/edge3/pallas_call | solution.py:514
  34.5 0.1 collective-permute-start.6
  34.6 3.0 %collective-permute-start.7 = (bf16[192,384]{1,0:T(8,128)(2,1)S(1)}, bf16[192,384]{1,0:T(8,128)(2,1)S(1)}, u32[]{:S(2)}, u32[]{:S(2)}) collective-permute-start(bf16[192,384]{1,0:T(8,128)(2,1)S(1)} %get-tuple-element.68), channel_id=1, source_target_pairs={{0,127},{1,2},{2,1},{3,4},{4,3},{5,6},{6,5},{7,8},{8,7},{9,10},{10... | collective-permute-start | bytes 442376 | tf_op jit(solution)/shard_map/ppermute | solution.py:434
  37.6 2.7 %step.3 = (f32[64,1536]{1,0:T(8,128)}, f32[64,1536]{1,0:T(8,128)S(1)}, f32[64,768]{1,0:T(8,128)S(1)}, f32[64,768]{1,0:T(8,128)S(1)}, f32[64,1536]{1,0:T(8,128)S(1)}, /*index=5*/f32[64,64]{1,0:T(8,128)S(1)}) custom-call(f32[64,2304]{1,0:T(8,128)S(1)} %get-tuple-element.70.refs_0_, f32[64,768]{1,0:T(8,128)S(1)} %get-tuple-element.71.refs_1_, ...), custom_call_target="tpu_custom_call" | custom-call | flops 981467136 | bytes 8388608 | tf_op jit(solution)/shard_map/step/pallas_call | solution.py:494
  40.3 4.6 %collective-permute-done.7.ro_ref = bf16[192,384]{1,0:T(8,128)(2,1)S(1)} collective-permute-done((bf16[192,384]{1,0:T(8,128)(2,1)S(1)}, bf16[192,384]{1,0:T(8,128)(2,1)S(1)}, u32[]{:S(2)}, u32[]{:S(2)}) %collective-permute-start.7) | collective-permute-done | bytes 147488 | tf_op jit(solution)/shard_map/ppermute | solution.py:434
  44.9 1.8 %final.1 = (f32[64,2304]{1,0:T(8,128)S(1)}, f32[32,128]{1,0:T(8,128)S(1)}) custom-call(bf16[192,384]{1,0:T(8,128)(2,1)S(1)} %collective-permute-done.6.re_ref, bf16[192,384]{1,0:T(8,128)(2,1)S(1)} %collective-permute-done.7.ro_ref, f32[64,768]{1,0:T(8,128)S(1)} %get-tuple-element.69.z_ref, f32[64,768]{1,0:T(8,128)S(1)} %get-tuple-element.74.o_ref, ...), custom_call_target="tpu_custom_call" | custom-call | tf_op jit(solution)/shard_map/final/pallas_call | solution.py:523
  46.8 1.2 %collective-permute-done.8 = f32[32,128]{1,0:T(8,128)S(1)} collective-permute-done((f32[32,128]{1,0:T(8,128)S(1)}, f32[32,128]{1,0:T(8,128)S(1)}, u32[]{:S(2)}, u32[]{:S(2)}) %collective-permute-start.8) | collective-permute-done | bytes 16416 | tf_op jit(solution)/shard_map/ppermute | solution.py:532
  47.9 0.1 collective-permute-start.10
  48.0 3.4 %collective-permute-start.9 = (f32[32,128]{1,0:T(8,128)S(1)}, f32[32,128]{1,0:T(8,128)S(1)}, u32[]{:S(2)}, u32[]{:S(2)}) collective-permute-start(f32[32,128]{1,0:T(8,128)S(1)} %add.30), channel_id=1, source_target_pairs={{0,1},{1,0},{2,3},{3,2},{4,5},{5,4},{6,7},{7,6},{8,9},{9,8},{10,11... | collective-permute-start | bytes 49160 | tf_op jit(solution)/shard_map/ppermute | solution.py:532
  51.4 1.8 %collective-permute-done.11 = f32[32,128]{1,0:T(8,128)S(1)} collective-permute-done((f32[32,128]{1,0:T(8,128)S(1)}, f32[32,128]{1,0:T(8,128)S(1)}, u32[]{:S(2)}, u32[]{:S(2)}) %collective-permute-start.11) | collective-permute-done | bytes 16416 | tf_op jit(solution)/shard_map/ppermute | solution.py:532
  53.2 0.1 collective-permute-start.14
  53.3 0.7 %collective-permute-start.13 = (f32[32,128]{1,0:T(8,128)S(1)}, f32[32,128]{1,0:T(8,128)S(1)}, u32[]{:S(2)}, u32[]{:S(2)}) collective-permute-start(f32[32,128]{1,0:T(8,128)S(1)} %add_add_fusion.2), channel_id=1, source_target_pairs={{0,12},{1,13},{2,14},{3,15},{4,8},{5,9},{6,10},{7,11},{8,4},{9,5},... | collective-permute-start | bytes 49160 | tf_op jit(solution)/shard_map/ppermute | solution.py:532
  54.0 2.8 %collective-permute-start.12 = (f32[32,128]{1,0:T(8,128)S(1)}, f32[32,128]{1,0:T(8,128)S(1)}, u32[]{:S(2)}, u32[]{:S(2)}) collective-permute-start(f32[32,128]{1,0:T(8,128)S(1)} %add_add_fusion.2), channel_id=1, source_target_pairs={{0,4},{1,5},{2,6},{3,7},{4,0},{5,1},{6,2},{7,3},{8,12},{9,13},{10,... | collective-permute-start | bytes 49160 | tf_op jit(solution)/shard_map/ppermute | solution.py:532
  56.8 1.8 %collective-permute-done.14 = f32[32,128]{1,0:T(8,128)S(1)} collective-permute-done((f32[32,128]{1,0:T(8,128)S(1)}, f32[32,128]{1,0:T(8,128)S(1)}, u32[]{:S(2)}, u32[]{:S(2)}) %collective-permute-start.14) | collective-permute-done | bytes 16416 | tf_op jit(solution)/shard_map/ppermute | solution.py:532
  58.6 2.2 %collective-permute-start.17 = (f32[32,128]{1,0:T(8,128)S(1)}, f32[32,128]{1,0:T(8,128)S(1)}, u32[]{:S(2)}, u32[]{:S(2)}) collective-permute-start(f32[32,128]{1,0:T(8,128)S(1)} %add_add_fusion.1), channel_id=1, source_target_pairs={{0,64},{1,65},{2,66},{3,67},{4,68},{5,69},{6,70},{7,71},{8,72},{9,... | collective-permute-start | bytes 49160 | tf_op jit(solution)/shard_map/ppermute | solution.py:532
  60.8 1.2 %collective-permute-start.16 = (f32[32,128]{1,0:T(8,128)S(1)}, f32[32,128]{1,0:T(8,128)S(1)}, u32[]{:S(2)}, u32[]{:S(2)}) collective-permute-start(f32[32,128]{1,0:T(8,128)S(1)} %add_add_fusion.1), channel_id=1, source_target_pairs={{0,96},{1,97},{2,98},{3,99},{4,100},{5,101},{6,102},{7,103},{8,104... | collective-permute-start | bytes 49160 | tf_op jit(solution)/shard_map/ppermute | solution.py:532
  62.0 0.5 collective-permute-start.15
  62.5 1.4 %collective-permute-done.17 = f32[32,128]{1,0:T(8,128)S(1)} collective-permute-done((f32[32,128]{1,0:T(8,128)S(1)}, f32[32,128]{1,0:T(8,128)S(1)}, u32[]{:S(2)}, u32[]{:S(2)}) %collective-permute-start.17) | collective-permute-done | bytes 16416 | tf_op jit(solution)/shard_map/ppermute | solution.py:532
  63.9 1.9 %collective-permute-done.16 = f32[32,128]{1,0:T(8,128)S(1)} collective-permute-done((f32[32,128]{1,0:T(8,128)S(1)}, f32[32,128]{1,0:T(8,128)S(1)}, u32[]{:S(2)}, u32[]{:S(2)}) %collective-permute-start.16) | collective-permute-done | bytes 16416 | tf_op jit(solution)/shard_map/ppermute | solution.py:532
  65.8 3.4 %whiten.1 = f32[64,3072]{1,0:T(8,128)} custom-call(f32[32,128]{1,0:T(8,128)S(1)} %add_add_fusion.g_ref, f32[64,2304]{1,0:T(8,128)S(1)} %get-tuple-element.79.e_ref, f32[64,768]{1,0:T(8,128)S(1)} %get-tuple-element.80.i_ref), custom_call_target="tpu_custom_call" | custom-call | tf_op jit(solution)/shard_map/whiten/pallas_call | solution.py:535
  (16 shorter events, 0.1 us)
Async XLA Ops:
  2.5 13.5 %collective-permute-start = (bf16[512,384]{1,0:T(8,128)(2,1)S(1)}, bf16[512,384]{1,0:T(8,128)(2,1)S(1)}, u32[]{:S(2)}, u32[]{:S(2)}) collective-permute-start(bf16[512,384]{1,0:T(8,128)(2,1)S(1)} %get-tuple-element.48), channel_id=1, source_target_pairs={{0,1},{1,0},{2,3},{3,2},{4,5},{5,4},{6,7},{7,6},{8,9},{9,8},{10,11... | collective-permute-start | bytes 1179656 | tf_op jit(solution)/shard_map/ppermute | solution.py:435
  4.3 17.0 %collective-permute-start.1 = (bf16[512,384]{1,0:T(8,128)(2,1)S(1)}, bf16[512,384]{1,0:T(8,128)(2,1)S(1)}, u32[]{:S(2)}, u32[]{:S(2)}) collective-permute-start(bf16[512,384]{1,0:T(8,128)(2,1)S(1)} %get-tuple-element.50), channel_id=1, source_target_pairs={{0,127},{1,2},{2,1},{3,4},{4,3},{5,6},{6,5},{7,8},{8,7},{9,10},{10... | collective-permute-start | bytes 1179656 | tf_op jit(solution)/shard_map/ppermute | solution.py:434
  16.1 16.5 %collective-permute-start.4 = (bf16[384,384]{1,0:T(8,128)(2,1)S(1)}, bf16[384,384]{1,0:T(8,128)(2,1)S(1)}, u32[]{:S(2)}, u32[]{:S(2)}) collective-permute-start(bf16[384,384]{1,0:T(8,128)(2,1)S(1)} %get-tuple-element.65), channel_id=1, source_target_pairs={{0,1},{1,0},{2,3},{3,2},{4,5},{5,4},{6,7},{7,6},{8,9},{9,8},{10,11... | collective-permute-start | bytes 884744 | tf_op jit(solution)/shard_map/ppermute | solution.py:435
  16.2 16.4 %collective-permute-start.5 = (bf16[384,384]{1,0:T(8,128)(2,1)S(1)}, bf16[384,384]{1,0:T(8,128)(2,1)S(1)}, u32[]{:S(2)}, u32[]{:S(2)}) collective-permute-start(bf16[384,384]{1,0:T(8,128)(2,1)S(1)} %get-tuple-element.66), channel_id=1, source_target_pairs={{0,127},{1,2},{2,1},{3,4},{4,3},{5,6},{6,5},{7,8},{8,7},{9,10},{10... | collective-permute-start | bytes 884744 | tf_op jit(solution)/shard_map/ppermute | solution.py:434
  22.4 5.5 %collective-permute-start.2 = (bf16[192,384]{1,0:T(8,128)(2,1)S(1)}, bf16[192,384]{1,0:T(8,128)(2,1)S(1)}, u32[]{:S(2)}, u32[]{:S(2)}) collective-permute-start(bf16[192,384]{1,0:T(8,128)(2,1)S(1)} %get-tuple-element.57), channel_id=1, source_target_pairs={{0,1},{1,0},{2,3},{3,2},{4,5},{5,4},{6,7},{7,6},{8,9},{9,8},{10,11... | collective-permute-start | bytes 442376 | tf_op jit(solution)/shard_map/ppermute | solution.py:435
  22.5 10.1 %collective-permute-start.3 = (bf16[192,384]{1,0:T(8,128)(2,1)S(1)}, bf16[192,384]{1,0:T(8,128)(2,1)S(1)}, u32[]{:S(2)}, u32[]{:S(2)}) collective-permute-start(bf16[192,384]{1,0:T(8,128)(2,1)S(1)} %get-tuple-element.58), channel_id=1, source_target_pairs={{0,127},{1,2},{2,1},{3,4},{4,3},{5,6},{6,5},{7,8},{8,7},{9,10},{10... | collective-permute-start | bytes 442376 | tf_op jit(solution)/shard_map/ppermute | solution.py:434
  34.5 5.8 %collective-permute-start.6 = (bf16[192,384]{1,0:T(8,128)(2,1)S(1)}, bf16[192,384]{1,0:T(8,128)(2,1)S(1)}, u32[]{:S(2)}, u32[]{:S(2)}) collective-permute-start(bf16[192,384]{1,0:T(8,128)(2,1)S(1)} %get-tuple-element.67), channel_id=1, source_target_pairs={{0,1},{1,0},{2,3},{3,2},{4,5},{5,4},{6,7},{7,6},{8,9},{9,8},{10,11... | collective-permute-start | bytes 442376 | tf_op jit(solution)/shard_map/ppermute | solution.py:435
  34.6 10.3 %collective-permute-start.7 = (bf16[192,384]{1,0:T(8,128)(2,1)S(1)}, bf16[192,384]{1,0:T(8,128)(2,1)S(1)}, u32[]{:S(2)}, u32[]{:S(2)}) collective-permute-start(bf16[192,384]{1,0:T(8,128)(2,1)S(1)} %get-tuple-element.68), channel_id=1, source_target_pairs={{0,127},{1,2},{2,1},{3,4},{4,3},{5,6},{6,5},{7,8},{8,7},{9,10},{10... | collective-permute-start | bytes 442376 | tf_op jit(solution)/shard_map/ppermute | solution.py:434
  46.7 1.2 %collective-permute-start.8 = (f32[32,128]{1,0:T(8,128)S(1)}, f32[32,128]{1,0:T(8,128)S(1)}, u32[]{:S(2)}, u32[]{:S(2)}) collective-permute-start(f32[32,128]{1,0:T(8,128)S(1)} %get-tuple-element.78), channel_id=1, source_target_pairs={{0,16},{1,17},{2,18},{3,19},{4,20},{5,21},{6,22},{7,23},{8,24},{9,... | collective-permute-start | bytes 49160 | tf_op jit(solution)/shard_map/ppermute | solution.py:532
  47.9 5.3 %collective-permute-start.11 = (f32[32,128]{1,0:T(8,128)S(1)}, f32[32,128]{1,0:T(8,128)S(1)}, u32[]{:S(2)}, u32[]{:S(2)}) collective-permute-start(f32[32,128]{1,0:T(8,128)S(1)} %add.30), channel_id=1, source_target_pairs={{0,2},{1,3},{2,0},{3,1},{4,6},{5,7},{6,4},{7,5},{8,10},{9,11},{10,... | collective-permute-start | bytes 49160 | tf_op jit(solution)/shard_map/ppermute | solution.py:532
  47.9 5.3 %collective-permute-start.10 = (f32[32,128]{1,0:T(8,128)S(1)}, f32[32,128]{1,0:T(8,128)S(1)}, u32[]{:S(2)}, u32[]{:S(2)}) collective-permute-start(f32[32,128]{1,0:T(8,128)S(1)} %add.30), channel_id=1, source_target_pairs={{0,3},{1,2},{2,1},{3,0},{4,7},{5,6},{6,5},{7,4},{8,11},{9,10},{10,... | collective-permute-start | bytes 49160 | tf_op jit(solution)/shard_map/ppermute | solution.py:532
  48.0 5.2 %collective-permute-start.9 = (f32[32,128]{1,0:T(8,128)S(1)}, f32[32,128]{1,0:T(8,128)S(1)}, u32[]{:S(2)}, u32[]{:S(2)}) collective-permute-start(f32[32,128]{1,0:T(8,128)S(1)} %add.30), channel_id=1, source_target_pairs={{0,1},{1,0},{2,3},{3,2},{4,5},{5,4},{6,7},{7,6},{8,9},{9,8},{10,11... | collective-permute-start | bytes 49160 | tf_op jit(solution)/shard_map/ppermute | solution.py:532
  53.2 5.3 %collective-permute-start.14 = (f32[32,128]{1,0:T(8,128)S(1)}, f32[32,128]{1,0:T(8,128)S(1)}, u32[]{:S(2)}, u32[]{:S(2)}) collective-permute-start(f32[32,128]{1,0:T(8,128)S(1)} %add_add_fusion.2), channel_id=1, source_target_pairs={{0,8},{1,9},{2,10},{3,11},{4,12},{5,13},{6,14},{7,15},{8,0},{9,1},... | collective-permute-start | bytes 49160 | tf_op jit(solution)/shard_map/ppermute | solution.py:532
  53.3 5.2 %collective-permute-start.13 = (f32[32,128]{1,0:T(8,128)S(1)}, f32[32,128]{1,0:T(8,128)S(1)}, u32[]{:S(2)}, u32[]{:S(2)}) collective-permute-start(f32[32,128]{1,0:T(8,128)S(1)} %add_add_fusion.2), channel_id=1, source_target_pairs={{0,12},{1,13},{2,14},{3,15},{4,8},{5,9},{6,10},{7,11},{8,4},{9,5},... | collective-permute-start | bytes 49160 | tf_op jit(solution)/shard_map/ppermute | solution.py:532
  54.0 4.5 %collective-permute-start.12 = (f32[32,128]{1,0:T(8,128)S(1)}, f32[32,128]{1,0:T(8,128)S(1)}, u32[]{:S(2)}, u32[]{:S(2)}) collective-permute-start(f32[32,128]{1,0:T(8,128)S(1)} %add_add_fusion.2), channel_id=1, source_target_pairs={{0,4},{1,5},{2,6},{3,7},{4,0},{5,1},{6,2},{7,3},{8,12},{9,13},{10,... | collective-permute-start | bytes 49160 | tf_op jit(solution)/shard_map/ppermute | solution.py:532
  58.6 5.3 %collective-permute-start.17 = (f32[32,128]{1,0:T(8,128)S(1)}, f32[32,128]{1,0:T(8,128)S(1)}, u32[]{:S(2)}, u32[]{:S(2)}) collective-permute-start(f32[32,128]{1,0:T(8,128)S(1)} %add_add_fusion.1), channel_id=1, source_target_pairs={{0,64},{1,65},{2,66},{3,67},{4,68},{5,69},{6,70},{7,71},{8,72},{9,... | collective-permute-start | bytes 49160 | tf_op jit(solution)/shard_map/ppermute | solution.py:532
  60.8 4.9 %collective-permute-start.16 = (f32[32,128]{1,0:T(8,128)S(1)}, f32[32,128]{1,0:T(8,128)S(1)}, u32[]{:S(2)}, u32[]{:S(2)}) collective-permute-start(f32[32,128]{1,0:T(8,128)S(1)} %add_add_fusion.1), channel_id=1, source_target_pairs={{0,96},{1,97},{2,98},{3,99},{4,100},{5,101},{6,102},{7,103},{8,104... | collective-permute-start | bytes 49160 | tf_op jit(solution)/shard_map/ppermute | solution.py:532
  62.0 3.8 %collective-permute-start.15 = (f32[32,128]{1,0:T(8,128)S(1)}, f32[32,128]{1,0:T(8,128)S(1)}, u32[]{:S(2)}, u32[]{:S(2)}) collective-permute-start(f32[32,128]{1,0:T(8,128)S(1)} %add_add_fusion.1), channel_id=1, source_target_pairs={{0,32},{1,33},{2,34},{3,35},{4,36},{5,37},{6,38},{7,39},{8,40},{9,... | collective-permute-start | bytes 49160 | tf_op jit(solution)/shard_map/ppermute | solution.py:532

commit v5 on v4

--- a/solution.py
+++ b/solution.py
@@ -478,7 +478,7 @@
         cost_estimate=cost(40),
         name="load",
     )(inv, hbm(modes), hbm(tiles), pin(w_out), pin(w_edge))
-    fe, fo, re = lax.optimization_barrier((fe, fo, re))
+    fo, re = lax.optimization_barrier((fo, re))
     fe, fo = exchange(fe, fo)
     e, z, se, so, wn = pl.pallas_call(
         edge2_kernel,

time: 69.5 us -> 69.3 us (level)
  waiting for transfers between devices: 17.5 us -> 16.3 us
  starting transfers between devices: 30.9 us -> 31.9 us
    ppermute x4, waiting for transfers between devices: 9.26 us -> 8.02 us  [exchange(): ro = lax.ppermute(so, AXES, pairs_odd)]
  transfers between devices with their start and end apart: 18 -> 18, of which waited for: 8 -> 9; matrix products, arithmetic and copies ran while one was open for 0% -> 0% of each run, Pallas kernels for 16% -> 16%
where the time goes in v5:
time: 69.3 us; the launch traced here: 69.1 us
  starting transfers between devices  31.9 us (46%)
  Pallas kernels  20.6 us (30%)
  waiting for transfers between devices  16.3 us (24%)
    ppermute x4, starting transfers between devices, exchange(): ro = lax.ppermute(so, AXES, pairs_odd)  18.4 us
    ppermute x10, starting transfers between devices, local(): lax.ppermute(g, AXES, [(i, i ^ bits) for i in range(count)])  11.5 us
    ppermute x4, waiting for transfers between devices, exchange(): ro = lax.ppermute(so, AXES, pairs_odd)  8.02 us
    ppermute x10, waiting for transfers between devices, local(): lax.ppermute(g, AXES, [(i, i ^ bits) for i in range(count)])  7.7 us
    pallas_call x2, Pallas kernels, local(): pl.pallas_call(functools.partial(step_kernel, later, later), out_shape=(f...  5.04 us
    pallas_call x1, Pallas kernels, local(): pl.pallas_call(load_kernel, out_shape=(weights(18), f32(6), f32(4), f32(4...  4.77 us
    pallas_call x1, Pallas kernels, local(): pl.pallas_call(functools.partial(whiten_kernel, 1.0 / (ROWS * count)), ou...  3.4 us
    pallas_call x1, Pallas kernels, local(): pl.pallas_call(first_kernel, out_shape=(weights(4), weights(2), f32(2), s...  2.54 us
  transfers between devices with their start and end apart: 18, of which 9 were waited for; matrix products, arithmetic and copies ran while one was open for 0% of the time, Pallas kernels for 16%

profile of v5, /device:TPU:0, one launch (start us, length us, event | category | flops | bytes accessed | tf_op | source)
XLA Modules:
  0.0 69.1 jit_solution(3092477259181207211)
XLA Ops:
  0.0 2.5 %first.1 = (bf16[1536,384]{1,0:T(8,128)(2,1)S(1)}, bf16[768,384]{1,0:T(8,128)(2,1)S(1)}, f32[64,768]{1,0:T(8,128)S(1)}, bf16[512,384]{1,0:T(8,128)(2,1)S(1)}, bf...) custom-call(s32[1,2]{1,0:T(1,128)} %bound_ref.1, s32[24]{0:T(128)} %pair_ref.1, f32[64,3072]{1,0:T(8,128)} %modes_ref.3, ...), custom_call_target="tpu_custom_call" | custom-call | tf_op jit(solution)/shard_map/first/pallas_call | solution.py:447
  2.5 1.7 %collective-permute-start = (bf16[512,384]{1,0:T(8,128)(2,1)S(1)}, bf16[512,384]{1,0:T(8,128)(2,1)S(1)}, u32[]{:S(2)}, u32[]{:S(2)}) collective-permute-start(bf16[512,384]{1,0:T(8,128)(2,1)S(1)} %get-tuple-element.46), channel_id=1, source_target_pairs={{0,1},{1,0},{2,3},{3,2},{4,5},{5,4},{6,7},{7,6},{8,9},{9,8},{10,11... | collective-permute-start | bytes 1179656 | tf_op jit(solution)/shard_map/ppermute | solution.py:435
  4.3 7.0 %collective-permute-start.1 = (bf16[512,384]{1,0:T(8,128)(2,1)S(1)}, bf16[512,384]{1,0:T(8,128)(2,1)S(1)}, u32[]{:S(2)}, u32[]{:S(2)}) collective-permute-start(bf16[512,384]{1,0:T(8,128)(2,1)S(1)} %get-tuple-element.48), channel_id=1, source_target_pairs={{0,127},{1,2},{2,1},{3,4},{4,3},{5,6},{6,5},{7,8},{8,7},{9,10},{10... | collective-permute-start | bytes 1179656 | tf_op jit(solution)/shard_map/ppermute | solution.py:434
  11.3 4.8 %load.1 = (bf16[6912,384]{1,0:T(8,128)(2,1)S(1)}, f32[64,2304]{1,0:T(8,128)S(1)}, f32[64,1536]{1,0:T(8,128)S(1)}, f32[64,1536]{1,0:T(8,128)S(1)}, f32[64,768]{1,...) custom-call(s32[24]{0:T(128)S(4)} %get-tuple-element.42.inv_ref, f32[64,3072]{1,0:T(8,128)} %modes_ref.3, ...), custom_call_target="tpu_custom_call" | custom-call | flops 754974720 | bytes 8388608 | tf_op jit(solution)/shard_map/load/pallas_call | solution.py:465
  16.1 0.1 collective-permute-start.4
  16.2 4.6 %collective-permute-start.5 = (bf16[384,384]{1,0:T(8,128)(2,1)S(1)}, bf16[384,384]{1,0:T(8,128)(2,1)S(1)}, u32[]{:S(2)}, u32[]{:S(2)}) collective-permute-start(bf16[384,384]{1,0:T(8,128)(2,1)S(1)} %get-tuple-element.64), channel_id=1, source_target_pairs={{0,127},{1,2},{2,1},{3,4},{4,3},{5,6},{6,5},{7,8},{8,7},{9,10},{10... | collective-permute-start | bytes 884744 | tf_op jit(solution)/shard_map/ppermute | solution.py:434
  20.8 1.1 %edge2.1 = (f32[64,1536]{1,0:T(8,128)S(1)}, f32[64,768]{1,0:T(8,128)S(1)}, bf16[192,384]{1,0:T(8,128)(2,1)S(1)}, bf16[192,384]{1,0:T(8,128)(2,1)S(1)}, bf16[768,384]{1,0:T(8,128)(2,1)S(1)}) custom-call(bf16[512,384]{1,0:T(8,128)(2,1)S(1)} %collective-permute-done.re_ref, bf16[512,384]{1,0:T(8,128)(2,1)S(1)} %collective-permute-done.1.ro_ref, ...), custom_call_target="tpu_custom_call" | custom-call | tf_op jit(solution)/shard_map/edge2/pallas_call | solution.py:483
  22.0 0.1 collective-permute-start.2
  22.1 3.3 %collective-permute-start.3 = (bf16[192,384]{1,0:T(8,128)(2,1)S(1)}, bf16[192,384]{1,0:T(8,128)(2,1)S(1)}, u32[]{:S(2)}, u32[]{:S(2)}) collective-permute-start(bf16[192,384]{1,0:T(8,128)(2,1)S(1)} %get-tuple-element.56), channel_id=1, source_target_pairs={{0,127},{1,2},{2,1},{3,4},{4,3},{5,6},{6,5},{7,8},{8,7},{9,10},{10... | collective-permute-start | bytes 442376 | tf_op jit(solution)/shard_map/ppermute | solution.py:434
  25.4 2.3 %step.2 = (f32[64,1536]{1,0:T(8,128)S(1)}, f32[64,1536]{1,0:T(8,128)S(1)}, f32[64,768]{1,0:T(8,128)S(1)}, f32[64,768]{1,0:T(8,128)S(1)}, f32[64,1536]{1,0:T(8,128)S(1)}) custom-call(f32[64,1536]{1,0:T(8,128)S(1)} %get-tuple-element.58.refs_0_, f32[64,1536]{1,0:T(8,128)S(1)} %get-tuple-element.53.m_ref.refs_1_, ...), custom_call_target="tpu_custom_call" | custom-call | flops 981467136 | bytes 8388608 | tf_op jit(solution)/shard_map/step/pallas_call | solution.py:494
  27.7 0.6 collective-permute-done.2.re_ref
  28.3 3.9 %collective-permute-done.3.ro_ref = bf16[192,384]{1,0:T(8,128)(2,1)S(1)} collective-permute-done((bf16[192,384]{1,0:T(8,128)(2,1)S(1)}, bf16[192,384]{1,0:T(8,128)(2,1)S(1)}, u32[]{:S(2)}, u32[]{:S(2)}) %collective-permute-start.3) | collective-permute-done | bytes 147488 | tf_op jit(solution)/shard_map/ppermute | solution.py:434
  32.2 1.9 %edge3.1 = (f32[64,2304]{1,0:T(8,128)S(1)}, f32[64,768]{1,0:T(8,128)S(1)}, f32[64,768]{1,0:T(8,128)S(1)}, bf16[192,384]{1,0:T(8,128)(2,1)S(1)}, bf16[192,384]{1,0:T(8,128)(2,1)S(1)}) custom-call(bf16[192,384]{1,0:T(8,128)(2,1)S(1)} %collective-permute-done.2.re_ref, bf16[192,384]{1,0:T(8,128)(2,1)S(1)} %collective-permute-done.3.ro_ref, ...), custom_call_target="tpu_custom_call" | custom-call | tf_op jit(solution)/shard_map/edge3/pallas_call | solution.py:514
  34.2 3.5 %collective-permute-start.7 = (bf16[192,384]{1,0:T(8,128)(2,1)S(1)}, bf16[192,384]{1,0:T(8,128)(2,1)S(1)}, u32[]{:S(2)}, u32[]{:S(2)}) collective-permute-start(bf16[192,384]{1,0:T(8,128)(2,1)S(1)} %get-tuple-element.66), channel_id=1, source_target_pairs={{0,127},{1,2},{2,1},{3,4},{4,3},{5,6},{6,5},{7,8},{8,7},{9,10},{10... | collective-permute-start | bytes 442376 | tf_op jit(solution)/shard_map/ppermute | solution.py:434
  37.7 2.7 %step.3 = (f32[64,1536]{1,0:T(8,128)}, f32[64,1536]{1,0:T(8,128)S(1)}, f32[64,768]{1,0:T(8,128)S(1)}, f32[64,768]{1,0:T(8,128)S(1)}, f32[64,1536]{1,0:T(8,128)S(1)}, /*index=5*/f32[64,64]{1,0:T(8,128)S(1)}) custom-call(f32[64,2304]{1,0:T(8,128)S(1)} %get-tuple-element.68.refs_0_, f32[64,768]{1,0:T(8,128)S(1)} %get-tuple-element.69.refs_1_, ...), custom_call_target="tpu_custom_call" | custom-call | flops 981467136 | bytes 8388608 | tf_op jit(solution)/shard_map/step/pallas_call | solution.py:494
  40.4 4.1 %collective-permute-done.7.ro_ref = bf16[192,384]{1,0:T(8,128)(2,1)S(1)} collective-permute-done((bf16[192,384]{1,0:T(8,128)(2,1)S(1)}, bf16[192,384]{1,0:T(8,128)(2,1)S(1)}, u32[]{:S(2)}, u32[]{:S(2)}) %collective-permute-start.7) | collective-permute-done | bytes 147488 | tf_op jit(solution)/shard_map/ppermute | solution.py:434
  44.5 1.8 %final.1 = (f32[64,2304]{1,0:T(8,128)S(1)}, f32[32,128]{1,0:T(8,128)S(1)}) custom-call(bf16[192,384]{1,0:T(8,128)(2,1)S(1)} %collective-permute-done.6.re_ref, bf16[192,384]{1,0:T(8,128)(2,1)S(1)} %collective-permute-done.7.ro_ref, f32[64,768]{1,0:T(8,128)S(1)} %get-tuple-element.67.z_ref, f32[64,768]{1,0:T(8,128)S(1)} %get-tuple-element.72.o_ref, ...), custom_call_target="tpu_custom_call" | custom-call | tf_op jit(solution)/shard_map/final/pallas_call | solution.py:523
  46.4 1.2 %collective-permute-done.8 = f32[32,128]{1,0:T(8,128)S(1)} collective-permute-done((f32[32,128]{1,0:T(8,128)S(1)}, f32[32,128]{1,0:T(8,128)S(1)}, u32[]{:S(2)}, u32[]{:S(2)}) %collective-permute-start.8) | collective-permute-done | bytes 16416 | tf_op jit(solution)/shard_map/ppermute | solution.py:532
  47.6 0.1 collective-permute-start.10
  47.7 3.4 %collective-permute-start.9 = (f32[32,128]{1,0:T(8,128)S(1)}, f32[32,128]{1,0:T(8,128)S(1)}, u32[]{:S(2)}, u32[]{:S(2)}) collective-permute-start(f32[32,128]{1,0:T(8,128)S(1)} %add.30), channel_id=1, source_target_pairs={{0,1},{1,0},{2,3},{3,2},{4,5},{5,4},{6,7},{7,6},{8,9},{9,8},{10,11... | collective-permute-start | bytes 49160 | tf_op jit(solution)/shard_map/ppermute | solution.py:532
  51.1 1.8 %collective-permute-done.11 = f32[32,128]{1,0:T(8,128)S(1)} collective-permute-done((f32[32,128]{1,0:T(8,128)S(1)}, f32[32,128]{1,0:T(8,128)S(1)}, u32[]{:S(2)}, u32[]{:S(2)}) %collective-permute-start.11) | collective-permute-done | bytes 16416 | tf_op jit(solution)/shard_map/ppermute | solution.py:532
  52.9 0.1 collective-permute-start.14
  53.0 0.6 collective-permute-start.13
  53.6 2.9 %collective-permute-start.12 = (f32[32,128]{1,0:T(8,128)S(1)}, f32[32,128]{1,0:T(8,128)S(1)}, u32[]{:S(2)}, u32[]{:S(2)}) collective-permute-start(f32[32,128]{1,0:T(8,128)S(1)} %add_add_fusion.2), channel_id=1, source_target_pairs={{0,4},{1,5},{2,6},{3,7},{4,0},{5,1},{6,2},{7,3},{8,12},{9,13},{10,... | collective-permute-start | bytes 49160 | tf_op jit(solution)/shard_map/ppermute | solution.py:532
  56.4 1.8 %collective-permute-done.14 = f32[32,128]{1,0:T(8,128)S(1)} collective-permute-done((f32[32,128]{1,0:T(8,128)S(1)}, f32[32,128]{1,0:T(8,128)S(1)}, u32[]{:S(2)}, u32[]{:S(2)}) %collective-permute-start.14) | collective-permute-done | bytes 16416 | tf_op jit(solution)/shard_map/ppermute | solution.py:532
  58.2 2.1 %collective-permute-start.17 = (f32[32,128]{1,0:T(8,128)S(1)}, f32[32,128]{1,0:T(8,128)S(1)}, u32[]{:S(2)}, u32[]{:S(2)}) collective-permute-start(f32[32,128]{1,0:T(8,128)S(1)} %add_add_fusion.1), channel_id=1, source_target_pairs={{0,64},{1,65},{2,66},{3,67},{4,68},{5,69},{6,70},{7,71},{8,72},{9,... | collective-permute-start | bytes 49160 | tf_op jit(solution)/shard_map/ppermute | solution.py:532
  60.3 1.5 %collective-permute-start.16 = (f32[32,128]{1,0:T(8,128)S(1)}, f32[32,128]{1,0:T(8,128)S(1)}, u32[]{:S(2)}, u32[]{:S(2)}) collective-permute-start(f32[32,128]{1,0:T(8,128)S(1)} %add_add_fusion.1), channel_id=1, source_target_pairs={{0,96},{1,97},{2,98},{3,99},{4,100},{5,101},{6,102},{7,103},{8,104... | collective-permute-start | bytes 49160 | tf_op jit(solution)/shard_map/ppermute | solution.py:532
  61.8 0.8 %collective-permute-start.15 = (f32[32,128]{1,0:T(8,128)S(1)}, f32[32,128]{1,0:T(8,128)S(1)}, u32[]{:S(2)}, u32[]{:S(2)}) collective-permute-start(f32[32,128]{1,0:T(8,128)S(1)} %add_add_fusion.1), channel_id=1, source_target_pairs={{0,32},{1,33},{2,34},{3,35},{4,36},{5,37},{6,38},{7,39},{8,40},{9,... | collective-permute-start | bytes 49160 | tf_op jit(solution)/shard_map/ppermute | solution.py:532
  62.6 0.9 %collective-permute-done.17 = f32[32,128]{1,0:T(8,128)S(1)} collective-permute-done((f32[32,128]{1,0:T(8,128)S(1)}, f32[32,128]{1,0:T(8,128)S(1)}, u32[]{:S(2)}, u32[]{:S(2)}) %collective-permute-start.17) | collective-permute-done | bytes 16416 | tf_op jit(solution)/shard_map/ppermute | solution.py:532
  63.5 1.8 %collective-permute-done.16 = f32[32,128]{1,0:T(8,128)S(1)} collective-permute-done((f32[32,128]{1,0:T(8,128)S(1)}, f32[32,128]{1,0:T(8,128)S(1)}, u32[]{:S(2)}, u32[]{:S(2)}) %collective-permute-start.16) | collective-permute-done | bytes 16416 | tf_op jit(solution)/shard_map/ppermute | solution.py:532
  65.3 0.3 collective-permute-done.15
  65.6 3.4 %whiten.1 = f32[64,3072]{1,0:T(8,128)} custom-call(f32[32,128]{1,0:T(8,128)S(1)} %add_add_fusion.g_ref, f32[64,2304]{1,0:T(8,128)S(1)} %get-tuple-element.77.e_ref, f32[64,768]{1,0:T(8,128)S(1)} %get-tuple-element.78.i_ref), custom_call_target="tpu_custom_call" | custom-call | tf_op jit(solution)/shard_map/whiten/pallas_call | solution.py:535
  (16 shorter events, 0.2 us)
Async XLA Ops:
  2.5 13.6 %collective-permute-start = (bf16[512,384]{1,0:T(8,128)(2,1)S(1)}, bf16[512,384]{1,0:T(8,128)(2,1)S(1)}, u32[]{:S(2)}, u32[]{:S(2)}) collective-permute-start(bf16[512,384]{1,0:T(8,128)(2,1)S(1)} %get-tuple-element.46), channel_id=1, source_target_pairs={{0,1},{1,0},{2,3},{3,2},{4,5},{5,4},{6,7},{7,6},{8,9},{9,8},{10,11... | collective-permute-start | bytes 1179656 | tf_op jit(solution)/shard_map/ppermute | solution.py:435
  4.3 16.5 %collective-permute-start.1 = (bf16[512,384]{1,0:T(8,128)(2,1)S(1)}, bf16[512,384]{1,0:T(8,128)(2,1)S(1)}, u32[]{:S(2)}, u32[]{:S(2)}) collective-permute-start(bf16[512,384]{1,0:T(8,128)(2,1)S(1)} %get-tuple-element.48), channel_id=1, source_target_pairs={{0,127},{1,2},{2,1},{3,4},{4,3},{5,6},{6,5},{7,8},{8,7},{9,10},{10... | collective-permute-start | bytes 1179656 | tf_op jit(solution)/shard_map/ppermute | solution.py:434
  16.1 11.6 %collective-permute-start.4 = (bf16[384,384]{1,0:T(8,128)(2,1)S(1)}, bf16[384,384]{1,0:T(8,128)(2,1)S(1)}, u32[]{:S(2)}, u32[]{:S(2)}) collective-permute-start(bf16[384,384]{1,0:T(8,128)(2,1)S(1)} %get-tuple-element.63), channel_id=1, source_target_pairs={{0,1},{1,0},{2,3},{3,2},{4,5},{5,4},{6,7},{7,6},{8,9},{9,8},{10,11... | collective-permute-start | bytes 884744 | tf_op jit(solution)/shard_map/ppermute | solution.py:435
  16.2 16.1 %collective-permute-start.5 = (bf16[384,384]{1,0:T(8,128)(2,1)S(1)}, bf16[384,384]{1,0:T(8,128)(2,1)S(1)}, u32[]{:S(2)}, u32[]{:S(2)}) collective-permute-start(bf16[384,384]{1,0:T(8,128)(2,1)S(1)} %get-tuple-element.64), channel_id=1, source_target_pairs={{0,127},{1,2},{2,1},{3,4},{4,3},{5,6},{6,5},{7,8},{8,7},{9,10},{10... | collective-permute-start | bytes 884744 | tf_op jit(solution)/shard_map/ppermute | solution.py:434
  22.0 6.3 %collective-permute-start.2 = (bf16[192,384]{1,0:T(8,128)(2,1)S(1)}, bf16[192,384]{1,0:T(8,128)(2,1)S(1)}, u32[]{:S(2)}, u32[]{:S(2)}) collective-permute-start(bf16[192,384]{1,0:T(8,128)(2,1)S(1)} %get-tuple-element.55), channel_id=1, source_target_pairs={{0,1},{1,0},{2,3},{3,2},{4,5},{5,4},{6,7},{7,6},{8,9},{9,8},{10,11... | collective-permute-start | bytes 442376 | tf_op jit(solution)/shard_map/ppermute | solution.py:435
  22.1 10.2 %collective-permute-start.3 = (bf16[192,384]{1,0:T(8,128)(2,1)S(1)}, bf16[192,384]{1,0:T(8,128)(2,1)S(1)}, u32[]{:S(2)}, u32[]{:S(2)}) collective-permute-start(bf16[192,384]{1,0:T(8,128)(2,1)S(1)} %get-tuple-element.56), channel_id=1, source_target_pairs={{0,127},{1,2},{2,1},{3,4},{4,3},{5,6},{6,5},{7,8},{8,7},{9,10},{10... | collective-permute-start | bytes 442376 | tf_op jit(solution)/shard_map/ppermute | solution.py:434
  34.1 6.3 %collective-permute-start.6 = (bf16[192,384]{1,0:T(8,128)(2,1)S(1)}, bf16[192,384]{1,0:T(8,128)(2,1)S(1)}, u32[]{:S(2)}, u32[]{:S(2)}) collective-permute-start(bf16[192,384]{1,0:T(8,128)(2,1)S(1)} %get-tuple-element.65), channel_id=1, source_target_pairs={{0,1},{1,0},{2,3},{3,2},{4,5},{5,4},{6,7},{7,6},{8,9},{9,8},{10,11... | collective-permute-start | bytes 442376 | tf_op jit(solution)/shard_map/ppermute | solution.py:435
  34.2 10.3 %collective-permute-start.7 = (bf16[192,384]{1,0:T(8,128)(2,1)S(1)}, bf16[192,384]{1,0:T(8,128)(2,1)S(1)}, u32[]{:S(2)}, u32[]{:S(2)}) collective-permute-start(bf16[192,384]{1,0:T(8,128)(2,1)S(1)} %get-tuple-element.66), channel_id=1, source_target_pairs={{0,127},{1,2},{2,1},{3,4},{4,3},{5,6},{6,5},{7,8},{8,7},{9,10},{10... | collective-permute-start | bytes 442376 | tf_op jit(solution)/shard_map/ppermute | solution.py:434
  46.3 1.2 %collective-permute-start.8 = (f32[32,128]{1,0:T(8,128)S(1)}, f32[32,128]{1,0:T(8,128)S(1)}, u32[]{:S(2)}, u32[]{:S(2)}) collective-permute-start(f32[32,128]{1,0:T(8,128)S(1)} %get-tuple-element.76), channel_id=1, source_target_pairs={{0,16},{1,17},{2,18},{3,19},{4,20},{5,21},{6,22},{7,23},{8,24},{9,... | collective-permute-start | bytes 49160 | tf_op jit(solution)/shard_map/ppermute | solution.py:532
  47.6 5.3 %collective-permute-start.11 = (f32[32,128]{1,0:T(8,128)S(1)}, f32[32,128]{1,0:T(8,128)S(1)}, u32[]{:S(2)}, u32[]{:S(2)}) collective-permute-start(f32[32,128]{1,0:T(8,128)S(1)} %add.30), channel_id=1, source_target_pairs={{0,2},{1,3},{2,0},{3,1},{4,6},{5,7},{6,4},{7,5},{8,10},{9,11},{10,... | collective-permute-start | bytes 49160 | tf_op jit(solution)/shard_map/ppermute | solution.py:532
  47.6 5.3 %collective-permute-start.10 = (f32[32,128]{1,0:T(8,128)S(1)}, f32[32,128]{1,0:T(8,128)S(1)}, u32[]{:S(2)}, u32[]{:S(2)}) collective-permute-start(f32[32,128]{1,0:T(8,128)S(1)} %add.30), channel_id=1, source_target_pairs={{0,3},{1,2},{2,1},{3,0},{4,7},{5,6},{6,5},{7,4},{8,11},{9,10},{10,... | collective-permute-start | bytes 49160 | tf_op jit(solution)/shard_map/ppermute | solution.py:532
  47.7 5.2 %collective-permute-start.9 = (f32[32,128]{1,0:T(8,128)S(1)}, f32[32,128]{1,0:T(8,128)S(1)}, u32[]{:S(2)}, u32[]{:S(2)}) collective-permute-start(f32[32,128]{1,0:T(8,128)S(1)} %add.30), channel_id=1, source_target_pairs={{0,1},{1,0},{2,3},{3,2},{4,5},{5,4},{6,7},{7,6},{8,9},{9,8},{10,11... | collective-permute-start | bytes 49160 | tf_op jit(solution)/shard_map/ppermute | solution.py:532
  52.9 5.3 %collective-permute-start.14 = (f32[32,128]{1,0:T(8,128)S(1)}, f32[32,128]{1,0:T(8,128)S(1)}, u32[]{:S(2)}, u32[]{:S(2)}) collective-permute-start(f32[32,128]{1,0:T(8,128)S(1)} %add_add_fusion.2), channel_id=1, source_target_pairs={{0,8},{1,9},{2,10},{3,11},{4,12},{5,13},{6,14},{7,15},{8,0},{9,1},... | collective-permute-start | bytes 49160 | tf_op jit(solution)/shard_map/ppermute | solution.py:532
  53.0 5.2 %collective-permute-start.13 = (f32[32,128]{1,0:T(8,128)S(1)}, f32[32,128]{1,0:T(8,128)S(1)}, u32[]{:S(2)}, u32[]{:S(2)}) collective-permute-start(f32[32,128]{1,0:T(8,128)S(1)} %add_add_fusion.2), channel_id=1, source_target_pairs={{0,12},{1,13},{2,14},{3,15},{4,8},{5,9},{6,10},{7,11},{8,4},{9,5},... | collective-permute-start | bytes 49160 | tf_op jit(solution)/shard_map/ppermute | solution.py:532
  53.6 4.6 %collective-permute-start.12 = (f32[32,128]{1,0:T(8,128)S(1)}, f32[32,128]{1,0:T(8,128)S(1)}, u32[]{:S(2)}, u32[]{:S(2)}) collective-permute-start(f32[32,128]{1,0:T(8,128)S(1)} %add_add_fusion.2), channel_id=1, source_target_pairs={{0,4},{1,5},{2,6},{3,7},{4,0},{5,1},{6,2},{7,3},{8,12},{9,13},{10,... | collective-permute-start | bytes 49160 | tf_op jit(solution)/shard_map/ppermute | solution.py:532
  58.2 5.3 %collective-permute-start.17 = (f32[32,128]{1,0:T(8,128)S(1)}, f32[32,128]{1,0:T(8,128)S(1)}, u32[]{:S(2)}, u32[]{:S(2)}) collective-permute-start(f32[32,128]{1,0:T(8,128)S(1)} %add_add_fusion.1), channel_id=1, source_target_pairs={{0,64},{1,65},{2,66},{3,67},{4,68},{5,69},{6,70},{7,71},{8,72},{9,... | collective-permute-start | bytes 49160 | tf_op jit(solution)/shard_map/ppermute | solution.py:532
  60.3 4.9 %collective-permute-start.16 = (f32[32,128]{1,0:T(8,128)S(1)}, f32[32,128]{1,0:T(8,128)S(1)}, u32[]{:S(2)}, u32[]{:S(2)}) collective-permute-start(f32[32,128]{1,0:T(8,128)S(1)} %add_add_fusion.1), channel_id=1, source_target_pairs={{0,96},{1,97},{2,98},{3,99},{4,100},{5,101},{6,102},{7,103},{8,104... | collective-permute-start | bytes 49160 | tf_op jit(solution)/shard_map/ppermute | solution.py:532
  61.8 3.7 %collective-permute-start.15 = (f32[32,128]{1,0:T(8,128)S(1)}, f32[32,128]{1,0:T(8,128)S(1)}, u32[]{:S(2)}, u32[]{:S(2)}) collective-permute-start(f32[32,128]{1,0:T(8,128)S(1)} %add_add_fusion.1), channel_id=1, source_target_pairs={{0,32},{1,33},{2,34},{3,35},{4,36},{5,37},{6,38},{7,39},{8,40},{9,... | collective-permute-start | bytes 49160 | tf_op jit(solution)/shard_map/ppermute | solution.py:532

commit v6 on v5

--- a/solution.py
+++ b/solution.py
@@ -461,7 +461,8 @@
         compiler_params=params(8),
         name="first",
     )(hbm(boundary), hbm(tile_pair), hbm(modes), hbm(tiles))
-    re, ro = exchange(se, so)
+    re = lax.ppermute(se, AXES, pairs_even)
+    ro = lax.ppermute(so, AXES, pairs_odd)
     w_in, j, m, b, o, fe, fo = pl.pallas_call(
         load_kernel,
         out_shape=(weights(18), f32(6), f32(4), f32(4), f32(2), weights(1), weights(1)),

time: 69.3 us -> 69.3 us (level)
    ppermute x0 -> x2, starting transfers between devices: none -> 8.75 us  [the longest x1 7.01 us: local(): ro = lax.ppermute(so, AXES, pairs_odd)]
    ppermute x4 -> x3, starting transfers between devices: 18.4 us -> 11.4 us  [exchange(): ro = lax.ppermute(so, AXES, pairs_odd)]
    ppermute x4 -> x3, starting transfers between devices: 2 us -> 0.26 us  [exchange(): re = lax.ppermute(se, AXES, pairs_even)]
    ppermute x4 -> x3, waiting for transfers between devices: 8.02 us -> 8.02 us  [exchange(): ro = lax.ppermute(so, AXES, pairs_odd)]
where the time goes in v6:
time: 69.3 us; the launch traced here: 69.1 us
  starting transfers between devices  31.9 us (46%)
  Pallas kernels  20.6 us (30%)
  waiting for transfers between devices  16.3 us (24%)
    ppermute x10, starting transfers between devices, local(): lax.ppermute(g, AXES, [(i, i ^ bits) for i in range(count)])  11.5 us
    ppermute x3, starting transfers between devices, exchange(): ro = lax.ppermute(so, AXES, pairs_odd)  11.4 us
    ppermute x3, waiting for transfers between devices, exchange(): ro = lax.ppermute(so, AXES, pairs_odd)  8.02 us
    ppermute x10, waiting for transfers between devices, local(): lax.ppermute(g, AXES, [(i, i ^ bits) for i in range(count)])  7.7 us
    ppermute x1, starting transfers between devices, local(): ro = lax.ppermute(so, AXES, pairs_odd)  7.01 us
    pallas_call x2, Pallas kernels, local(): pl.pallas_call(functools.partial(step_kernel, later, later), out_shape=(f...  5.04 us
    pallas_call x1, Pallas kernels, local(): pl.pallas_call(load_kernel, out_shape=(weights(18), f32(6), f32(4), f32(4...  4.77 us
    pallas_call x1, Pallas kernels, local(): pl.pallas_call(functools.partial(whiten_kernel, 1.0 / (ROWS * count)), ou...  3.4 us
  transfers between devices with their start and end apart: 18, of which 9 were waited for; matrix products, arithmetic and copies ran while one was open for 0% of the time, Pallas kernels for 16%

profile of v6, /device:TPU:0, one launch (start us, length us, event | category | flops | bytes accessed | tf_op | source)
XLA Modules:
  0.0 69.1 jit_solution(3092477259181207211)
XLA Ops:
  0.0 2.5 %first.1 = (bf16[1536,384]{1,0:T(8,128)(2,1)S(1)}, bf16[768,384]{1,0:T(8,128)(2,1)S(1)}, f32[64,768]{1,0:T(8,128)S(1)}, bf16[512,384]{1,0:T(8,128)(2,1)S(1)}, bf...) custom-call(s32[1,2]{1,0:T(1,128)} %bound_ref.1, s32[24]{0:T(128)} %pair_ref.1, f32[64,3072]{1,0:T(8,128)} %modes_ref.3, ...), custom_call_target="tpu_custom_call" | custom-call | tf_op jit(solution)/shard_map/first/pallas_call | solution.py:447
  2.5 1.7 %collective-permute-start = (bf16[512,384]{1,0:T(8,128)(2,1)S(1)}, bf16[512,384]{1,0:T(8,128)(2,1)S(1)}, u32[]{:S(2)}, u32[]{:S(2)}) collective-permute-start(bf16[512,384]{1,0:T(8,128)(2,1)S(1)} %get-tuple-element.46), channel_id=1, source_target_pairs={{0,1},{1,0},{2,3},{3,2},{4,5},{5,4},{6,7},{7,6},{8,9},{9,8},{10,11... | collective-permute-start | bytes 1179656 | tf_op jit(solution)/shard_map/ppermute | solution.py:464
  4.3 7.0 %collective-permute-start.1 = (bf16[512,384]{1,0:T(8,128)(2,1)S(1)}, bf16[512,384]{1,0:T(8,128)(2,1)S(1)}, u32[]{:S(2)}, u32[]{:S(2)}) collective-permute-start(bf16[512,384]{1,0:T(8,128)(2,1)S(1)} %get-tuple-element.48), channel_id=1, source_target_pairs={{0,127},{1,2},{2,1},{3,4},{4,3},{5,6},{6,5},{7,8},{8,7},{9,10},{10... | collective-permute-start | bytes 1179656 | tf_op jit(solution)/shard_map/ppermute | solution.py:465
  11.3 4.8 %load.1 = (bf16[6912,384]{1,0:T(8,128)(2,1)S(1)}, f32[64,2304]{1,0:T(8,128)S(1)}, f32[64,1536]{1,0:T(8,128)S(1)}, f32[64,1536]{1,0:T(8,128)S(1)}, f32[64,768]{1,...) custom-call(s32[24]{0:T(128)S(4)} %get-tuple-element.42.inv_ref, f32[64,3072]{1,0:T(8,128)} %modes_ref.3, ...), custom_call_target="tpu_custom_call" | custom-call | flops 754974720 | bytes 8388608 | tf_op jit(solution)/shard_map/load/pallas_call | solution.py:466
  16.1 0.1 collective-permute-start.4
  16.2 4.6 %collective-permute-start.5 = (bf16[384,384]{1,0:T(8,128)(2,1)S(1)}, bf16[384,384]{1,0:T(8,128)(2,1)S(1)}, u32[]{:S(2)}, u32[]{:S(2)}) collective-permute-start(bf16[384,384]{1,0:T(8,128)(2,1)S(1)} %get-tuple-element.64), channel_id=1, source_target_pairs={{0,127},{1,2},{2,1},{3,4},{4,3},{5,6},{6,5},{7,8},{8,7},{9,10},{10... | collective-permute-start | bytes 884744 | tf_op jit(solution)/shard_map/ppermute | solution.py:434
  20.8 1.1 %edge2.1 = (f32[64,1536]{1,0:T(8,128)S(1)}, f32[64,768]{1,0:T(8,128)S(1)}, bf16[192,384]{1,0:T(8,128)(2,1)S(1)}, bf16[192,384]{1,0:T(8,128)(2,1)S(1)}, bf16[768,384]{1,0:T(8,128)(2,1)S(1)}) custom-call(bf16[512,384]{1,0:T(8,128)(2,1)S(1)} %collective-permute-done.re_ref, bf16[512,384]{1,0:T(8,128)(2,1)S(1)} %collective-permute-done.1.ro_ref, ...), custom_call_target="tpu_custom_call" | custom-call | tf_op jit(solution)/shard_map/edge2/pallas_call | solution.py:484
  22.0 0.1 collective-permute-start.2
  22.1 3.3 %collective-permute-start.3 = (bf16[192,384]{1,0:T(8,128)(2,1)S(1)}, bf16[192,384]{1,0:T(8,128)(2,1)S(1)}, u32[]{:S(2)}, u32[]{:S(2)}) collective-permute-start(bf16[192,384]{1,0:T(8,128)(2,1)S(1)} %get-tuple-element.56), channel_id=1, source_target_pairs={{0,127},{1,2},{2,1},{3,4},{4,3},{5,6},{6,5},{7,8},{8,7},{9,10},{10... | collective-permute-start | bytes 442376 | tf_op jit(solution)/shard_map/ppermute | solution.py:434
  25.4 2.3 %step.2 = (f32[64,1536]{1,0:T(8,128)S(1)}, f32[64,1536]{1,0:T(8,128)S(1)}, f32[64,768]{1,0:T(8,128)S(1)}, f32[64,768]{1,0:T(8,128)S(1)}, f32[64,1536]{1,0:T(8,128)S(1)}) custom-call(f32[64,1536]{1,0:T(8,128)S(1)} %get-tuple-element.58.refs_0_, f32[64,1536]{1,0:T(8,128)S(1)} %get-tuple-element.53.m_ref.refs_1_, ...), custom_call_target="tpu_custom_call" | custom-call | flops 981467136 | bytes 8388608 | tf_op jit(solution)/shard_map/step/pallas_call | solution.py:495
  27.7 0.6 collective-permute-done.2.re_ref
  28.3 3.9 %collective-permute-done.3.ro_ref = bf16[192,384]{1,0:T(8,128)(2,1)S(1)} collective-permute-done((bf16[192,384]{1,0:T(8,128)(2,1)S(1)}, bf16[192,384]{1,0:T(8,128)(2,1)S(1)}, u32[]{:S(2)}, u32[]{:S(2)}) %collective-permute-start.3) | collective-permute-done | bytes 147488 | tf_op jit(solution)/shard_map/ppermute | solution.py:434
  32.2 1.9 %edge3.1 = (f32[64,2304]{1,0:T(8,128)S(1)}, f32[64,768]{1,0:T(8,128)S(1)}, f32[64,768]{1,0:T(8,128)S(1)}, bf16[192,384]{1,0:T(8,128)(2,1)S(1)}, bf16[192,384]{1,0:T(8,128)(2,1)S(1)}) custom-call(bf16[192,384]{1,0:T(8,128)(2,1)S(1)} %collective-permute-done.2.re_ref, bf16[192,384]{1,0:T(8,128)(2,1)S(1)} %collective-permute-done.3.ro_ref, ...), custom_call_target="tpu_custom_call" | custom-call | tf_op jit(solution)/shard_map/edge3/pallas_call | solution.py:515
  34.2 3.5 %collective-permute-start.7 = (bf16[192,384]{1,0:T(8,128)(2,1)S(1)}, bf16[192,384]{1,0:T(8,128)(2,1)S(1)}, u32[]{:S(2)}, u32[]{:S(2)}) collective-permute-start(bf16[192,384]{1,0:T(8,128)(2,1)S(1)} %get-tuple-element.66), channel_id=1, source_target_pairs={{0,127},{1,2},{2,1},{3,4},{4,3},{5,6},{6,5},{7,8},{8,7},{9,10},{10... | collective-permute-start | bytes 442376 | tf_op jit(solution)/shard_map/ppermute | solution.py:434
  37.7 2.7 %step.3 = (f32[64,1536]{1,0:T(8,128)}, f32[64,1536]{1,0:T(8,128)S(1)}, f32[64,768]{1,0:T(8,128)S(1)}, f32[64,768]{1,0:T(8,128)S(1)}, f32[64,1536]{1,0:T(8,128)S(1)}, /*index=5*/f32[64,64]{1,0:T(8,128)S(1)}) custom-call(f32[64,2304]{1,0:T(8,128)S(1)} %get-tuple-element.68.refs_0_, f32[64,768]{1,0:T(8,128)S(1)} %get-tuple-element.69.refs_1_, ...), custom_call_target="tpu_custom_call" | custom-call | flops 981467136 | bytes 8388608 | tf_op jit(solution)/shard_map/step/pallas_call | solution.py:495
  40.4 4.1 %collective-permute-done.7.ro_ref = bf16[192,384]{1,0:T(8,128)(2,1)S(1)} collective-permute-done((bf16[192,384]{1,0:T(8,128)(2,1)S(1)}, bf16[192,384]{1,0:T(8,128)(2,1)S(1)}, u32[]{:S(2)}, u32[]{:S(2)}) %collective-permute-start.7) | collective-permute-done | bytes 147488 | tf_op jit(solution)/shard_map/ppermute | solution.py:434
  44.5 1.8 %final.1 = (f32[64,2304]{1,0:T(8,128)S(1)}, f32[32,128]{1,0:T(8,128)S(1)}) custom-call(bf16[192,384]{1,0:T(8,128)(2,1)S(1)} %collective-permute-done.6.re_ref, bf16[192,384]{1,0:T(8,128)(2,1)S(1)} %collective-permute-done.7.ro_ref, f32[64,768]{1,0:T(8,128)S(1)} %get-tuple-element.67.z_ref, f32[64,768]{1,0:T(8,128)S(1)} %get-tuple-element.72.o_ref, ...), custom_call_target="tpu_custom_call" | custom-call | tf_op jit(solution)/shard_map/final/pallas_call | solution.py:524
  46.4 1.2 %collective-permute-done.8 = f32[32,128]{1,0:T(8,128)S(1)} collective-permute-done((f32[32,128]{1,0:T(8,128)S(1)}, f32[32,128]{1,0:T(8,128)S(1)}, u32[]{:S(2)}, u32[]{:S(2)}) %collective-permute-start.8) | collective-permute-done | bytes 16416 | tf_op jit(solution)/shard_map/ppermute | solution.py:533
  47.6 0.1 collective-permute-start.10
  47.7 3.4 %collective-permute-start.9 = (f32[32,128]{1,0:T(8,128)S(1)}, f32[32,128]{1,0:T(8,128)S(1)}, u32[]{:S(2)}, u32[]{:S(2)}) collective-permute-start(f32[32,128]{1,0:T(8,128)S(1)} %add.30), channel_id=1, source_target_pairs={{0,1},{1,0},{2,3},{3,2},{4,5},{5,4},{6,7},{7,6},{8,9},{9,8},{10,11... | collective-permute-start | bytes 49160 | tf_op jit(solution)/shard_map/ppermute | solution.py:533
  51.1 1.8 %collective-permute-done.11 = f32[32,128]{1,0:T(8,128)S(1)} collective-permute-done((f32[32,128]{1,0:T(8,128)S(1)}, f32[32,128]{1,0:T(8,128)S(1)}, u32[]{:S(2)}, u32[]{:S(2)}) %collective-permute-start.11) | collective-permute-done | bytes 16416 | tf_op jit(solution)/shard_map/ppermute | solution.py:533
  52.9 0.1 collective-permute-start.14
  53.0 0.6 collective-permute-start.13
  53.6 2.9 %collective-permute-start.12 = (f32[32,128]{1,0:T(8,128)S(1)}, f32[32,128]{1,0:T(8,128)S(1)}, u32[]{:S(2)}, u32[]{:S(2)}) collective-permute-start(f32[32,128]{1,0:T(8,128)S(1)} %add_add_fusion.2), channel_id=1, source_target_pairs={{0,4},{1,5},{2,6},{3,7},{4,0},{5,1},{6,2},{7,3},{8,12},{9,13},{10,... | collective-permute-start | bytes 49160 | tf_op jit(solution)/shard_map/ppermute | solution.py:533
  56.4 1.8 %collective-permute-done.14 = f32[32,128]{1,0:T(8,128)S(1)} collective-permute-done((f32[32,128]{1,0:T(8,128)S(1)}, f32[32,128]{1,0:T(8,128)S(1)}, u32[]{:S(2)}, u32[]{:S(2)}) %collective-permute-start.14) | collective-permute-done | bytes 16416 | tf_op jit(solution)/shard_map/ppermute | solution.py:533
  58.2 2.1 %collective-permute-start.17 = (f32[32,128]{1,0:T(8,128)S(1)}, f32[32,128]{1,0:T(8,128)S(1)}, u32[]{:S(2)}, u32[]{:S(2)}) collective-permute-start(f32[32,128]{1,0:T(8,128)S(1)} %add_add_fusion.1), channel_id=1, source_target_pairs={{0,64},{1,65},{2,66},{3,67},{4,68},{5,69},{6,70},{7,71},{8,72},{9,... | collective-permute-start | bytes 49160 | tf_op jit(solution)/shard_map/ppermute | solution.py:533
  60.3 1.5 %collective-permute-start.16 = (f32[32,128]{1,0:T(8,128)S(1)}, f32[32,128]{1,0:T(8,128)S(1)}, u32[]{:S(2)}, u32[]{:S(2)}) collective-permute-start(f32[32,128]{1,0:T(8,128)S(1)} %add_add_fusion.1), channel_id=1, source_target_pairs={{0,96},{1,97},{2,98},{3,99},{4,100},{5,101},{6,102},{7,103},{8,104... | collective-permute-start | bytes 49160 | tf_op jit(solution)/shard_map/ppermute | solution.py:533
  61.8 0.8 %collective-permute-start.15 = (f32[32,128]{1,0:T(8,128)S(1)}, f32[32,128]{1,0:T(8,128)S(1)}, u32[]{:S(2)}, u32[]{:S(2)}) collective-permute-start(f32[32,128]{1,0:T(8,128)S(1)} %add_add_fusion.1), channel_id=1, source_target_pairs={{0,32},{1,33},{2,34},{3,35},{4,36},{5,37},{6,38},{7,39},{8,40},{9,... | collective-permute-start | bytes 49160 | tf_op jit(solution)/shard_map/ppermute | solution.py:533
  62.6 0.9 %collective-permute-done.17 = f32[32,128]{1,0:T(8,128)S(1)} collective-permute-done((f32[32,128]{1,0:T(8,128)S(1)}, f32[32,128]{1,0:T(8,128)S(1)}, u32[]{:S(2)}, u32[]{:S(2)}) %collective-permute-start.17) | collective-permute-done | bytes 16416 | tf_op jit(solution)/shard_map/ppermute | solution.py:533
  63.5 1.8 %collective-permute-done.16 = f32[32,128]{1,0:T(8,128)S(1)} collective-permute-done((f32[32,128]{1,0:T(8,128)S(1)}, f32[32,128]{1,0:T(8,128)S(1)}, u32[]{:S(2)}, u32[]{:S(2)}) %collective-permute-start.16) | collective-permute-done | bytes 16416 | tf_op jit(solution)/shard_map/ppermute | solution.py:533
  65.3 0.3 collective-permute-done.15
  65.6 3.4 %whiten.1 = f32[64,3072]{1,0:T(8,128)} custom-call(f32[32,128]{1,0:T(8,128)S(1)} %add_add_fusion.g_ref, f32[64,2304]{1,0:T(8,128)S(1)} %get-tuple-element.77.e_ref, f32[64,768]{1,0:T(8,128)S(1)} %get-tuple-element.78.i_ref), custom_call_target="tpu_custom_call" | custom-call | tf_op jit(solution)/shard_map/whiten/pallas_call | solution.py:536
  (16 shorter events, 0.2 us)
Async XLA Ops:
  2.5 13.6 %collective-permute-start = (bf16[512,384]{1,0:T(8,128)(2,1)S(1)}, bf16[512,384]{1,0:T(8,128)(2,1)S(1)}, u32[]{:S(2)}, u32[]{:S(2)}) collective-permute-start(bf16[512,384]{1,0:T(8,128)(2,1)S(1)} %get-tuple-element.46), channel_id=1, source_target_pairs={{0,1},{1,0},{2,3},{3,2},{4,5},{5,4},{6,7},{7,6},{8,9},{9,8},{10,11... | collective-permute-start | bytes 1179656 | tf_op jit(solution)/shard_map/ppermute | solution.py:464
  4.3 16.5 %collective-permute-start.1 = (bf16[512,384]{1,0:T(8,128)(2,1)S(1)}, bf16[512,384]{1,0:T(8,128)(2,1)S(1)}, u32[]{:S(2)}, u32[]{:S(2)}) collective-permute-start(bf16[512,384]{1,0:T(8,128)(2,1)S(1)} %get-tuple-element.48), channel_id=1, source_target_pairs={{0,127},{1,2},{2,1},{3,4},{4,3},{5,6},{6,5},{7,8},{8,7},{9,10},{10... | collective-permute-start | bytes 1179656 | tf_op jit(solution)/shard_map/ppermute | solution.py:465
  16.1 11.6 %collective-permute-start.4 = (bf16[384,384]{1,0:T(8,128)(2,1)S(1)}, bf16[384,384]{1,0:T(8,128)(2,1)S(1)}, u32[]{:S(2)}, u32[]{:S(2)}) collective-permute-start(bf16[384,384]{1,0:T(8,128)(2,1)S(1)} %get-tuple-element.63), channel_id=1, source_target_pairs={{0,1},{1,0},{2,3},{3,2},{4,5},{5,4},{6,7},{7,6},{8,9},{9,8},{10,11... | collective-permute-start | bytes 884744 | tf_op jit(solution)/shard_map/ppermute | solution.py:435
  16.2 16.1 %collective-permute-start.5 = (bf16[384,384]{1,0:T(8,128)(2,1)S(1)}, bf16[384,384]{1,0:T(8,128)(2,1)S(1)}, u32[]{:S(2)}, u32[]{:S(2)}) collective-permute-start(bf16[384,384]{1,0:T(8,128)(2,1)S(1)} %get-tuple-element.64), channel_id=1, source_target_pairs={{0,127},{1,2},{2,1},{3,4},{4,3},{5,6},{6,5},{7,8},{8,7},{9,10},{10... | collective-permute-start | bytes 884744 | tf_op jit(solution)/shard_map/ppermute | solution.py:434
  22.0 6.3 %collective-permute-start.2 = (bf16[192,384]{1,0:T(8,128)(2,1)S(1)}, bf16[192,384]{1,0:T(8,128)(2,1)S(1)}, u32[]{:S(2)}, u32[]{:S(2)}) collective-permute-start(bf16[192,384]{1,0:T(8,128)(2,1)S(1)} %get-tuple-element.55), channel_id=1, source_target_pairs={{0,1},{1,0},{2,3},{3,2},{4,5},{5,4},{6,7},{7,6},{8,9},{9,8},{10,11... | collective-permute-start | bytes 442376 | tf_op jit(solution)/shard_map/ppermute | solution.py:435
  22.1 10.2 %collective-permute-start.3 = (bf16[192,384]{1,0:T(8,128)(2,1)S(1)}, bf16[192,384]{1,0:T(8,128)(2,1)S(1)}, u32[]{:S(2)}, u32[]{:S(2)}) collective-permute-start(bf16[192,384]{1,0:T(8,128)(2,1)S(1)} %get-tuple-element.56), channel_id=1, source_target_pairs={{0,127},{1,2},{2,1},{3,4},{4,3},{5,6},{6,5},{7,8},{8,7},{9,10},{10... | collective-permute-start | bytes 442376 | tf_op jit(solution)/shard_map/ppermute | solution.py:434
  34.1 6.3 %collective-permute-start.6 = (bf16[192,384]{1,0:T(8,128)(2,1)S(1)}, bf16[192,384]{1,0:T(8,128)(2,1)S(1)}, u32[]{:S(2)}, u32[]{:S(2)}) collective-permute-start(bf16[192,384]{1,0:T(8,128)(2,1)S(1)} %get-tuple-element.65), channel_id=1, source_target_pairs={{0,1},{1,0},{2,3},{3,2},{4,5},{5,4},{6,7},{7,6},{8,9},{9,8},{10,11... | collective-permute-start | bytes 442376 | tf_op jit(solution)/shard_map/ppermute | solution.py:435
  34.2 10.3 %collective-permute-start.7 = (bf16[192,384]{1,0:T(8,128)(2,1)S(1)}, bf16[192,384]{1,0:T(8,128)(2,1)S(1)}, u32[]{:S(2)}, u32[]{:S(2)}) collective-permute-start(bf16[192,384]{1,0:T(8,128)(2,1)S(1)} %get-tuple-element.66), channel_id=1, source_target_pairs={{0,127},{1,2},{2,1},{3,4},{4,3},{5,6},{6,5},{7,8},{8,7},{9,10},{10... | collective-permute-start | bytes 442376 | tf_op jit(solution)/shard_map/ppermute | solution.py:434
  46.3 1.2 %collective-permute-start.8 = (f32[32,128]{1,0:T(8,128)S(1)}, f32[32,128]{1,0:T(8,128)S(1)}, u32[]{:S(2)}, u32[]{:S(2)}) collective-permute-start(f32[32,128]{1,0:T(8,128)S(1)} %get-tuple-element.76), channel_id=1, source_target_pairs={{0,16},{1,17},{2,18},{3,19},{4,20},{5,21},{6,22},{7,23},{8,24},{9,... | collective-permute-start | bytes 49160 | tf_op jit(solution)/shard_map/ppermute | solution.py:533
  47.6 5.3 %collective-permute-start.11 = (f32[32,128]{1,0:T(8,128)S(1)}, f32[32,128]{1,0:T(8,128)S(1)}, u32[]{:S(2)}, u32[]{:S(2)}) collective-permute-start(f32[32,128]{1,0:T(8,128)S(1)} %add.30), channel_id=1, source_target_pairs={{0,2},{1,3},{2,0},{3,1},{4,6},{5,7},{6,4},{7,5},{8,10},{9,11},{10,... | collective-permute-start | bytes 49160 | tf_op jit(solution)/shard_map/ppermute | solution.py:533
  47.6 5.3 %collective-permute-start.10 = (f32[32,128]{1,0:T(8,128)S(1)}, f32[32,128]{1,0:T(8,128)S(1)}, u32[]{:S(2)}, u32[]{:S(2)}) collective-permute-start(f32[32,128]{1,0:T(8,128)S(1)} %add.30), channel_id=1, source_target_pairs={{0,3},{1,2},{2,1},{3,0},{4,7},{5,6},{6,5},{7,4},{8,11},{9,10},{10,... | collective-permute-start | bytes 49160 | tf_op jit(solution)/shard_map/ppermute | solution.py:533
  47.7 5.2 %collective-permute-start.9 = (f32[32,128]{1,0:T(8,128)S(1)}, f32[32,128]{1,0:T(8,128)S(1)}, u32[]{:S(2)}, u32[]{:S(2)}) collective-permute-start(f32[32,128]{1,0:T(8,128)S(1)} %add.30), channel_id=1, source_target_pairs={{0,1},{1,0},{2,3},{3,2},{4,5},{5,4},{6,7},{7,6},{8,9},{9,8},{10,11... | collective-permute-start | bytes 49160 | tf_op jit(solution)/shard_map/ppermute | solution.py:533
  52.9 5.3 %collective-permute-start.14 = (f32[32,128]{1,0:T(8,128)S(1)}, f32[32,128]{1,0:T(8,128)S(1)}, u32[]{:S(2)}, u32[]{:S(2)}) collective-permute-start(f32[32,128]{1,0:T(8,128)S(1)} %add_add_fusion.2), channel_id=1, source_target_pairs={{0,8},{1,9},{2,10},{3,11},{4,12},{5,13},{6,14},{7,15},{8,0},{9,1},... | collective-permute-start | bytes 49160 | tf_op jit(solution)/shard_map/ppermute | solution.py:533
  53.0 5.2 %collective-permute-start.13 = (f32[32,128]{1,0:T(8,128)S(1)}, f32[32,128]{1,0:T(8,128)S(1)}, u32[]{:S(2)}, u32[]{:S(2)}) collective-permute-start(f32[32,128]{1,0:T(8,128)S(1)} %add_add_fusion.2), channel_id=1, source_target_pairs={{0,12},{1,13},{2,14},{3,15},{4,8},{5,9},{6,10},{7,11},{8,4},{9,5},... | collective-permute-start | bytes 49160 | tf_op jit(solution)/shard_map/ppermute | solution.py:533
  53.6 4.6 %collective-permute-start.12 = (f32[32,128]{1,0:T(8,128)S(1)}, f32[32,128]{1,0:T(8,128)S(1)}, u32[]{:S(2)}, u32[]{:S(2)}) collective-permute-start(f32[32,128]{1,0:T(8,128)S(1)} %add_add_fusion.2), channel_id=1, source_target_pairs={{0,4},{1,5},{2,6},{3,7},{4,0},{5,1},{6,2},{7,3},{8,12},{9,13},{10,... | collective-permute-start | bytes 49160 | tf_op jit(solution)/shard_map/ppermute | solution.py:533
  58.2 5.3 %collective-permute-start.17 = (f32[32,128]{1,0:T(8,128)S(1)}, f32[32,128]{1,0:T(8,128)S(1)}, u32[]{:S(2)}, u32[]{:S(2)}) collective-permute-start(f32[32,128]{1,0:T(8,128)S(1)} %add_add_fusion.1), channel_id=1, source_target_pairs={{0,64},{1,65},{2,66},{3,67},{4,68},{5,69},{6,70},{7,71},{8,72},{9,... | collective-permute-start | bytes 49160 | tf_op jit(solution)/shard_map/ppermute | solution.py:533
  60.3 4.9 %collective-permute-start.16 = (f32[32,128]{1,0:T(8,128)S(1)}, f32[32,128]{1,0:T(8,128)S(1)}, u32[]{:S(2)}, u32[]{:S(2)}) collective-permute-start(f32[32,128]{1,0:T(8,128)S(1)} %add_add_fusion.1), channel_id=1, source_target_pairs={{0,96},{1,97},{2,98},{3,99},{4,100},{5,101},{6,102},{7,103},{8,104... | collective-permute-start | bytes 49160 | tf_op jit(solution)/shard_map/ppermute | solution.py:533
  61.8 3.7 %collective-permute-start.15 = (f32[32,128]{1,0:T(8,128)S(1)}, f32[32,128]{1,0:T(8,128)S(1)}, u32[]{:S(2)}, u32[]{:S(2)}) collective-permute-start(f32[32,128]{1,0:T(8,128)S(1)} %add_add_fusion.1), channel_id=1, source_target_pairs={{0,32},{1,33},{2,34},{3,35},{4,36},{5,37},{6,38},{7,39},{8,40},{9,... | collective-permute-start | bytes 49160 | tf_op jit(solution)/shard_map/ppermute | solution.py:533
